TPU v7x, 256 devices: a whole 4x4x8 slice. The times are simulated.
256 devices in a mesh: atoms: 32 (over z_lo, x, core), waves: 8 (over z_hi, y).
Axes of the slice: x: 4, y: 4, z: 8 (z_hi: 2, z_lo: 4; z = z_hi * 4 + z_lo), core: 2. Of those that a mesh axis runs over, the one named last changes fastest.
Arguments:
- features: bfloat16 [64, 65536], P(None, 'atoms'), may hold values from -6 to 6
- coords: float32 [3, 65536], P(None, 'atoms'), may hold values from 0 to 1
- neighbours: int32 [27, 512], P(None, 'atoms'), may hold values from 0 to 511, as said below
- live_slots: int32 [27, 512], P(None, 'atoms'), may hold values 0 or 1
- block_count: int32 [32], P('atoms'), may hold values from 8 to 16, as said below
- kvec: int32 [3, 4096], P(None, 'waves'), may hold values from -64 to 64, as said below
- msg_weight: bfloat16 [1, 64, 64], replicated, may hold values from -0.75 to 0.75
- filter_weight: float32 [1, 64, 64], replicated, may hold values from -0.75 to 0.75
- mlp_in: bfloat16 [1, 128, 192], replicated, may hold values from -0.4375 to 0.4375
- mlp_out: bfloat16 [1, 64, 128], replicated, may hold values from -0.5 to 0.5
Outputs:
- updated: bfloat16 [64, 65536], P(None, 'atoms')
Inputs may be any that keep to these rules, and one draw needn't show every extreme that they name: `neighbours`: entry [s, b] names a block slot whose index of atoms, slot // 16, equals b // 16 or lies one before or one after it, cyclically, and which is live. `block_count`: some index of atoms has all 16 of its slots live in every draw. `kvec`: rows 1 and 2 lie in -5 to 5; no column is zero in all three rows.
All inputs are finite; a program needn't handle non-finite values. No bound on the sum of `live_slots` on one device may be relied on, other than what follows from the above.
Results may differ from a plain program's by a relative error of at most 0.0062.
Values may be sent and summed in bfloat16 or wider, within the bound.
No kernel may reach another device: no remote copies, remote signals or barrier semaphores. Data moves between devices by JAX's collectives and lax.ppermute only.
A program may use at most 64 MiB of HBM per device.

v0:
```python
import math

import jax
import jax.numpy as jnp
from jax import lax
from jax.sharding import PartitionSpec as P

K = 4096
BLOCK = 128


TWO_PI = 6.283185307179586
MSG_SCALE = 0.125
GAIN_TOP = 20.0


def with_halo(cells, sides, width):
    for axis, dim in sides:
        count = lax.axis_size(axis)
        head = lax.slice_in_dim(cells, 0, width, axis=dim)
        tail = lax.slice_in_dim(cells, cells.shape[dim] - width, cells.shape[dim], axis=dim)
        cells = jnp.concatenate(
            [
                lax.ppermute(tail, axis, [(i, (i + 1) % count) for i in range(count)]),
                cells,
                lax.ppermute(head, axis, [((i + 1) % count, i) for i in range(count)]),
            ],
            axis=dim,
        )
    return cells


def in_blocks(shard, dim, count):
    lengths = shard.shape
    pieces = shard.reshape(*lengths[:dim], count, lengths[dim] // count, *lengths[dim + 1 :])
    return jnp.moveaxis(pieces, dim, 0)


def sent_and_summed(shard, axis, dim):
    pieces = in_blocks(shard, dim, lax.axis_size(axis))
    arrived = lax.all_to_all(pieces, axis, split_axis=0, concat_axis=0, tiled=True)
    return arrived.sum(axis=0)


def laid_out(pieces, dim):
    lengths = list(pieces.shape[1:])
    lengths[dim] *= pieces.shape[0]
    return jnp.moveaxis(pieces, 0, dim).reshape(lengths)


def from_everyone(shard, axis):
    count = lax.axis_size(axis)
    return lax.all_to_all(
        jnp.broadcast_to(shard[None], (count, *shard.shape)), axis, 0, 0, tiled=True
    )


def gather_directly(shard, axis, dim):
    return laid_out(from_everyone(shard, axis), dim)


def pair_weights(own, near, scale_x, live):
    total = None
    for axis in range(3):
        diff = own[axis][None, :, :, None] - near[axis][:, :, None, :]
        diff = diff - jnp.floor(diff + 0.5)
        if axis == 0:
            diff = diff * scale_x
        total = diff * diff if total is None else total + diff * diff
    return (jnp.exp(-2.0 * total) * live[:, :, None, None]).astype(jnp.bfloat16)


def phase_tables(kf_rows, coords_group):
    theta = TWO_PI * (
        kf_rows[0][:, None] * coords_group[0][None, :]
        + kf_rows[1][:, None] * coords_group[1][None, :]
        + kf_rows[2][:, None] * coords_group[2][None, :]
    )
    return (jnp.cos(theta).astype(jnp.bfloat16), jnp.sin(theta).astype(jnp.bfloat16))


def short_range(hm_ext, pos_ext, coords, ext_index, live_slots, first, count, scale_x):
    chans = hm_ext.shape[0]
    hm3 = hm_ext.reshape(chans, -1, BLOCK)
    pos3 = pos_ext.reshape(3, -1, BLOCK)
    own3 = coords.reshape(3, -1, BLOCK)

    def short_step(index, buffer):
        blocks = first + index * 2 + jnp.arange(2, dtype=jnp.int32)
        idx = jnp.take(ext_index, blocks, axis=1)
        live = jnp.take(live_slots, blocks, axis=1).astype(jnp.float32)
        weights = pair_weights(jnp.take(own3, blocks, axis=1), pos3[:, idx], scale_x, live)
        near = hm3[:, idx]
        msg = jnp.einsum("csbj,sbij->cbi", near, weights, preferred_element_type=jnp.float32)
        msg = (msg * MSG_SCALE).astype(jnp.bfloat16).reshape(chans, 2 * BLOCK)
        return msg

    return lax.fori_loop(0, count // 2, short_step, jnp.zeros((chans, count * BLOCK), jnp.bfloat16))


def structure(kf_rows, coords, masked):
    size = 4 * BLOCK
    groups = masked.shape[1] // size
    chans = masked.shape[0]
    dims = (((1,), (1,)), ((), ()))

    def structure_step(index, acc):
        start = index * size
        pos = lax.dynamic_slice_in_dim(coords, start, size, 1)
        part = lax.dynamic_slice_in_dim(masked, start, size, 1)
        cosb, sinb = phase_tables(kf_rows, pos)
        term = jnp.concatenate(
            [
                lax.dot_general(cosb, part, dims, preferred_element_type=jnp.float32),
                lax.dot_general(sinb, part, dims, preferred_element_type=jnp.float32),
            ],
            axis=1,
        )
        return acc + term

    return lax.fori_loop(
        0, groups, structure_step, jnp.zeros((kf_rows.shape[1], 2 * chans), jnp.float32)
    )


def spectral(factor, gain, mixing, total):
    chans = mixing.shape[0]
    scaled = factor * (1.0 / math.sqrt(total))
    cos_part = jnp.dot(scaled[:, :chans], mixing, precision=lax.Precision.HIGHEST)
    sin_part = jnp.dot(scaled[:, chans:], mixing, precision=lax.Precision.HIGHEST)
    return (jnp.concatenate([cos_part, sin_part], axis=1) * gain[:, None]).astype(jnp.bfloat16)


def potentials(filtered, kf, coords):
    size = 4 * BLOCK
    chans = filtered.shape[1] // 2
    width = coords.shape[1]
    dims = (((0,), (0,)), ((), ()))

    def potentials_step(index, buffer):
        pos = lax.dynamic_slice_in_dim(coords, index * size, size, 1)
        cosb, sinb = phase_tables(kf, pos)
        term = lax.dot_general(
            filtered[:, :chans], cosb, dims, preferred_element_type=jnp.float32
        ) + lax.dot_general(filtered[:, chans:], sinb, dims, preferred_element_type=jnp.float32)
        return lax.dynamic_update_slice_in_dim(buffer, term * (1.0 / math.sqrt(K)), index * size, 1)

    return lax.fori_loop(0, width // size, potentials_step, jnp.zeros((chans, width), jnp.float32))


def update(h, msg, potential, live, first_layer, second_layer):
    stacked = jnp.concatenate([h, msg, potential.astype(jnp.bfloat16)], axis=0)
    hidden = jax.nn.silu(jnp.dot(first_layer, stacked, preferred_element_type=jnp.float32)).astype(
        jnp.bfloat16
    )
    out = h.astype(jnp.float32) + jnp.dot(second_layer, hidden, preferred_element_type=jnp.float32)
    return jnp.where(live[None, :], out, jnp.zeros_like(out)).astype(jnp.bfloat16)


def local(
    features,
    coords,
    neighbours,
    live_slots,
    block_count,
    kvec,
    msg_weight,
    filter_weight,
    mlp_in,
    mlp_out,
):
    width = features.shape[1]
    nblocks = width // BLOCK
    regions = lax.axis_size("atoms")
    groups_waves = lax.axis_size("waves")
    here = lax.axis_index("atoms")
    total = regions * width
    source = neighbours // nblocks
    offset = (source - here) % regions
    which = jnp.where(offset == 0, 1, jnp.where(offset == 1, 2, 0))
    ext_index = which * nblocks + neighbours % nblocks
    live_block = jnp.arange(nblocks, dtype=jnp.int32) < block_count[0]
    live = jnp.repeat(live_block, BLOCK)
    kf = kvec.astype(jnp.float32)
    kx = kf[0] / regions
    gain = GAIN_TOP / (4.0 + kx * kx + kf[1] * kf[1] + kf[2] * kf[2])
    wave_rows = kf.shape[1]
    pos_ext = with_halo(coords, (("atoms", 1),), width)
    h = features
    hm = jnp.dot(msg_weight[0], h, preferred_element_type=jnp.float32).astype(jnp.bfloat16)
    hm_ext = with_halo(hm, (("atoms", 1),), width)
    masked = jnp.where(live[None, :], h, jnp.zeros_like(h))
    owned = wave_rows // regions

    def term(start, count):
        return structure(kf, coords, masked)

    share = sent_and_summed(term(jnp.int32(0), owned * lax.axis_size("atoms")), "atoms", 0)
    gain_share = lax.dynamic_slice_in_dim(gain, here * owned, owned, 0)
    filtered_share = spectral(share, gain_share, filter_weight[0], total)
    filtered = gather_directly(filtered_share, "atoms", 0)
    partial_potential = potentials(filtered, kf, coords)
    per_group = nblocks // groups_waves
    first = lax.axis_index("waves") * per_group
    potential = sent_and_summed(partial_potential, "waves", 1)
    msg = short_range(hm_ext, pos_ext, coords, ext_index, live_slots, first, per_group, regions)
    h_share = lax.dynamic_slice_in_dim(h, first * BLOCK, per_group * BLOCK, 1)
    live_share = lax.dynamic_slice_in_dim(live, first * BLOCK, per_group * BLOCK, 0)
    new_share = update(h_share, msg, potential, live_share, mlp_in[0], mlp_out[0])
    h = gather_directly(new_share, "waves", 1)
    return h


def solution(mesh):
    in_specs = (
        P(None, "atoms"),
        P(None, "atoms"),
        P(None, "atoms"),
        P(None, "atoms"),
        P("atoms"),
        P(None, "waves"),
        P(),
        P(),
        P(),
        P(),
    )
    out_specs = P(None, "atoms")
    return jax.shard_map(local, mesh=mesh, in_specs=in_specs, out_specs=out_specs, check_vma=False)
```

profile of v0, /device:TPU:32, one launch (start us, length us, event | category | flops | bytes accessed | tf_op | source)
XLA Modules:
  0.0 154.6 jit_solution(1323257170041877949)
XLA Ops:
  0.0 1.2 convolution_convert_fusion
  1.3 3.8 %collective-permute-start.3 = (bf16[64,2048]{1,0:T(8,128)(2,1)S(1)}, bf16[64,2048]{1,0:T(8,128)(2,1)S(1)}, u32[]{:S(2)}, u32[]{:S(2)}) collective-permute-start(bf16[64,2048]{1,0:T(8,128)(2,1)S(1)} %convolution_convert_fusion), channel_id=1, source_target_pairs={{8,0},{16,8},{24,16},{32,24},{40,32},{48,40},{56,48},{64,56},{72,6... | collective-permute-start | bytes 786440 | tf_op jit(solution)/shard_map/ppermute | solution.py:26
  5.1 3.9 %collective-permute-start.1 = (f32[3,2048]{1,0:T(4,128)}, f32[3,2048]{1,0:T(4,128)S(1)}, u32[]{:S(2)}, u32[]{:S(2)}) collective-permute-start(f32[3,2048]{1,0:T(4,128)} %param.17), channel_id=1, source_target_pairs={{8,0},{16,8},{24,16},{32,24},{40,32},{48,40},{56,48},{64,56},{72,6... | collective-permute-start | bytes 73736 | tf_op jit(solution)/shard_map/ppermute | solution.py:26
  9.0 0.7 convert_element_type.74
  10.4 1.0 broadcast_select_fusion
  11.4 32.2 %while.33 = (s32[]{:T(128)}, f32[512,128]{0,1:T(8,128)S(1)}, f32[3,512]{1,0:T(4,128)S(1)}, f32[3,2048]{1,0:T(4,128)S(1)}, bf16[64,2048]{1,0:T(8,128)(2,1)S(1)}, ...) while((s32[]{:T(128)}, f32[512,128]{0,1:T(8,128)S(1)}, ...), condition=%wide.region_1.3_spmd.clone, body=%wide.region_0.2_spmd.clone.sunk | while | flops 70975496 | bytes 1229009 | solution.py:121
  11.5 3.9 %fusion.114 = f32[512,64]{0,1:T(8,128)S(1)} fusion(f32[512]{0:T(512)S(1)} %bitcast.156, f32[512]{0:T(512)S(1)} %bitcast.160, f32[512]{0:T(512)S(1)} %bitcast.154, f32[512]{0:T(512)S(1)} %bitcast.158, f32[512]{0:T(512)S(1)} %bitcast.152, f32[512]{0:T(512)S(1)} %bitcast.162, bf16[64,2048]{1,0:T(8,128)(2,1)S(1)} %get-tuple-element.399, s32[]{:T(128)S(6)} %select_n.143), kind=kOutput, calls=%fused_computation.28.clone.1 | convolution fusion | flops 35389440 | bytes 208900 | tf_op jit(solution)/shard_map/while/body/eval_jaxpr/dot_general | solution.py:114
  15.4 3.9 %fusion.113 = f32[512,64]{0,1:T(8,128)S(1)} fusion(f32[512]{0:T(512)S(1)} %bitcast.157, f32[512]{0:T(512)S(1)} %bitcast.161, f32[512]{0:T(512)S(1)} %bitcast.155, f32[512]{0:T(512)S(1)} %bitcast.159, f32[512]{0:T(512)S(1)} %bitcast.153, f32[512]{0:T(512)S(1)} %bitcast.163, bf16[64,2048]{1,0:T(8,128)(2,1)S(1)} %get-tuple-element.399, s32[]{:T(128)S(6)} %select_n.143), kind=kOutput, calls=%fused_computation.29.clone.1 | convolution fusion | flops 35389440 | bytes 208900 | tf_op jit(solution)/shard_map/while/body/eval_jaxpr/dot_general | solution.py:115
  19.6 3.9 %fusion.114 = f32[512,64]{0,1:T(8,128)S(1)} fusion(f32[512]{0:T(512)S(1)} %bitcast.156, f32[512]{0:T(512)S(1)} %bitcast.160, f32[512]{0:T(512)S(1)} %bitcast.154, f32[512]{0:T(512)S(1)} %bitcast.158, f32[512]{0:T(512)S(1)} %bitcast.152, f32[512]{0:T(512)S(1)} %bitcast.162, bf16[64,2048]{1,0:T(8,128)(2,1)S(1)} %get-tuple-element.399, s32[]{:T(128)S(6)} %select_n.143), kind=kOutput, calls=%fused_computation.28.clone.1 | convolution fusion | flops 35389440 | bytes 208900 | tf_op jit(solution)/shard_map/while/body/eval_jaxpr/dot_general | solution.py:114
  23.5 3.9 %fusion.113 = f32[512,64]{0,1:T(8,128)S(1)} fusion(f32[512]{0:T(512)S(1)} %bitcast.157, f32[512]{0:T(512)S(1)} %bitcast.161, f32[512]{0:T(512)S(1)} %bitcast.155, f32[512]{0:T(512)S(1)} %bitcast.159, f32[512]{0:T(512)S(1)} %bitcast.153, f32[512]{0:T(512)S(1)} %bitcast.163, bf16[64,2048]{1,0:T(8,128)(2,1)S(1)} %get-tuple-element.399, s32[]{:T(128)S(6)} %select_n.143), kind=kOutput, calls=%fused_computation.29.clone.1 | convolution fusion | flops 35389440 | bytes 208900 | tf_op jit(solution)/shard_map/while/body/eval_jaxpr/dot_general | solution.py:115
  27.6 3.9 %fusion.114 = f32[512,64]{0,1:T(8,128)S(1)} fusion(f32[512]{0:T(512)S(1)} %bitcast.156, f32[512]{0:T(512)S(1)} %bitcast.160, f32[512]{0:T(512)S(1)} %bitcast.154, f32[512]{0:T(512)S(1)} %bitcast.158, f32[512]{0:T(512)S(1)} %bitcast.152, f32[512]{0:T(512)S(1)} %bitcast.162, bf16[64,2048]{1,0:T(8,128)(2,1)S(1)} %get-tuple-element.399, s32[]{:T(128)S(6)} %select_n.143), kind=kOutput, calls=%fused_computation.28.clone.1 | convolution fusion | flops 35389440 | bytes 208900 | tf_op jit(solution)/shard_map/while/body/eval_jaxpr/dot_general | solution.py:114
  31.5 3.9 %fusion.113 = f32[512,64]{0,1:T(8,128)S(1)} fusion(f32[512]{0:T(512)S(1)} %bitcast.157, f32[512]{0:T(512)S(1)} %bitcast.161, f32[512]{0:T(512)S(1)} %bitcast.155, f32[512]{0:T(512)S(1)} %bitcast.159, f32[512]{0:T(512)S(1)} %bitcast.153, f32[512]{0:T(512)S(1)} %bitcast.163, bf16[64,2048]{1,0:T(8,128)(2,1)S(1)} %get-tuple-element.399, s32[]{:T(128)S(6)} %select_n.143), kind=kOutput, calls=%fused_computation.29.clone.1 | convolution fusion | flops 35389440 | bytes 208900 | tf_op jit(solution)/shard_map/while/body/eval_jaxpr/dot_general | solution.py:115
  35.6 3.9 %fusion.114 = f32[512,64]{0,1:T(8,128)S(1)} fusion(f32[512]{0:T(512)S(1)} %bitcast.156, f32[512]{0:T(512)S(1)} %bitcast.160, f32[512]{0:T(512)S(1)} %bitcast.154, f32[512]{0:T(512)S(1)} %bitcast.158, f32[512]{0:T(512)S(1)} %bitcast.152, f32[512]{0:T(512)S(1)} %bitcast.162, bf16[64,2048]{1,0:T(8,128)(2,1)S(1)} %get-tuple-element.399, s32[]{:T(128)S(6)} %select_n.143), kind=kOutput, calls=%fused_computation.28.clone.1 | convolution fusion | flops 35389440 | bytes 208900 | tf_op jit(solution)/shard_map/while/body/eval_jaxpr/dot_general | solution.py:114
  39.5 3.9 %fusion.113 = f32[512,64]{0,1:T(8,128)S(1)} fusion(f32[512]{0:T(512)S(1)} %bitcast.157, f32[512]{0:T(512)S(1)} %bitcast.161, f32[512]{0:T(512)S(1)} %bitcast.155, f32[512]{0:T(512)S(1)} %bitcast.159, f32[512]{0:T(512)S(1)} %bitcast.153, f32[512]{0:T(512)S(1)} %bitcast.163, bf16[64,2048]{1,0:T(8,128)(2,1)S(1)} %get-tuple-element.399, s32[]{:T(128)S(6)} %select_n.143), kind=kOutput, calls=%fused_computation.29.clone.1 | convolution fusion | flops 35389440 | bytes 208900 | tf_op jit(solution)/shard_map/while/body/eval_jaxpr/dot_general | solution.py:115
  43.6 0.8 copy.36
  44.4 9.0 %all-to-all-start = ((f32[32,16,128]{2,1,0:T(8,128)}), f32[32,16,128]{2,1,0:T(8,128)S(1)}, u32[]{:S(2)}, u32[]{:S(2)}) async-start(f32[32,16,128]{2,1,0:T(8,128)} %bitcast.30), calls=%async_computation | async-start | bytes 524288 | tf_op jit(solution)/shard_map/all_to_all | solution.py:41
  53.6 0.6 gather_fusion.3
  54.1 0.6 gather_fusion.4
  54.9 0.6 gather_fusion
  55.6 7.9 %all-to-all-done = f32[32,16,128]{2,1,0:T(8,128)S(1)} async-done(((f32[32,16,128]{2,1,0:T(8,128)}), f32[32,16,128]{2,1,0:T(8,128)S(1)}, u32[]{:S(2)}, u32[]{:S(2)}) %all-to-all-start) | async-done | bytes 262176 | tf_op jit(solution)/shard_map/all_to_all | solution.py:41
  63.6 0.2 fusion.67
  63.8 0.1 fusion.69
  64.0 0.7 broadcast_in_dim.93
  64.7 4.8 %all-to-all-start.1 = ((bf16[32,16,128]{2,1,0:T(8,128)(2,1)}), bf16[32,16,128]{2,1,0:T(8,128)(2,1)S(1)}, u32[]{:S(2)}, u32[]{:S(2)}) async-start(bf16[32,16,128]{2,1,0:T(8,128)(2,1)} %broadcast_in_dim.93), calls=%async_computation.1 | async-start | bytes 262144 | tf_op jit(solution)/shard_map/all_to_all | solution.py:53
  69.6 0.8 constant_dynamic-slice_fusion.5
  70.3 0.1 copy.29
  70.4 0.1 reshape.144
  70.7 0.6 gather_fusion.1
  71.3 5.8 %all-to-all-done.1 = bf16[32,16,128]{2,1,0:T(8,128)(2,1)S(1)} async-done(((bf16[32,16,128]{2,1,0:T(8,128)(2,1)}), bf16[32,16,128]{2,1,0:T(8,128)(2,1)S(1)}, u32[]{:S(2)}, u32[]{:S(2)}) %all-to-all-start.1) | async-done | bytes 131104 | tf_op jit(solution)/shard_map/all_to_all | solution.py:53
  77.1 32.0 %while.32 = (s32[]{:T(128)}, f32[64,2048]{1,0:T(8,128)S(1)}, f32[3,512]{1,0:T(4,128)S(1)}, f32[3,2048]{1,0:T(4,128)S(1)}, bf16[512,128]{1,0:T(8,128)(2,1)S(1)}, ...) while((s32[]{:T(128)}, f32[64,2048]{1,0:T(8,128)S(1)}, ...), condition=%wide.region_4.6_spmd, body=%wide.region_3.5_spmd.sunk | while | flops 70844424 | bytes 704707 | solution.py:148
  77.2 3.9 %fusion.109 = f32[512,64]{0,1:T(8,128)S(1)} fusion(f32[512]{0:T(512)S(1)} %bitcast.144, f32[512]{0:T(512)S(1)} %bitcast.148, f32[512]{0:T(512)S(1)} %bitcast.142, f32[512]{0:T(512)S(1)} %bitcast.146, f32[512]{0:T(512)S(1)} %bitcast.140, f32[512]{0:T(512)S(1)} %bitcast.150, bf16[512,128]{1,0:T(8,128)(2,1)S(1)} %get-tuple-element.432), kind=kOutput, calls=%fused_computation.19.clone.1 | convolution fusion | flops 35389440 | bytes 274432 | tf_op jit(solution)/shard_map/while/body/eval_jaxpr/dot_general | solution.py:143
  81.1 4.0 %fusion.110 = f32[64,2048]{1,0:T(8,128)S(1)} fusion(f32[64,2048]{1,0:T(8,128)S(1)} %get-tuple-element.418, s32[]{:T(128)S(6)} %select_n.142, f32[512,64]{0,1:T(8,128)S(1)} %fusion.109, f32[512]{0:T(512)S(1)} %bitcast.145, f32[512]{0:T(512)S(1)} %bitcast.149, f32[512]{0:T(512)S(1)} %bitcast.143, f32[512]{0:T(512)S(1)} %bitcast.147, ...), kind=kOutput, calls=%fused_computation.8.clone.1 | convolution fusion | flops 35454976 | bytes 405508 | tf_op jit(solution)/shard_map/while/body/eval_jaxpr/dot_general | solution.py:145
  85.2 3.9 %fusion.109 = f32[512,64]{0,1:T(8,128)S(1)} fusion(f32[512]{0:T(512)S(1)} %bitcast.144, f32[512]{0:T(512)S(1)} %bitcast.148, f32[512]{0:T(512)S(1)} %bitcast.142, f32[512]{0:T(512)S(1)} %bitcast.146, f32[512]{0:T(512)S(1)} %bitcast.140, f32[512]{0:T(512)S(1)} %bitcast.150, bf16[512,128]{1,0:T(8,128)(2,1)S(1)} %get-tuple-element.432), kind=kOutput, calls=%fused_computation.19.clone.1 | convolution fusion | flops 35389440 | bytes 274432 | tf_op jit(solution)/shard_map/while/body/eval_jaxpr/dot_general | solution.py:143
  89.1 4.0 %fusion.110 = f32[64,2048]{1,0:T(8,128)S(1)} fusion(f32[64,2048]{1,0:T(8,128)S(1)} %get-tuple-element.418, s32[]{:T(128)S(6)} %select_n.142, f32[512,64]{0,1:T(8,128)S(1)} %fusion.109, f32[512]{0:T(512)S(1)} %bitcast.145, f32[512]{0:T(512)S(1)} %bitcast.149, f32[512]{0:T(512)S(1)} %bitcast.143, f32[512]{0:T(512)S(1)} %bitcast.147, ...), kind=kOutput, calls=%fused_computation.8.clone.1 | convolution fusion | flops 35454976 | bytes 405508 | tf_op jit(solution)/shard_map/while/body/eval_jaxpr/dot_general | solution.py:145
  93.2 3.9 %fusion.109 = f32[512,64]{0,1:T(8,128)S(1)} fusion(f32[512]{0:T(512)S(1)} %bitcast.144, f32[512]{0:T(512)S(1)} %bitcast.148, f32[512]{0:T(512)S(1)} %bitcast.142, f32[512]{0:T(512)S(1)} %bitcast.146, f32[512]{0:T(512)S(1)} %bitcast.140, f32[512]{0:T(512)S(1)} %bitcast.150, bf16[512,128]{1,0:T(8,128)(2,1)S(1)} %get-tuple-element.432), kind=kOutput, calls=%fused_computation.19.clone.1 | convolution fusion | flops 35389440 | bytes 274432 | tf_op jit(solution)/shard_map/while/body/eval_jaxpr/dot_general | solution.py:143
  97.1 4.0 %fusion.110 = f32[64,2048]{1,0:T(8,128)S(1)} fusion(f32[64,2048]{1,0:T(8,128)S(1)} %get-tuple-element.418, s32[]{:T(128)S(6)} %select_n.142, f32[512,64]{0,1:T(8,128)S(1)} %fusion.109, f32[512]{0:T(512)S(1)} %bitcast.145, f32[512]{0:T(512)S(1)} %bitcast.149, f32[512]{0:T(512)S(1)} %bitcast.143, f32[512]{0:T(512)S(1)} %bitcast.147, ...), kind=kOutput, calls=%fused_computation.8.clone.1 | convolution fusion | flops 35454976 | bytes 405508 | tf_op jit(solution)/shard_map/while/body/eval_jaxpr/dot_general | solution.py:145
  101.2 3.9 %fusion.109 = f32[512,64]{0,1:T(8,128)S(1)} fusion(f32[512]{0:T(512)S(1)} %bitcast.144, f32[512]{0:T(512)S(1)} %bitcast.148, f32[512]{0:T(512)S(1)} %bitcast.142, f32[512]{0:T(512)S(1)} %bitcast.146, f32[512]{0:T(512)S(1)} %bitcast.140, f32[512]{0:T(512)S(1)} %bitcast.150, bf16[512,128]{1,0:T(8,128)(2,1)S(1)} %get-tuple-element.432), kind=kOutput, calls=%fused_computation.19.clone.1 | convolution fusion | flops 35389440 | bytes 274432 | tf_op jit(solution)/shard_map/while/body/eval_jaxpr/dot_general | solution.py:143
  105.1 4.0 %fusion.110 = f32[64,2048]{1,0:T(8,128)S(1)} fusion(f32[64,2048]{1,0:T(8,128)S(1)} %get-tuple-element.418, s32[]{:T(128)S(6)} %select_n.142, f32[512,64]{0,1:T(8,128)S(1)} %fusion.109, f32[512]{0:T(512)S(1)} %bitcast.145, f32[512]{0:T(512)S(1)} %bitcast.149, f32[512]{0:T(512)S(1)} %bitcast.143, f32[512]{0:T(512)S(1)} %bitcast.147, ...), kind=kOutput, calls=%fused_computation.8.clone.1 | convolution fusion | flops 35454976 | bytes 405508 | tf_op jit(solution)/shard_map/while/body/eval_jaxpr/dot_general | solution.py:145
  109.1 0.2 copy.43
  109.3 1.0 copy.37
  110.3 9.4 %all-to-all-start.2 = ((f32[8,64,256]{2,1,0:T(8,128)}), f32[8,64,256]{2,1,0:T(8,128)S(1)}, u32[]{:S(2)}, u32[]{:S(2)}) async-start(f32[8,64,256]{2,1,0:T(8,128)} %copy.37), calls=%async_computation.2 | async-start | bytes 1048576 | tf_op jit(solution)/shard_map/all_to_all | solution.py:41
  119.8 0.2 copy_bitcast_fusion
  120.0 0.7 gather_fusion.2
  120.7 3.0 %fusion.50 = bf16[2,8,8,128]{3,2,1,0:T(8,128)(2,1)S(1)} fusion(f32[27,2]{0,1:T(2,128)S(1)} %bitcast_convert_fusion, f32[27,2,128]{2,0,1:T(8,128)S(1)} %copy.32, f32[2,128]{1,0:T(2,128)S(1)} %bitcast.166, f32[27,2,128]{2,0,1:T(8,128)S(1)} %copy.31, f32[2,128]{1,0:T(2,128)S(1)} %bitcast.167, f32[27,2,128]{2,0,1:T(8,128)S(1)} %copy.30, ...), kind=kOutput, calls=%fused_computation.67 | convolution fusion | flops 131858432 | bytes 1003736 | tf_op jit(solution)/shard_map/while/body/eval_jaxpr/csbj,sbij->cbi/dot_general | solution.py:94
  123.8 15.2 %all-to-all-done.2 = f32[8,64,256]{2,1,0:T(8,128)S(1)} async-done(((f32[8,64,256]{2,1,0:T(8,128)}), f32[8,64,256]{2,1,0:T(8,128)S(1)}, u32[]{:S(2)}, u32[]{:S(2)}) %all-to-all-start.2) | async-done | bytes 524320 | tf_op jit(solution)/shard_map/all_to_all | solution.py:41
  139.0 0.4 fusion.49
  139.4 14.4 %all_to_all.20 = bf16[8,64,256]{2,1,0:T(8,128)(2,1)S(1)} all-to-all(bf16[8,64,256]{2,1,0:T(8,128)(2,1)S(1)} %broadcast_in_dim.95), channel_id=1, replica_groups=mesh['atoms'=32,'waves'=8] {'waves'}, dimensions={0} | all-to-all | bytes 524288 | tf_op jit(solution)/shard_map/all_to_all | solution.py:53
  153.8 0.7 copy.42
  (59 shorter events, 2.0 us)
Async XLA Ops:
  0.0 139.0 %copy-start = (bf16[1,128,192]{1,2,0:T(8,128)(2,1)S(1)}, bf16[1,128,192]{1,2,0:T(8,128)(2,1)}, u32[]{:S(2)}) copy-start(bf16[1,128,192]{1,2,0:T(8,128)(2,1)} %param.24) | copy-start | bytes 147460
  0.0 11.4 %copy-start.2 = (f32[3,2048]{1,0:T(4,128)S(1)}, f32[3,2048]{1,0:T(4,128)}, u32[]{:S(2)}) copy-start(f32[3,2048]{1,0:T(4,128)} %param.17) | copy-start | bytes 73732
  1.2 118.5 %collective-permute-start.2 = (bf16[64,2048]{1,0:T(8,128)(2,1)S(1)}, bf16[64,2048]{1,0:T(8,128)(2,1)S(1)}, u32[]{:S(2)}, u32[]{:S(2)}) collective-permute-start(bf16[64,2048]{1,0:T(8,128)(2,1)S(1)} %convolution_convert_fusion), channel_id=1, source_target_pairs={{0,8},{8,16},{16,24},{24,32},{32,40},{40,48},{48,56},{56,64},{64,7... | collective-permute-start | bytes 786440 | tf_op jit(solution)/shard_map/ppermute | solution.py:24
  1.3 118.5 %collective-permute-start.3 = (bf16[64,2048]{1,0:T(8,128)(2,1)S(1)}, bf16[64,2048]{1,0:T(8,128)(2,1)S(1)}, u32[]{:S(2)}, u32[]{:S(2)}) collective-permute-start(bf16[64,2048]{1,0:T(8,128)(2,1)S(1)} %convolution_convert_fusion), channel_id=1, source_target_pairs={{8,0},{16,8},{24,16},{32,24},{40,32},{48,40},{56,48},{64,56},{72,6... | collective-permute-start | bytes 786440 | tf_op jit(solution)/shard_map/ppermute | solution.py:26
  5.1 65.5 %collective-permute-start = (f32[3,2048]{1,0:T(4,128)}, f32[3,2048]{1,0:T(4,128)S(1)}, u32[]{:S(2)}, u32[]{:S(2)}) collective-permute-start(f32[3,2048]{1,0:T(4,128)} %param.17), channel_id=1, source_target_pairs={{0,8},{8,16},{16,24},{24,32},{32,40},{40,48},{48,56},{56,64},{64,7... | collective-permute-start | bytes 73736 | tf_op jit(solution)/shard_map/ppermute | solution.py:24
  5.1 65.5 %collective-permute-start.1 = (f32[3,2048]{1,0:T(4,128)}, f32[3,2048]{1,0:T(4,128)S(1)}, u32[]{:S(2)}, u32[]{:S(2)}) collective-permute-start(f32[3,2048]{1,0:T(4,128)} %param.17), channel_id=1, source_target_pairs={{8,0},{16,8},{24,16},{32,24},{40,32},{48,40},{56,48},{64,56},{72,6... | collective-permute-start | bytes 73736 | tf_op jit(solution)/shard_map/ppermute | solution.py:26
  43.6 10.0 %copy-start.4 = (s32[27,16]{0,1:T(8,128)S(1)}, s32[27,16]{0,1:T(8,128)}, u32[]{:S(2)}) copy-start(s32[27,16]{0,1:T(8,128)} %param.18) | copy-start | bytes 5188
  43.6 10.6 %copy-start.1 = (s32[27,16]{0,1:T(8,128)S(1)}, s32[27,16]{0,1:T(8,128)}, u32[]{:S(2)}) copy-start(s32[27,16]{0,1:T(8,128)} %param.19) | copy-start | bytes 5188
  43.6 20.0 %copy-start.3 = (f32[1,64,64]{2,1,0:T(8,128)S(1)}, f32[1,64,64]{2,1,0:T(8,128)}, u32[]{:S(2)}) copy-start(f32[1,64,64]{2,1,0:T(8,128)} %param.23) | copy-start | bytes 49156
  44.4 19.1 %all-to-all-start = ((f32[32,16,128]{2,1,0:T(8,128)}), f32[32,16,128]{2,1,0:T(8,128)S(1)}, u32[]{:S(2)}, u32[]{:S(2)}) async-start(f32[32,16,128]{2,1,0:T(8,128)} %bitcast.30), calls=%async_computation | async-start | bytes 524288 | tf_op jit(solution)/shard_map/all_to_all | solution.py:41
  64.7 12.4 %all-to-all-start.1 = ((bf16[32,16,128]{2,1,0:T(8,128)(2,1)}), bf16[32,16,128]{2,1,0:T(8,128)(2,1)S(1)}, u32[]{:S(2)}, u32[]{:S(2)}) async-start(bf16[32,16,128]{2,1,0:T(8,128)(2,1)} %broadcast_in_dim.93), calls=%async_computation.1 | async-start | bytes 262144 | tf_op jit(solution)/shard_map/all_to_all | solution.py:53
  110.3 28.7 %all-to-all-start.2 = ((f32[8,64,256]{2,1,0:T(8,128)}), f32[8,64,256]{2,1,0:T(8,128)S(1)}, u32[]{:S(2)}, u32[]{:S(2)}) async-start(f32[8,64,256]{2,1,0:T(8,128)} %copy.37), calls=%async_computation.2 | async-start | bytes 1048576 | tf_op jit(solution)/shard_map/all_to_all | solution.py:41
  120.7 18.3 %copy-start.5 = (bf16[1,64,128]{2,1,0:T(8,128)(2,1)S(1)}, bf16[1,64,128]{2,1,0:T(8,128)(2,1)}, u32[]{:S(2)}) copy-start(bf16[1,64,128]{2,1,0:T(8,128)(2,1)} %param.25) | copy-start | bytes 49156
where the time goes:
time: 155 us
  matrix products  67.8 us (44%)
  starting transfers between devices  31 us (20%)
  waiting for transfers between devices  28.9 us (19%)
  blocking collectives  14.4 us (9%)
  local copies, waits for them, and re-layouts  8.39 us (5%)
  other arithmetic  2.79 us (2%)
    all_to_all x2, waiting for transfers between devices, sent_and_summed(): lax.all_to_all(pieces, axis, split_axis=0, concat_axis=0, tiled=True)  23.1 us
    all_to_all x2, starting transfers between devices, sent_and_summed(): lax.all_to_all(pieces, axis, split_axis=0, concat_axis=0, tiled=True)  18.4 us
    dot_general x4, matrix products, potentials_step(): lax.dot_general(filtered[:, chans:], sinb, dims, preferred_element_type=j...  15.9 us
    dot_general x4, matrix products, structure_step(): lax.dot_general(sinb, part, dims, preferred_element_type=jnp.float32)  15.7 us
    dot_general x4, matrix products, potentials_step(): lax.dot_general(filtered[:, :chans], cosb, dims, preferred_element_type=j...  15.7 us
    dot_general x4, matrix products, structure_step(): lax.dot_general(cosb, part, dims, preferred_element_type=jnp.float32)  15.6 us
    all_to_all x1, blocking collectives, from_everyone(): lax.all_to_all(jnp.broadcast_to(shard[None], (count, *shard.shape)), axis...  14.4 us
    ppermute x2, starting transfers between devices, with_halo(): lax.ppermute(head, axis, [((i + 1) % count, i) for i in range(count)])  7.69 us
  transfers between devices with their start and end apart: 7, of which 3 were waited for; matrix products, arithmetic and copies ran while one was open for 50% of the time, Pallas kernels for 0%

commit v1 on v0

--- a/solution.py
+++ b/solution.py
@@ -1,8 +1,11 @@
+import functools
 import math
 
 import jax
 import jax.numpy as jnp
 from jax import lax
+from jax.experimental import pallas as pl
+from jax.experimental.pallas import tpu as pltpu
 from jax.sharding import PartitionSpec as P
 
 K = 4096
@@ -30,18 +33,6 @@
     return cells
 
 
-def in_blocks(shard, dim, count):
-    lengths = shard.shape
-    pieces = shard.reshape(*lengths[:dim], count, lengths[dim] // count, *lengths[dim + 1 :])
-    return jnp.moveaxis(pieces, dim, 0)
-
-
-def sent_and_summed(shard, axis, dim):
-    pieces = in_blocks(shard, dim, lax.axis_size(axis))
-    arrived = lax.all_to_all(pieces, axis, split_axis=0, concat_axis=0, tiled=True)
-    return arrived.sum(axis=0)
-
-
 def laid_out(pieces, dim):
     lengths = list(pieces.shape[1:])
     lengths[dim] *= pieces.shape[0]
@@ -70,15 +61,6 @@
     return (jnp.exp(-2.0 * total) * live[:, :, None, None]).astype(jnp.bfloat16)
 
 
-def phase_tables(kf_rows, coords_group):
-    theta = TWO_PI * (
-        kf_rows[0][:, None] * coords_group[0][None, :]
-        + kf_rows[1][:, None] * coords_group[1][None, :]
-        + kf_rows[2][:, None] * coords_group[2][None, :]
-    )
-    return (jnp.cos(theta).astype(jnp.bfloat16), jnp.sin(theta).astype(jnp.bfloat16))
-
-
 def short_range(hm_ext, pos_ext, coords, ext_index, live_slots, first, count, scale_x):
     chans = hm_ext.shape[0]
     hm3 = hm_ext.reshape(chans, -1, BLOCK)
@@ -98,29 +80,111 @@
     return lax.fori_loop(0, count // 2, short_step, jnp.zeros((chans, count * BLOCK), jnp.bfloat16))
 
 
-def structure(kf_rows, coords, masked):
-    size = 4 * BLOCK
-    groups = masked.shape[1] // size
-    chans = masked.shape[0]
-    dims = (((1,), (1,)), ((), ()))
-
-    def structure_step(index, acc):
-        start = index * size
-        pos = lax.dynamic_slice_in_dim(coords, start, size, 1)
-        part = lax.dynamic_slice_in_dim(masked, start, size, 1)
-        cosb, sinb = phase_tables(kf_rows, pos)
-        term = jnp.concatenate(
-            [
-                lax.dot_general(cosb, part, dims, preferred_element_type=jnp.float32),
-                lax.dot_general(sinb, part, dims, preferred_element_type=jnp.float32),
-            ],
-            axis=1,
+SIN_COEFS = (3.1415926401307073, -5.167710083507923, 2.5500775232148563, -0.5982912856211671, 0.07765766030589402)
+COS_COEFS = (0.9999999532476085, -4.934792830619664, 4.058411352862771, -1.3318765680813944, 0.21968961109803095)
+ROOT2 = math.sqrt(2.0)
+VMEM_SPEC = pl.BlockSpec(memory_space=pltpu.VMEM)
+
+
+def horner(coefs, scale, u):
+    value = coefs[-1] * scale
+    for coef in coefs[-2::-1]:
+        value = value * u + coef * scale
+    return value
+
+
+def phases_of(turns):
+    r = turns - jnp.round(turns)
+    u = r * r
+    s = r * horner(SIN_COEFS, ROOT2, u)
+    c = horner(COS_COEFS, ROOT2, u)
+    return 1.0 - s * s, s * c
+
+
+def three_pieces(values):
+    first = values.astype(jnp.bfloat16)
+    rest = values - first.astype(jnp.float32)
+    second = rest.astype(jnp.bfloat16)
+    third = (rest - second.astype(jnp.float32)).astype(jnp.bfloat16)
+    return first.astype(jnp.float32), second.astype(jnp.float32), third.astype(jnp.float32)
+
+
+def structure_kernel(tile, kf_ref, coords_ref, h_ref, count_ref, table_ref, out_ref, ka_ref, xs_ref):
+    waves = kf_ref.shape[1]
+    atoms = coords_ref.shape[1]
+    chans = h_ref.shape[0]
+    kf = kf_ref[...].astype(jnp.float32)
+    pad_k = jnp.zeros((7, waves), jnp.float32)
+    ka = jnp.concatenate([kf, kf, kf, pad_k], axis=0)
+    ka_ref[...] = ka.T.astype(jnp.bfloat16)
+    first, second, third = three_pieces(coords_ref[...])
+    xs = jnp.concatenate([first, second, third, jnp.zeros((7, atoms), jnp.float32)], axis=0)
+    xs_ref[...] = xs.astype(jnp.bfloat16)
+    live_atoms = count_ref[0] * BLOCK
+    rows = 64
+    acc = jnp.zeros((waves, 2 * chans), jnp.float32)
+    nt = (((1,), (1,)), ((), ()))
+    for start in range(0, atoms, tile):
+        xt = xs_ref[:, start : start + tile]
+        for k in range(0, waves, rows):
+            turns = jnp.dot(ka_ref[k : k + rows, :], xt, preferred_element_type=jnp.float32)
+            cosv, sinv = phases_of(turns)
+            table_ref[k : k + rows, start : start + tile] = cosv.astype(jnp.bfloat16)
+            table_ref[k : k + rows, atoms + start : atoms + start + tile] = sinv.astype(jnp.bfloat16)
+        lane = lax.broadcasted_iota(jnp.int32, (chans, tile), 1) + start
+        ht = jnp.where(lane < live_atoms, h_ref[:, start : start + tile].astype(jnp.float32), 0.0)
+        zero = jnp.zeros_like(ht)
+        hc = jnp.concatenate([ht, zero], axis=0).astype(jnp.bfloat16)
+        hs = jnp.concatenate([zero, ht], axis=0).astype(jnp.bfloat16)
+        acc = acc + lax.dot_general(table_ref[:, start : start + tile], hc, nt, preferred_element_type=jnp.float32)
+        acc = acc + lax.dot_general(
+            table_ref[:, atoms + start : atoms + start + tile], hs, nt, preferred_element_type=jnp.float32
         )
-        return acc + term
-
-    return lax.fori_loop(
-        0, groups, structure_step, jnp.zeros((kf_rows.shape[1], 2 * chans), jnp.float32)
-    )
+    out_ref[...] = acc.astype(jnp.bfloat16).reshape(out_ref.shape)
+
+
+def structure(kvec, coords, h, count, pieces):
+    waves, atoms, chans = kvec.shape[1], coords.shape[1], h.shape[0]
+    return pl.pallas_call(
+        functools.partial(structure_kernel, 256),
+        out_shape=(
+            jax.ShapeDtypeStruct((waves, 2 * atoms), jnp.bfloat16),
+            jax.ShapeDtypeStruct((pieces, waves // pieces, 2 * chans), jnp.bfloat16),
+        ),
+        in_specs=[VMEM_SPEC, VMEM_SPEC, VMEM_SPEC, pl.BlockSpec(memory_space=pltpu.SMEM)],
+        out_specs=(VMEM_SPEC, VMEM_SPEC),
+        scratch_shapes=[pltpu.VMEM((waves, 16), jnp.bfloat16), pltpu.VMEM((16, atoms), jnp.bfloat16)],
+        name="structure",
+    )(kvec, coords, h, count)
+
+
+def potentials_kernel(filtered_ref, table_ref, out_ref):
+    chans = out_ref.shape[1]
+    pieces, _, width = out_ref.shape
+    atoms = pieces * width
+    tn = (((0,), (0,)), ((), ()))
+    fc = filtered_ref[:, :chans]
+    fs = filtered_ref[:, chans:]
+    for piece in range(pieces):
+        start = piece * width
+        term = lax.dot_general(
+            fc, table_ref[:, start : start + width], tn, preferred_element_type=jnp.float32
+        ) + lax.dot_general(
+            fs, table_ref[:, atoms + start : atoms + start + width], tn, preferred_element_type=jnp.float32
+        )
+        out_ref[piece] = (term * (1.0 / math.sqrt(K))).astype(jnp.bfloat16)
+
+
+def potentials(filtered, table, pieces):
+    chans = filtered.shape[1] // 2
+    atoms = table.shape[1] // 2
+    return pl.pallas_call(
+        potentials_kernel,
+        out_shape=jax.ShapeDtypeStruct((pieces, chans, atoms // pieces), jnp.bfloat16),
+        in_specs=[VMEM_SPEC, VMEM_SPEC],
+        out_specs=VMEM_SPEC,
+        name="potentials",
+    )(filtered, table)
 
 
 def spectral(factor, gain, mixing, total):
@@ -129,23 +193,6 @@
     cos_part = jnp.dot(scaled[:, :chans], mixing, precision=lax.Precision.HIGHEST)
     sin_part = jnp.dot(scaled[:, chans:], mixing, precision=lax.Precision.HIGHEST)
     return (jnp.concatenate([cos_part, sin_part], axis=1) * gain[:, None]).astype(jnp.bfloat16)
-
-
-def potentials(filtered, kf, coords):
-    size = 4 * BLOCK
-    chans = filtered.shape[1] // 2
-    width = coords.shape[1]
-    dims = (((0,), (0,)), ((), ()))
-
-    def potentials_step(index, buffer):
-        pos = lax.dynamic_slice_in_dim(coords, index * size, size, 1)
-        cosb, sinb = phase_tables(kf, pos)
-        term = lax.dot_general(
-            filtered[:, :chans], cosb, dims, preferred_element_type=jnp.float32
-        ) + lax.dot_general(filtered[:, chans:], sinb, dims, preferred_element_type=jnp.float32)
-        return lax.dynamic_update_slice_in_dim(buffer, term * (1.0 / math.sqrt(K)), index * size, 1)
-
-    return lax.fori_loop(0, width // size, potentials_step, jnp.zeros((chans, width), jnp.float32))
 
 
 def update(h, msg, potential, live, first_layer, second_layer):
@@ -189,20 +236,17 @@
     h = features
     hm = jnp.dot(msg_weight[0], h, preferred_element_type=jnp.float32).astype(jnp.bfloat16)
     hm_ext = with_halo(hm, (("atoms", 1),), width)
-    masked = jnp.where(live[None, :], h, jnp.zeros_like(h))
     owned = wave_rows // regions
-
-    def term(start, count):
-        return structure(kf, coords, masked)
-
-    share = sent_and_summed(term(jnp.int32(0), owned * lax.axis_size("atoms")), "atoms", 0)
+    table, partial_factor = structure(kvec, coords, h, block_count, regions)
+    arrived = lax.all_to_all(partial_factor, "atoms", 0, 0, tiled=True)
+    share = arrived.astype(jnp.float32).sum(axis=0)
     gain_share = lax.dynamic_slice_in_dim(gain, here * owned, owned, 0)
     filtered_share = spectral(share, gain_share, filter_weight[0], total)
     filtered = gather_directly(filtered_share, "atoms", 0)
-    partial_potential = potentials(filtered, kf, coords)
+    partial_potential = potentials(filtered, table, groups_waves)
     per_group = nblocks // groups_waves
     first = lax.axis_index("waves") * per_group
-    potential = sent_and_summed(partial_potential, "waves", 1)
+    potential = lax.all_to_all(partial_potential, "waves", 0, 0, tiled=True).astype(jnp.float32).sum(axis=0)
     msg = short_range(hm_ext, pos_ext, coords, ext_index, live_slots, first, per_group, regions)
     h_share = lax.dynamic_slice_in_dim(h, first * BLOCK, per_group * BLOCK, 1)
     live_share = lax.dynamic_slice_in_dim(live, first * BLOCK, per_group * BLOCK, 0)

time: 155 us -> 97.2 us (0.63)
  matrix products: 67.8 us -> 6.46 us
  waiting for transfers between devices: 28.9 us -> 17.5 us
  Pallas kernels: 0 us -> 11.2 us
  starting transfers between devices: 31 us -> 35.3 us
    dot_general x16 -> x0, matrix products: 62.8 us -> none  [the longest x4 15.9 us: potentials_step(): lax.dot_general(filtered[:, chans:], sinb, dims, preferred_element_type=j...]
    all_to_all x2, waiting for transfers between devices: 23.1 us -> 11.2 us  [the longest x1 11.2 us: local(): lax.all_to_all(partial_potential, 'waves', 0, 0, tiled=True)]
    pallas_call x0 -> x2, Pallas kernels: none -> 11.2 us  [the longest x1 7.32 us: structure(): pl.pallas_call(functools.partial(structure_kernel, 256), out_shape=(jax.S...]
    all_to_all x2, starting transfers between devices: 18.4 us -> 21.9 us  [the longest x1 13.5 us: local(): arrived = lax.all_to_all(partial_factor, 'atoms', 0, 0, tiled=True)]
    all_to_all x1, starting transfers between devices: 4.85 us -> 7.73 us  [from_everyone(): lax.all_to_all(jnp.broadcast_to(shard[None], (count, *shard.shape)), axis...]
    ppermute x2, starting transfers between devices: 7.69 us -> 5.67 us  [with_halo(): lax.ppermute(head, axis, [((i + 1) % count, i) for i in range(count)])]
  transfers between devices with their start and end apart: 7 -> 7, of which waited for: 3 -> 2; matrix products, arithmetic and copies ran while one was open for 50% -> 16% of each run, Pallas kernels for 0% -> 8%
where the time goes in v1:
time: 97.2 us; the launch traced here: 96.3 us
  starting transfers between devices  35.3 us (36%)
  waiting for transfers between devices  17.5 us (18%)
  blocking collectives  14.2 us (15%)
  Pallas kernels  11.2 us (12%)
  local copies, waits for them, and re-layouts  7.8 us (8%)
  matrix products  6.46 us (7%)
  other arithmetic  2.92 us (3%)
    all_to_all x1, blocking collectives, from_everyone(): lax.all_to_all(jnp.broadcast_to(shard[None], (count, *shard.shape)), axis...  14.2 us
    all_to_all x1, starting transfers between devices, local(): arrived = lax.all_to_all(partial_factor, 'atoms', 0, 0, tiled=True)  13.5 us
    all_to_all x1, waiting for transfers between devices, local(): lax.all_to_all(partial_potential, 'waves', 0, 0, tiled=True)  11.2 us
    all_to_all x1, starting transfers between devices, local(): lax.all_to_all(partial_potential, 'waves', 0, 0, tiled=True)  8.39 us
    all_to_all x1, starting transfers between devices, from_everyone(): lax.all_to_all(jnp.broadcast_to(shard[None], (count, *shard.shape)), axis...  7.73 us
    pallas_call x1, Pallas kernels, structure(): pl.pallas_call(functools.partial(structure_kernel, 256), out_shape=(jax.S...  7.32 us
    all_to_all x1, waiting for transfers between devices, from_everyone(): lax.all_to_all(jnp.broadcast_to(shard[None], (count, *shard.shape)), axis...  6.36 us
    ppermute x2, starting transfers between devices, with_halo(): lax.ppermute(head, axis, [((i + 1) % count, i) for i in range(count)])  5.67 us
  transfers between devices with their start and end apart: 7, of which 2 were waited for; matrix products, arithmetic and copies ran while one was open for 16% of the time, Pallas kernels for 8%

profile of v1, /device:TPU:32, one launch (start us, length us, event | category | flops | bytes accessed | tf_op | source)
XLA Modules:
  0.0 96.3 jit_solution(7810390360798657708)
XLA Ops:
  0.0 0.0 copy-start
  0.0 1.7 %collective-permute-start.1 = (f32[3,2048]{1,0:T(4,128)}, f32[3,2048]{1,0:T(4,128)S(1)}, u32[]{:S(2)}, u32[]{:S(2)}) collective-permute-start(f32[3,2048]{1,0:T(4,128)} %coords_ref.1), channel_id=1, source_target_pairs={{8,0},{16,8},{24,16},{32,24},{40,32},{48,40},{56,48},{64,56},{72,6... | collective-permute-start | bytes 73736 | tf_op jit(solution)/shard_map/ppermute | solution.py:29
  1.7 0.0 collective-permute-start
  1.7 1.2 %convolution_convert_fusion = bf16[64,2048]{1,0:T(8,128)(2,1)S(1)} fusion(bf16[64,2048]{1,0:T(8,128)(2,1)} %h_ref.1, bf16[1,64,64]{2,1,0:T(8,128)(2,1)} %param.18), kind=kOutput, calls=%fused_computation.24 | convolution fusion | flops 16908288 | bytes 532480 | tf_op jit(solution)/shard_map/dot_general | solution.py:237
  2.9 3.9 %collective-permute-start.3 = (bf16[64,2048]{1,0:T(8,128)(2,1)S(1)}, bf16[64,2048]{1,0:T(8,128)(2,1)S(1)}, u32[]{:S(2)}, u32[]{:S(2)}) collective-permute-start(bf16[64,2048]{1,0:T(8,128)(2,1)S(1)} %convolution_convert_fusion), channel_id=1, source_target_pairs={{8,0},{16,8},{24,16},{32,24},{40,32},{48,40},{56,48},{64,56},{72,6... | collective-permute-start | bytes 786440 | tf_op jit(solution)/shard_map/ppermute | solution.py:29
  6.9 0.0 collective-permute-start.2
  7.5 7.3 %structure.1 = (bf16[512,4096]{1,0:T(8,128)(2,1)}, bf16[32,16,128]{2,1,0:T(8,128)(2,1)}) custom-call(s32[3,512]{1,0:T(4,128)} %kf_ref.1, f32[3,2048]{1,0:T(4,128)} %coords_ref.1, bf16[64,2048]{1,0:T(8,128)(2,1)} %h_ref.1, s32[1]{0:T(128)} %copy.44.count_ref), custom_call_target="tpu_custom_call" | custom-call | tf_op jit(solution)/shard_map/structure/pallas_call | solution.py:148
  14.8 13.5 %all-to-all-start = ((bf16[32,16,128]{2,1,0:T(8,128)(2,1)}), bf16[32,16,128]{2,1,0:T(8,128)(2,1)S(1)}, u32[]{:S(2)}, u32[]{:S(2)}) async-start(bf16[32,16,128]{2,1,0:T(8,128)(2,1)} %get-tuple-element.23), calls=%async_computation | async-start | bytes 262144 | tf_op jit(solution)/shard_map/all_to_all | solution.py:241
  28.3 0.7 convert_element_type.49
  29.1 1.3 %gather_fusion.4 = s32[2,27]{1,0:T(2,128)S(1)} fusion(s32[27,16]{0,1:T(8,128)} %param.15, s32[1024]{0:T(1024)S(1)} %pad_clamp_fusion.1), kind=kCustom, calls=%fused_computation.1.clone | custom fusion | bytes 440 | tf_op jit(solution)/shard_map/while/body/eval_jaxpr/jit(_take)/gather | solution.py:73
  30.4 0.7 fusion.52
  31.1 0.6 gather_fusion.3
  31.6 0.1 bitcast_convert_fusion
  31.7 0.1 compare_select_fusion
  31.8 0.1 copy.27
  31.9 0.1 reshape.129
  32.0 1.3 %gather_fusion = f32[2,3,128]{2,1,0:T(4,128)S(1)} fusion(f32[3,16,128]{2,0,1:T(4,128)} %bitcast.87, s32[1024]{0:T(1024)S(1)} %pad_clamp_fusion.2), kind=kCustom, calls=%fused_computation.2 | custom fusion | bytes 6152 | tf_op jit(solution)/shard_map/while/body/eval_jaxpr/jit(_take)/gather | solution.py:74
  33.3 0.1 select_bitcast_fusion
  33.4 0.8 constant_dynamic-slice_fusion.3
  34.2 0.1 broadcast_bitcast_fusion
  34.3 0.1 divide_bitcast_fusion
  34.4 0.1 dynamic_slice.9
  34.4 0.0 collective-permute-done.1
  34.4 0.0 collective-permute-done
  34.4 0.8 maximum_bitcast_fusion.1
  35.2 0.6 gather_fusion.1
  35.9 0.0 all-to-all-done
  35.9 1.0 fusion.44
  36.9 0.9 fusion.46
  37.8 0.1 fusion.55
  37.9 0.7 broadcast_in_dim.72
  38.6 7.7 %all-to-all-start.1 = ((bf16[32,16,128]{2,1,0:T(8,128)(2,1)}), bf16[32,16,128]{2,1,0:T(8,128)(2,1)S(1)}, u32[]{:S(2)}, u32[]{:S(2)}) async-start(bf16[32,16,128]{2,1,0:T(8,128)(2,1)} %broadcast_in_dim.72), calls=%async_computation.1 | async-start | bytes 262144 | tf_op jit(solution)/shard_map/all_to_all | solution.py:44
  46.3 0.1 fusion.70
  46.4 0.0 collective-permute-done.3
  46.4 0.0 collective-permute-done.2
  46.4 0.2 copy_bitcast_fusion
  46.7 0.7 gather_fusion.2
  47.4 6.4 %all-to-all-done.1 = bf16[32,16,128]{2,1,0:T(8,128)(2,1)S(1)} async-done(((bf16[32,16,128]{2,1,0:T(8,128)(2,1)}), bf16[32,16,128]{2,1,0:T(8,128)(2,1)S(1)}, u32[]{:S(2)}, u32[]{:S(2)}) %all-to-all-start.1) | async-done | bytes 131104 | tf_op jit(solution)/shard_map/all_to_all | solution.py:44
  53.7 0.6 copy-done.1
  54.4 3.9 %potentials.1 = bf16[8,64,256]{2,1,0:T(8,128)(2,1)} custom-call(bf16[512,128]{1,0:T(8,128)(2,1)} %bitcast.85, bf16[512,4096]{1,0:T(8,128)(2,1)} %get-tuple-element.24.table_ref), custom_call_target="tpu_custom_call" | custom-call | tf_op jit(solution)/shard_map/potentials/pallas_call | solution.py:181
  58.3 8.4 %all-to-all-start.2 = ((bf16[8,64,256]{2,1,0:T(8,128)(2,1)}), bf16[8,64,256]{2,1,0:T(8,128)(2,1)S(1)}, u32[]{:S(2)}, u32[]{:S(2)}) async-start(bf16[8,64,256]{2,1,0:T(8,128)(2,1)} %potentials.1), calls=%async_computation.2 | async-start | bytes 524288 | tf_op jit(solution)/shard_map/all_to_all | solution.py:249
  66.7 3.0 %fusion.27 = bf16[2,8,8,128]{3,2,1,0:T(8,128)(2,1)S(1)} fusion(f32[27,2]{0,1:T(2,128)S(1)} %bitcast_convert_fusion, f32[27,2,128]{2,0,1:T(8,128)S(1)} %copy.30, f32[2,128]{1,0:T(2,128)S(1)} %bitcast.93, f32[27,2,128]{2,0,1:T(8,128)S(1)} %copy.29, f32[2,128]{1,0:T(2,128)S(1)} %bitcast.94, f32[27,2,128]{2,0,1:T(8,128)S(1)} %copy.28, ...), kind=kOutput, calls=%fused_computation.34 | convolution fusion | flops 131858432 | bytes 1003736 | tf_op jit(solution)/shard_map/while/body/eval_jaxpr/csbj,sbij->cbi/dot_general | solution.py:76
  69.8 11.2 %all-to-all-done.2 = bf16[8,64,256]{2,1,0:T(8,128)(2,1)S(1)} async-done(((bf16[8,64,256]{2,1,0:T(8,128)(2,1)}), bf16[8,64,256]{2,1,0:T(8,128)(2,1)S(1)}, u32[]{:S(2)}, u32[]{:S(2)}) %all-to-all-start.2) | async-done | bytes 262176 | tf_op jit(solution)/shard_map/all_to_all | solution.py:249
  81.0 0.0 copy-done
  81.0 0.0 copy-done.2
  81.0 0.4 fusion.26
  81.4 14.2 %all_to_all.20 = bf16[8,64,256]{2,1,0:T(8,128)(2,1)S(1)} all-to-all(bf16[8,64,256]{2,1,0:T(8,128)(2,1)S(1)} %broadcast_in_dim.74), channel_id=1, replica_groups=mesh['atoms'=32,'waves'=8] {'waves'}, dimensions={0} | all-to-all | bytes 524288 | tf_op jit(solution)/shard_map/all_to_all | solution.py:44
  95.6 0.7 copy.38
  (19 shorter events, 0.2 us)
Async XLA Ops:
  0.0 81.0 %copy-start = (bf16[1,128,192]{1,2,0:T(8,128)(2,1)S(1)}, bf16[1,128,192]{1,2,0:T(8,128)(2,1)}, u32[]{:S(2)}) copy-start(bf16[1,128,192]{1,2,0:T(8,128)(2,1)} %param.20) | copy-start | bytes 147460
  0.0 34.4 %collective-permute-start.1 = (f32[3,2048]{1,0:T(4,128)}, f32[3,2048]{1,0:T(4,128)S(1)}, u32[]{:S(2)}, u32[]{:S(2)}) collective-permute-start(f32[3,2048]{1,0:T(4,128)} %coords_ref.1), channel_id=1, source_target_pairs={{8,0},{16,8},{24,16},{32,24},{40,32},{48,40},{56,48},{64,56},{72,6... | collective-permute-start | bytes 73736 | tf_op jit(solution)/shard_map/ppermute | solution.py:29
  1.7 32.7 %collective-permute-start = (f32[3,2048]{1,0:T(4,128)}, f32[3,2048]{1,0:T(4,128)S(1)}, u32[]{:S(2)}, u32[]{:S(2)}) collective-permute-start(f32[3,2048]{1,0:T(4,128)} %coords_ref.1), channel_id=1, source_target_pairs={{0,8},{8,16},{16,24},{24,32},{32,40},{40,48},{48,56},{56,64},{64,7... | collective-permute-start | bytes 73736 | tf_op jit(solution)/shard_map/ppermute | solution.py:27
  2.9 43.5 %collective-permute-start.3 = (bf16[64,2048]{1,0:T(8,128)(2,1)S(1)}, bf16[64,2048]{1,0:T(8,128)(2,1)S(1)}, u32[]{:S(2)}, u32[]{:S(2)}) collective-permute-start(bf16[64,2048]{1,0:T(8,128)(2,1)S(1)} %convolution_convert_fusion), channel_id=1, source_target_pairs={{8,0},{16,8},{24,16},{32,24},{40,32},{48,40},{56,48},{64,56},{72,6... | collective-permute-start | bytes 786440 | tf_op jit(solution)/shard_map/ppermute | solution.py:29
  6.9 39.6 %collective-permute-start.2 = (bf16[64,2048]{1,0:T(8,128)(2,1)S(1)}, bf16[64,2048]{1,0:T(8,128)(2,1)S(1)}, u32[]{:S(2)}, u32[]{:S(2)}) collective-permute-start(bf16[64,2048]{1,0:T(8,128)(2,1)S(1)} %convolution_convert_fusion), channel_id=1, source_target_pairs={{0,8},{8,16},{16,24},{24,32},{32,40},{40,48},{48,56},{56,64},{64,7... | collective-permute-start | bytes 786440 | tf_op jit(solution)/shard_map/ppermute | solution.py:27
  14.8 21.0 %all-to-all-start = ((bf16[32,16,128]{2,1,0:T(8,128)(2,1)}), bf16[32,16,128]{2,1,0:T(8,128)(2,1)S(1)}, u32[]{:S(2)}, u32[]{:S(2)}) async-start(bf16[32,16,128]{2,1,0:T(8,128)(2,1)} %get-tuple-element.23), calls=%async_computation | async-start | bytes 262144 | tf_op jit(solution)/shard_map/all_to_all | solution.py:241
  38.6 15.2 %all-to-all-start.1 = ((bf16[32,16,128]{2,1,0:T(8,128)(2,1)}), bf16[32,16,128]{2,1,0:T(8,128)(2,1)S(1)}, u32[]{:S(2)}, u32[]{:S(2)}) async-start(bf16[32,16,128]{2,1,0:T(8,128)(2,1)} %broadcast_in_dim.72), calls=%async_computation.1 | async-start | bytes 262144 | tf_op jit(solution)/shard_map/all_to_all | solution.py:44
  53.7 0.7 copy-start.1
  58.3 22.6 %all-to-all-start.2 = ((bf16[8,64,256]{2,1,0:T(8,128)(2,1)}), bf16[8,64,256]{2,1,0:T(8,128)(2,1)S(1)}, u32[]{:S(2)}, u32[]{:S(2)}) async-start(bf16[8,64,256]{2,1,0:T(8,128)(2,1)} %potentials.1), calls=%async_computation.2 | async-start | bytes 524288 | tf_op jit(solution)/shard_map/all_to_all | solution.py:249
  66.7 14.3 %copy-start.2 = (bf16[1,64,128]{2,1,0:T(8,128)(2,1)S(1)}, bf16[1,64,128]{2,1,0:T(8,128)(2,1)}, u32[]{:S(2)}) copy-start(bf16[1,64,128]{2,1,0:T(8,128)(2,1)} %param.21) | copy-start | bytes 49156

commit v2 on v1

--- a/solution.py
+++ b/solution.py
@@ -8,11 +8,11 @@
 from jax.experimental.pallas import tpu as pltpu
 from jax.sharding import PartitionSpec as P
 
+
 K = 4096
 BLOCK = 128
 
 
-TWO_PI = 6.283185307179586
 MSG_SCALE = 0.125
 GAIN_TOP = 20.0
 
@@ -39,17 +39,6 @@
     return jnp.moveaxis(pieces, 0, dim).reshape(lengths)
 
 
-def from_everyone(shard, axis):
-    count = lax.axis_size(axis)
-    return lax.all_to_all(
-        jnp.broadcast_to(shard[None], (count, *shard.shape)), axis, 0, 0, tiled=True
-    )
-
-
-def gather_directly(shard, axis, dim):
-    return laid_out(from_everyone(shard, axis), dim)
-
-
 def pair_weights(own, near, scale_x, live):
     total = None
     for axis in range(3):
@@ -83,6 +72,10 @@
 SIN_COEFS = (3.1415926401307073, -5.167710083507923, 2.5500775232148563, -0.5982912856211671, 0.07765766030589402)
 COS_COEFS = (0.9999999532476085, -4.934792830619664, 4.058411352862771, -1.3318765680813944, 0.21968961109803095)
 ROOT2 = math.sqrt(2.0)
+LIMIT = 16 * 2**20
+WIDE_LIMIT = 62 * 10**6
+TILE = 256
+ANY_SPEC = pl.BlockSpec(memory_space=pl.ANY)
 VMEM_SPEC = pl.BlockSpec(memory_space=pltpu.VMEM)
 
 
@@ -109,7 +102,21 @@
     return first.astype(jnp.float32), second.astype(jnp.float32), third.astype(jnp.float32)
 
 
-def structure_kernel(tile, kf_ref, coords_ref, h_ref, count_ref, table_ref, out_ref, ka_ref, xs_ref):
+def structure_kernel(
+    tile,
+    kf_ref,
+    coords_ref,
+    h_ref,
+    weight_ref,
+    count_ref,
+    stored_ref,
+    out_ref,
+    carry_ref,
+    ka_ref,
+    xs_ref,
+    table_ref,
+    sems,
+):
     waves = kf_ref.shape[1]
     atoms = coords_ref.shape[1]
     chans = h_ref.shape[0]
@@ -123,6 +130,7 @@
     live_atoms = count_ref[0] * BLOCK
     rows = 64
     acc = jnp.zeros((waves, 2 * chans), jnp.float32)
+    copies = []
     nt = (((1,), (1,)), ((), ()))
     for start in range(0, atoms, tile):
         xt = xs_ref[:, start : start + tile]
@@ -131,6 +139,13 @@
             cosv, sinv = phases_of(turns)
             table_ref[k : k + rows, start : start + tile] = cosv.astype(jnp.bfloat16)
             table_ref[k : k + rows, atoms + start : atoms + start + tile] = sinv.astype(jnp.bfloat16)
+        for half in range(2):
+            span = pl.ds(half * atoms + start, tile)
+            copy = pltpu.make_async_copy(
+                table_ref.at[:, span], stored_ref.at[:, span], sems.at[half, start // tile]
+            )
+            copy.start()
+            copies.append(copy)
         lane = lax.broadcasted_iota(jnp.int32, (chans, tile), 1) + start
         ht = jnp.where(lane < live_atoms, h_ref[:, start : start + tile].astype(jnp.float32), 0.0)
         zero = jnp.zeros_like(ht)
@@ -141,32 +156,54 @@
             table_ref[:, atoms + start : atoms + start + tile], hs, nt, preferred_element_type=jnp.float32
         )
     out_ref[...] = acc.astype(jnp.bfloat16).reshape(out_ref.shape)
-
-
-def structure(kvec, coords, h, count, pieces):
+    carry_ref[:chans, :] = jnp.dot(weight_ref[...], h_ref[...], preferred_element_type=jnp.float32).astype(
+        jnp.bfloat16
+    )
+    carry_ref[chans:, :] = xs_ref[...]
+    for copy in copies:
+        copy.wait()
+
+
+def structure(kvec, coords, h, weight, count, pieces):
     waves, atoms, chans = kvec.shape[1], coords.shape[1], h.shape[0]
     return pl.pallas_call(
-        functools.partial(structure_kernel, 256),
+        functools.partial(structure_kernel, TILE),
         out_shape=(
             jax.ShapeDtypeStruct((waves, 2 * atoms), jnp.bfloat16),
             jax.ShapeDtypeStruct((pieces, waves // pieces, 2 * chans), jnp.bfloat16),
+            jax.ShapeDtypeStruct((chans + 16, atoms), jnp.bfloat16),
         ),
-        in_specs=[VMEM_SPEC, VMEM_SPEC, VMEM_SPEC, pl.BlockSpec(memory_space=pltpu.SMEM)],
-        out_specs=(VMEM_SPEC, VMEM_SPEC),
-        scratch_shapes=[pltpu.VMEM((waves, 16), jnp.bfloat16), pltpu.VMEM((16, atoms), jnp.bfloat16)],
+        in_specs=[VMEM_SPEC] * 4 + [pl.BlockSpec(memory_space=pltpu.SMEM)],
+        out_specs=(ANY_SPEC, VMEM_SPEC, VMEM_SPEC),
+        scratch_shapes=[
+            pltpu.VMEM((waves, 16), jnp.bfloat16),
+            pltpu.VMEM((16, atoms), jnp.bfloat16),
+            pltpu.VMEM((waves, 2 * atoms), jnp.bfloat16),
+            pltpu.SemaphoreType.DMA((2, atoms // TILE)),
+        ],
+        compiler_params=pltpu.CompilerParams(vmem_limit_bytes=WIDE_LIMIT),
         name="structure",
-    )(kvec, coords, h, count)
-
-
-def potentials_kernel(filtered_ref, table_ref, out_ref):
+    )(kvec, coords, h, weight, count)
+
+
+def potentials_kernel(filtered_ref, stored_ref, out_ref, table_ref, sems):
     chans = out_ref.shape[1]
     pieces, _, width = out_ref.shape
     atoms = pieces * width
     tn = (((0,), (0,)), ((), ()))
+    copies = []
+    for piece in range(pieces):
+        for half in range(2):
+            span = pl.ds(half * atoms + piece * width, width)
+            copy = pltpu.make_async_copy(stored_ref.at[:, span], table_ref.at[:, span], sems.at[half, piece])
+            copy.start()
+            copies.append(copy)
     fc = filtered_ref[:, :chans]
     fs = filtered_ref[:, chans:]
     for piece in range(pieces):
         start = piece * width
+        copies[2 * piece].wait()
+        copies[2 * piece + 1].wait()
         term = lax.dot_general(
             fc, table_ref[:, start : start + width], tn, preferred_element_type=jnp.float32
         ) + lax.dot_general(
@@ -181,27 +218,63 @@
     return pl.pallas_call(
         potentials_kernel,
         out_shape=jax.ShapeDtypeStruct((pieces, chans, atoms // pieces), jnp.bfloat16),
-        in_specs=[VMEM_SPEC, VMEM_SPEC],
+        in_specs=[VMEM_SPEC, ANY_SPEC],
         out_specs=VMEM_SPEC,
+        scratch_shapes=[pltpu.VMEM(table.shape, jnp.bfloat16), pltpu.SemaphoreType.DMA((2, pieces))],
+        compiler_params=pltpu.CompilerParams(vmem_limit_bytes=WIDE_LIMIT),
         name="potentials",
     )(filtered, table)
 
 
-def spectral(factor, gain, mixing, total):
-    chans = mixing.shape[0]
-    scaled = factor * (1.0 / math.sqrt(total))
-    cos_part = jnp.dot(scaled[:, :chans], mixing, precision=lax.Precision.HIGHEST)
-    sin_part = jnp.dot(scaled[:, chans:], mixing, precision=lax.Precision.HIGHEST)
-    return (jnp.concatenate([cos_part, sin_part], axis=1) * gain[:, None]).astype(jnp.bfloat16)
-
-
-def update(h, msg, potential, live, first_layer, second_layer):
-    stacked = jnp.concatenate([h, msg, potential.astype(jnp.bfloat16)], axis=0)
-    hidden = jax.nn.silu(jnp.dot(first_layer, stacked, preferred_element_type=jnp.float32)).astype(
-        jnp.bfloat16
-    )
-    out = h.astype(jnp.float32) + jnp.dot(second_layer, hidden, preferred_element_type=jnp.float32)
-    return jnp.where(live[None, :], out, jnp.zeros_like(out)).astype(jnp.bfloat16)
+def spectral_kernel(scale, arrived_ref, gain_ref, mixing_ref, out_ref):
+    chans = mixing_ref.shape[0]
+    factor = arrived_ref[0].astype(jnp.float32)
+    for piece in range(1, arrived_ref.shape[0]):
+        factor = factor + arrived_ref[piece].astype(jnp.float32)
+    factor = factor * scale
+    high = lax.Precision.HIGHEST
+    mixing = mixing_ref[...]
+    cos_part = jnp.dot(factor[:, :chans], mixing, precision=high, preferred_element_type=jnp.float32)
+    sin_part = jnp.dot(factor[:, chans:], mixing, precision=high, preferred_element_type=jnp.float32)
+    filtered = (jnp.concatenate([cos_part, sin_part], axis=1) * gain_ref[...]).astype(jnp.bfloat16)
+    for piece in range(out_ref.shape[0]):
+        out_ref[piece] = filtered
+
+
+def spectral(arrived, gain, mixing, total):
+    return pl.pallas_call(
+        functools.partial(spectral_kernel, 1.0 / math.sqrt(total)),
+        out_shape=jax.ShapeDtypeStruct(arrived.shape, jnp.bfloat16),
+        in_specs=[VMEM_SPEC] * 3,
+        out_specs=VMEM_SPEC,
+        compiler_params=pltpu.CompilerParams(vmem_limit_bytes=LIMIT),
+        name="spectral",
+    )(arrived, gain, mixing)
+
+
+def update_kernel(arrived_ref, h_ref, msg_ref, live_ref, first_ref, second_ref, out_ref):
+    potential = arrived_ref[0].astype(jnp.float32)
+    for piece in range(1, arrived_ref.shape[0]):
+        potential = potential + arrived_ref[piece].astype(jnp.float32)
+    h = h_ref[...]
+    stacked = jnp.concatenate([h, msg_ref[...], potential.astype(jnp.bfloat16)], axis=0)
+    inner = jnp.dot(first_ref[...], stacked, preferred_element_type=jnp.float32)
+    hidden = jax.nn.silu(inner).astype(jnp.bfloat16)
+    out = h.astype(jnp.float32) + jnp.dot(second_ref[...], hidden, preferred_element_type=jnp.float32)
+    new = jnp.where(live_ref[...] > 0.0, out, 0.0).astype(jnp.bfloat16)
+    for piece in range(out_ref.shape[0]):
+        out_ref[piece] = new
+
+
+def update(arrived, h, msg, live, first_layer, second_layer):
+    return pl.pallas_call(
+        update_kernel,
+        out_shape=jax.ShapeDtypeStruct(arrived.shape, jnp.bfloat16),
+        in_specs=[VMEM_SPEC] * 6,
+        out_specs=VMEM_SPEC,
+        compiler_params=pltpu.CompilerParams(vmem_limit_bytes=LIMIT),
+        name="update",
+    )(arrived, h, msg, live, first_layer, second_layer)
 
 
 def local(
@@ -226,33 +299,33 @@
     offset = (source - here) % regions
     which = jnp.where(offset == 0, 1, jnp.where(offset == 1, 2, 0))
     ext_index = which * nblocks + neighbours % nblocks
-    live_block = jnp.arange(nblocks, dtype=jnp.int32) < block_count[0]
-    live = jnp.repeat(live_block, BLOCK)
     kf = kvec.astype(jnp.float32)
     kx = kf[0] / regions
     gain = GAIN_TOP / (4.0 + kx * kx + kf[1] * kf[1] + kf[2] * kf[2])
-    wave_rows = kf.shape[1]
-    pos_ext = with_halo(coords, (("atoms", 1),), width)
     h = features
-    hm = jnp.dot(msg_weight[0], h, preferred_element_type=jnp.float32).astype(jnp.bfloat16)
-    hm_ext = with_halo(hm, (("atoms", 1),), width)
-    owned = wave_rows // regions
-    table, partial_factor = structure(kvec, coords, h, block_count, regions)
+    chans = h.shape[0]
+    owned = kf.shape[1] // regions
+    table, partial_factor, carry = structure(kvec, coords, h, msg_weight[0], block_count, regions)
     arrived = lax.all_to_all(partial_factor, "atoms", 0, 0, tiled=True)
-    share = arrived.astype(jnp.float32).sum(axis=0)
+    carry_ext = with_halo(carry, (("atoms", 1),), width)
+    hm_ext = carry_ext[:chans]
+    pieces = carry_ext[chans : chans + 9].astype(jnp.float32)
+    pos_ext = (pieces[6:9] + pieces[3:6]) + pieces[:3]
     gain_share = lax.dynamic_slice_in_dim(gain, here * owned, owned, 0)
-    filtered_share = spectral(share, gain_share, filter_weight[0], total)
-    filtered = gather_directly(filtered_share, "atoms", 0)
+    gain_rows = jnp.broadcast_to(gain_share[:, None], (owned, 2 * chans))
+    everyone = spectral(arrived, gain_rows, filter_weight[0], total)
+    filtered = lax.all_to_all(everyone, "atoms", 0, 0, tiled=True).reshape(kf.shape[1], 2 * chans)
     partial_potential = potentials(filtered, table, groups_waves)
     per_group = nblocks // groups_waves
     first = lax.axis_index("waves") * per_group
-    potential = lax.all_to_all(partial_potential, "waves", 0, 0, tiled=True).astype(jnp.float32).sum(axis=0)
+    share = per_group * BLOCK
+    potential = lax.all_to_all(partial_potential, "waves", 0, 0, tiled=True)
     msg = short_range(hm_ext, pos_ext, coords, ext_index, live_slots, first, per_group, regions)
-    h_share = lax.dynamic_slice_in_dim(h, first * BLOCK, per_group * BLOCK, 1)
-    live_share = lax.dynamic_slice_in_dim(live, first * BLOCK, per_group * BLOCK, 0)
-    new_share = update(h_share, msg, potential, live_share, mlp_in[0], mlp_out[0])
-    h = gather_directly(new_share, "waves", 1)
-    return h
+    h_share = lax.dynamic_slice_in_dim(h, first * BLOCK, share, 1)
+    atom = jnp.arange(share, dtype=jnp.int32) + first * BLOCK
+    live_share = (atom < block_count[0] * BLOCK).astype(jnp.float32)[None, :]
+    new = update(potential, h_share, msg, live_share, mlp_in[0], mlp_out[0])
+    return laid_out(lax.all_to_all(new, "waves", 0, 0, tiled=True), 1)
 
 
 def solution(mesh):

time: 97.2 us -> 87.5 us (0.900)
  starting transfers between devices: 35.3 us -> 27 us
  matrix products: 6.46 us -> 3.02 us
  Pallas kernels: 11.2 us -> 13.5 us
  local copies, waits for them, and re-layouts: 7.8 us -> 9.24 us
  other arithmetic: 2.92 us -> 1.83 us
    all_to_all x1, starting transfers between devices: 13.5 us -> 7.17 us  [local(): arrived = lax.all_to_all(partial_factor, 'atoms', 0, 0, tiled=True)]
    dot_general x4 -> x0, matrix products: 3.42 us -> none  [the longest x1 1.17 us: local(): jnp.dot(msg_weight[0], h, preferred_element_type=jnp.float32)]
    unnamed x6 -> x11, local copies, waits for them, and re-layouts: 0.66 us -> 3.34 us
    ppermute x2 -> x1, starting transfers between devices: 5.67 us -> 3.84 us  [with_halo(): lax.ppermute(head, axis, [((i + 1) % count, i) for i in range(count)])]
    all_to_all x2, waiting for transfers between devices: 17.5 us -> 15.7 us  [the longest x1 11.2 us: local(): potential = lax.all_to_all(partial_potential, 'waves', 0, 0, tiled=True)]
    all_to_all x1, waiting for transfers between devices: 0.01 us -> 1.34 us  [local(): arrived = lax.all_to_all(partial_factor, 'atoms', 0, 0, tiled=True)]
    pallas_call x1, Pallas kernels: 3.91 us -> 5.1 us  [potentials(): pl.pallas_call(potentials_kernel, out_shape=jax.ShapeDtypeStruct((pieces,...]
    pallas_call x1 -> x3, Pallas kernels: 7.32 us -> 8.37 us  [the longest x1 7.04 us: structure(): pl.pallas_call(functools.partial(structure_kernel, TILE), out_shape=(jax....]
  transfers between devices with their start and end apart: 7 -> 5, of which waited for: 2 -> 3; matrix products, arithmetic and copies ran while one was open for 16% -> 14% of each run, Pallas kernels for 8% -> 1%
where the time goes in v2:
time: 87.5 us; the launch traced here: 86.7 us
  starting transfers between devices  27 us (31%)
  waiting for transfers between devices  17.1 us (20%)
  blocking collectives  14.2 us (16%)
  Pallas kernels  13.5 us (15%)
  local copies, waits for them, and re-layouts  9.24 us (11%)
  matrix products  3.02 us (3%)
  other arithmetic  1.83 us (2%)
  between operations  0.91 us (1%)
    all_to_all x1, blocking collectives, local(): return laid_out(lax.all_to_all(new, 'waves', 0, 0, tiled=True), 1)  14.2 us
    all_to_all x1, waiting for transfers between devices, local(): potential = lax.all_to_all(partial_potential, 'waves', 0, 0, tiled=True)  11.2 us
    all_to_all x1, starting transfers between devices, local(): potential = lax.all_to_all(partial_potential, 'waves', 0, 0, tiled=True)  9.4 us
    all_to_all x1, starting transfers between devices, local(): arrived = lax.all_to_all(partial_factor, 'atoms', 0, 0, tiled=True)  7.17 us
    pallas_call x1, Pallas kernels, structure(): pl.pallas_call(functools.partial(structure_kernel, TILE), out_shape=(jax....  7.04 us
    all_to_all x1, starting transfers between devices, local(): lax.all_to_all(everyone, 'atoms', 0, 0, tiled=True)  6.46 us
    pallas_call x1, Pallas kernels, potentials(): pl.pallas_call(potentials_kernel, out_shape=jax.ShapeDtypeStruct((pieces,...  5.1 us
    all_to_all x1, waiting for transfers between devices, local(): lax.all_to_all(everyone, 'atoms', 0, 0, tiled=True)  4.56 us
  transfers between devices with their start and end apart: 5, of which 3 were waited for; matrix products, arithmetic and copies ran while one was open for 14% of the time, Pallas kernels for 1%

profile of v2, /device:TPU:32, one launch (start us, length us, event | category | flops | bytes accessed | tf_op | source)
XLA Modules:
  0.0 86.7 jit_solution(17479384860571087039)
XLA Ops:
  0.0 0.0 copy-start
  0.7 7.0 %structure.1 = (bf16[512,4096]{1,0:T(8,128)(2,1)}, bf16[32,16,128]{2,1,0:T(8,128)(2,1)}, bf16[80,2048]{1,0:T(8,128)(2,1)}) custom-call(s32[3,512]{1,0:T(4,128)} %kf_ref.1, f32[3,2048]{1,0:T(4,128)} %coords_ref.1, bf16[64,2048]{1,0:T(8,128)(2,1)} %h_ref.1, bf16[64,64]{1,0:T(8,128)(2,1)} %bitcast.66, s32[1]{0:T(128)S(6)} %copy.36.count_ref), custom_call_target="tpu_custom_call" | custom-call | tf_op jit(solution)/shard_map/structure/pallas_call | solution.py:169
  7.7 0.1 collective-permute-start
  7.8 3.8 %collective-permute-start.1 = (bf16[80,2048]{1,0:T(8,128)(2,1)}, bf16[80,2048]{1,0:T(8,128)(2,1)S(1)}, u32[]{:S(2)}, u32[]{:S(2)}) collective-permute-start(bf16[80,2048]{1,0:T(8,128)(2,1)} %get-tuple-element.26), channel_id=1, source_target_pairs={{8,0},{16,8},{24,16},{32,24},{40,32},{48,40},{56,48},{64,56},{72,6... | collective-permute-start | bytes 983048 | tf_op jit(solution)/shard_map/ppermute | solution.py:29
  11.6 7.2 %all-to-all-start = ((bf16[32,16,128]{2,1,0:T(8,128)(2,1)}), bf16[32,16,128]{2,1,0:T(8,128)(2,1)S(1)}, u32[]{:S(2)}, u32[]{:S(2)}) async-start(bf16[32,16,128]{2,1,0:T(8,128)(2,1)} %get-tuple-element.24), calls=%async_computation | async-start | bytes 262144 | tf_op jit(solution)/shard_map/all_to_all | solution.py:309
  18.8 0.7 convert_element_type.31
  19.6 0.8 constant_dynamic-slice_fusion.3.h_ref
  20.4 0.7 fusion.31
  21.1 0.0 copy-done
  21.1 0.6 gather_fusion.4
  21.6 0.6 gather_fusion.3
  22.2 0.1 bitcast_convert_fusion
  22.3 0.1 compare_select_fusion
  22.3 0.1 copy.15
  22.4 0.1 reshape.112
  22.6 1.3 %gather_fusion = f32[2,3,128]{2,1,0:T(4,128)S(1)} fusion(f32[3,16,128]{2,0,1:T(4,128)} %bitcast.65, s32[1024]{0:T(1024)S(1)} %get-tuple-element.48), kind=kCustom, calls=%fused_computation.2 | custom fusion | bytes 6152 | tf_op jit(solution)/shard_map/while/body/eval_jaxpr/jit(_take)/gather | solution.py:63
  23.9 0.1 select_bitcast_fusion
  24.0 0.1 divide_bitcast_fusion
  24.1 0.9 %copy.23 = bf16[1,128,192]{2,1,0:T(8,128)(2,1)S(1)} copy(bf16[1,128,192]{1,2,0:T(8,128)(2,1)} %param.20) | data formatting | bytes 98304 | tf_op args[8]
  25.0 1.3 %all-to-all-done.arrived_ref = bf16[32,16,128]{2,1,0:T(8,128)(2,1)S(1)} async-done(((bf16[32,16,128]{2,1,0:T(8,128)(2,1)}), bf16[32,16,128]{2,1,0:T(8,128)(2,1)S(1)}, u32[]{:S(2)}, u32[]{:S(2)}) %all-to-all-start) | async-done | bytes 131104 | tf_op jit(solution)/shard_map/all_to_all | solution.py:309
  26.3 0.1 broadcast_in_dim.45.gain_ref
  26.4 0.0 copy-start.1
  26.4 0.8 copy-done.1
  27.2 1.0 %spectral.1 = bf16[32,16,128]{2,1,0:T(8,128)(2,1)} custom-call(bf16[32,16,128]{2,1,0:T(8,128)(2,1)S(1)} %all-to-all-done.arrived_ref, f32[16,128]{1,0:T(8,128)S(1)} %broadcast_in_dim.45.gain_ref, f32[64,64]{1,0:T(8,128)S(1)} %bitcast.56), custom_call_target="tpu_custom_call" | custom-call | tf_op jit(solution)/shard_map/spectral/pallas_call | solution.py:245
  28.2 6.5 %all-to-all-start.1 = ((bf16[32,16,128]{2,1,0:T(8,128)(2,1)}), bf16[32,16,128]{2,1,0:T(8,128)(2,1)S(1)}, u32[]{:S(2)}, u32[]{:S(2)}) async-start(bf16[32,16,128]{2,1,0:T(8,128)(2,1)} %spectral.1), calls=%async_computation.1 | async-start | bytes 262144 | tf_op jit(solution)/shard_map/all_to_all | solution.py:317
  34.6 0.0 collective-permute-done
  34.7 1.0 %constant_dynamic-update-slice_fusion.1 = bf16[80,6144]{1,0:T(8,128)(2,1)S(1)} fusion(bf16[80,6144]{1,0:T(8,128)(2,1)S(1)} %constant_dynamic-update-slice_fusion.2, bf16[80,2048]{1,0:T(8,128)(2,1)} %get-tuple-element.26), kind=kLoop, calls=%fused_computation.51 | loop fusion | bytes 655360
  35.7 0.0 collective-permute-done.1
  35.8 0.6 gather_fusion.1
  36.4 0.1 fusion.43
  36.6 0.2 copy_bitcast_fusion
  36.8 0.7 gather_fusion.2
  37.5 4.6 %all-to-all-done.1 = bf16[32,16,128]{2,1,0:T(8,128)(2,1)S(1)} async-done(((bf16[32,16,128]{2,1,0:T(8,128)(2,1)}), bf16[32,16,128]{2,1,0:T(8,128)(2,1)S(1)}, u32[]{:S(2)}, u32[]{:S(2)}) %all-to-all-start.1) | async-done | bytes 131104 | tf_op jit(solution)/shard_map/all_to_all | solution.py:317
  42.1 0.0 copy-start.3
  42.1 0.7 copy-done.3
  42.7 5.1 %potentials.1 = bf16[8,64,256]{2,1,0:T(8,128)(2,1)} custom-call(bf16[512,128]{1,0:T(8,128)(2,1)} %bitcast.60, bf16[512,4096]{1,0:T(8,128)(2,1)} %get-tuple-element.25.stored_ref), custom_call_target="tpu_custom_call" | custom-call | tf_op jit(solution)/shard_map/potentials/pallas_call | solution.py:218
  47.8 9.4 %all-to-all-start.2 = ((bf16[8,64,256]{2,1,0:T(8,128)(2,1)}), bf16[8,64,256]{2,1,0:T(8,128)(2,1)S(1)}, u32[]{:S(2)}, u32[]{:S(2)}) async-start(bf16[8,64,256]{2,1,0:T(8,128)(2,1)} %potentials.1), calls=%async_computation.2 | async-start | bytes 524288 | tf_op jit(solution)/shard_map/all_to_all | solution.py:322
  57.2 0.0 copy-start.2
  57.2 3.0 %fusion.24 = bf16[2,8,8,128]{3,2,1,0:T(8,128)(2,1)S(1)} fusion(f32[27,2]{0,1:T(2,128)S(1)} %bitcast_convert_fusion, f32[27,2,128]{2,0,1:T(8,128)S(1)} %copy.19, f32[2,128]{1,0:T(2,128)S(1)} %bitcast.68, f32[27,2,128]{2,0,1:T(8,128)S(1)} %copy.18, f32[2,128]{1,0:T(2,128)S(1)} %bitcast.69, f32[27,2,128]{2,0,1:T(8,128)S(1)} %copy.17, ...), kind=kOutput, calls=%fused_computation.28 | convolution fusion | flops 131858432 | bytes 1003736 | tf_op jit(solution)/shard_map/while/body/eval_jaxpr/csbj,sbij->cbi/dot_general | solution.py:65
  60.3 11.2 %all-to-all-done.2.arrived_ref = bf16[8,64,256]{2,1,0:T(8,128)(2,1)S(1)} async-done(((bf16[8,64,256]{2,1,0:T(8,128)(2,1)}), bf16[8,64,256]{2,1,0:T(8,128)(2,1)S(1)}, u32[]{:S(2)}, u32[]{:S(2)}) %all-to-all-start.2) | async-done | bytes 262176 | tf_op jit(solution)/shard_map/all_to_all | solution.py:322
  71.5 0.0 copy-done.2
  71.5 0.3 update.1
  71.8 14.2 %all_to_all.20 = bf16[8,64,256]{2,1,0:T(8,128)(2,1)S(1)} all-to-all(bf16[8,64,256]{2,1,0:T(8,128)(2,1)S(1)} %update.1), channel_id=1, replica_groups=mesh['atoms'=32,'waves'=8] {'waves'}, dimensions={0} | all-to-all | bytes 524288 | tf_op jit(solution)/shard_map/all_to_all | solution.py:328
  86.0 0.7 copy.28
  (16 shorter events, 0.2 us)
Async XLA Ops:
  0.0 21.1 %copy-start = (s32[27,16]{0,1:T(8,128)S(1)}, s32[27,16]{0,1:T(8,128)}, u32[]{:S(2)}) copy-start(s32[27,16]{0,1:T(8,128)} %param.15) | copy-start | bytes 5188
  7.7 26.9 %collective-permute-start = (bf16[80,2048]{1,0:T(8,128)(2,1)}, bf16[80,2048]{1,0:T(8,128)(2,1)S(1)}, u32[]{:S(2)}, u32[]{:S(2)}) collective-permute-start(bf16[80,2048]{1,0:T(8,128)(2,1)} %get-tuple-element.26), channel_id=1, source_target_pairs={{0,8},{8,16},{16,24},{24,32},{32,40},{40,48},{48,56},{56,64},{64,7... | collective-permute-start | bytes 983048 | tf_op jit(solution)/shard_map/ppermute | solution.py:27
  7.8 27.9 %collective-permute-start.1 = (bf16[80,2048]{1,0:T(8,128)(2,1)}, bf16[80,2048]{1,0:T(8,128)(2,1)S(1)}, u32[]{:S(2)}, u32[]{:S(2)}) collective-permute-start(bf16[80,2048]{1,0:T(8,128)(2,1)} %get-tuple-element.26), channel_id=1, source_target_pairs={{8,0},{16,8},{24,16},{32,24},{40,32},{48,40},{56,48},{64,56},{72,6... | collective-permute-start | bytes 983048 | tf_op jit(solution)/shard_map/ppermute | solution.py:29
  11.6 14.7 %all-to-all-start = ((bf16[32,16,128]{2,1,0:T(8,128)(2,1)}), bf16[32,16,128]{2,1,0:T(8,128)(2,1)S(1)}, u32[]{:S(2)}, u32[]{:S(2)}) async-start(bf16[32,16,128]{2,1,0:T(8,128)(2,1)} %get-tuple-element.24), calls=%async_computation | async-start | bytes 262144 | tf_op jit(solution)/shard_map/all_to_all | solution.py:309
  26.4 0.8 copy-start.1
  28.2 13.9 %all-to-all-start.1 = ((bf16[32,16,128]{2,1,0:T(8,128)(2,1)}), bf16[32,16,128]{2,1,0:T(8,128)(2,1)S(1)}, u32[]{:S(2)}, u32[]{:S(2)}) async-start(bf16[32,16,128]{2,1,0:T(8,128)(2,1)} %spectral.1), calls=%async_computation.1 | async-start | bytes 262144 | tf_op jit(solution)/shard_map/all_to_all | solution.py:317
  42.1 0.7 copy-start.3
  47.8 23.6 %all-to-all-start.2 = ((bf16[8,64,256]{2,1,0:T(8,128)(2,1)}), bf16[8,64,256]{2,1,0:T(8,128)(2,1)S(1)}, u32[]{:S(2)}, u32[]{:S(2)}) async-start(bf16[8,64,256]{2,1,0:T(8,128)(2,1)} %potentials.1), calls=%async_computation.2 | async-start | bytes 524288 | tf_op jit(solution)/shard_map/all_to_all | solution.py:322
  57.2 14.2 %copy-start.2 = (bf16[1,64,128]{2,1,0:T(8,128)(2,1)S(1)}, bf16[1,64,128]{2,1,0:T(8,128)(2,1)}, u32[]{:S(2)}) copy-start(bf16[1,64,128]{2,1,0:T(8,128)(2,1)} %param.21) | copy-start | bytes 49156

commit v3 on v1

v3 whole, which is shorter than its diff:
```python
import functools
import math

import jax
import jax.numpy as jnp
from jax import lax
from jax.experimental import pallas as pl
from jax.experimental.pallas import tpu as pltpu
from jax.sharding import PartitionSpec as P


K = 4096
BLOCK = 128

MSG_SCALE = 0.125
GAIN_TOP = 20.0
SIN_COEFS = (3.1415926401307073, -5.167710083507923, 2.5500775232148563, -0.5982912856211671, 0.07765766030589402)
COS_COEFS = (0.9999999532476085, -4.934792830619664, 4.058411352862771, -1.3318765680813944, 0.21968961109803095)
ROOT2 = math.sqrt(2.0)
TILE = 256
ROWS = 64
LIMIT = 16 * 2**20
VMEM_SPEC = pl.BlockSpec(memory_space=pltpu.VMEM)
SMEM_SPEC = pl.BlockSpec(memory_space=pltpu.SMEM)
ANY_SPEC = pl.BlockSpec(memory_space=pl.ANY)
HBM_SPEC = pl.BlockSpec(memory_space=pltpu.HBM)
PARAMS = pltpu.CompilerParams(vmem_limit_bytes=LIMIT)
NT = (((1,), (1,)), ((), ()))
TN = (((0,), (0,)), ((), ()))


def kept_rows(waves):
    return waves * 5 // 8


def horner(coefs, scale, u):
    value = coefs[-1] * scale
    for coef in coefs[-2::-1]:
        value = value * u + coef * scale
    return value


def phases_of(turns):
    r = turns - jnp.round(turns)
    u = r * r
    s = r * horner(SIN_COEFS, ROOT2, u)
    c = horner(COS_COEFS, ROOT2, u)
    return 1.0 - s * s, s * c


def three_pieces(values):
    first = values.astype(jnp.bfloat16)
    rest = values - first.astype(jnp.float32)
    second = rest.astype(jnp.bfloat16)
    third = (rest - second.astype(jnp.float32)).astype(jnp.bfloat16)
    return first.astype(jnp.float32), second.astype(jnp.float32), third.astype(jnp.float32)


def structure_kernel(
    kvec_ref, coords_ref, h_ref, weight_ref, count_ref, low_ref, high_out, out_ref, carry_out,
    ka_ref, xs_ref, high_ref, carry_ref, sems, carry_sem,
):
    waves = kvec_ref.shape[1]
    atoms = coords_ref.shape[1]
    chans = h_ref.shape[0]
    kept = low_ref.shape[0]
    kf = kvec_ref[...].astype(jnp.float32)
    ka = jnp.concatenate([kf, kf, kf, jnp.zeros((7, waves), jnp.float32)], axis=0)
    ka_ref[...] = ka.T.astype(jnp.bfloat16)
    first, second, third = three_pieces(coords_ref[...])
    xs = jnp.concatenate([first, second, third, jnp.zeros((7, atoms), jnp.float32)], axis=0)
    xs_ref[...] = xs.astype(jnp.bfloat16)
    carry_ref[:chans, :] = jnp.dot(weight_ref[...], h_ref[...], preferred_element_type=jnp.float32).astype(
        jnp.bfloat16
    )
    carry_ref[chans:, :] = xs.astype(jnp.bfloat16)
    carry_copy = pltpu.make_async_copy(carry_ref, carry_out, carry_sem)
    carry_copy.start()
    copies = [carry_copy]
    live_atoms = count_ref[0] * BLOCK
    low_sum = jnp.zeros((kept, 2 * chans), jnp.float32)
    high_sum = jnp.zeros((waves - kept, 2 * chans), jnp.float32)
    for start in range(0, atoms, TILE):
        cos_span = slice(start, start + TILE)
        sin_span = slice(atoms + start, atoms + start + TILE)
        xt = xs_ref[:, cos_span]
        for row in range(0, waves, ROWS):
            turns = jnp.dot(ka_ref[row : row + ROWS, :], xt, preferred_element_type=jnp.float32)
            cosv, sinv = phases_of(turns)
            place, at = (low_ref, row) if row < kept else (high_ref, row - kept)
            place[at : at + ROWS, cos_span] = cosv.astype(jnp.bfloat16)
            place[at : at + ROWS, sin_span] = sinv.astype(jnp.bfloat16)
        for half in range(2):
            span = pl.ds(half * atoms + start, TILE)
            copy = pltpu.make_async_copy(
                high_ref.at[:, span], high_out.at[:, span], sems.at[half, start // TILE]
            )
            copy.start()
            copies.append(copy)
        lane = lax.broadcasted_iota(jnp.int32, (chans, TILE), 1) + start
        ht = jnp.where(lane < live_atoms, h_ref[:, cos_span].astype(jnp.float32), 0.0)
        zero = jnp.zeros_like(ht)
        hc = jnp.concatenate([ht, zero], axis=0).astype(jnp.bfloat16)
        hs = jnp.concatenate([zero, ht], axis=0).astype(jnp.bfloat16)
        f32 = dict(preferred_element_type=jnp.float32)
        low_sum = low_sum + lax.dot_general(low_ref[:, cos_span], hc, NT, **f32)
        low_sum = low_sum + lax.dot_general(low_ref[:, sin_span], hs, NT, **f32)
        high_sum = high_sum + lax.dot_general(high_ref[:, cos_span], hc, NT, **f32)
        high_sum = high_sum + lax.dot_general(high_ref[:, sin_span], hs, NT, **f32)
    owned = out_ref.shape[1]
    out_ref[: kept // owned] = low_sum.astype(jnp.bfloat16).reshape(kept // owned, owned, 2 * chans)
    out_ref[kept // owned :] = high_sum.astype(jnp.bfloat16).reshape(-1, owned, 2 * chans)
    for copy in copies:
        copy.wait()


def structure(kvec, coords, h, weight, count, pieces):
    waves, atoms, chans = kvec.shape[1], coords.shape[1], h.shape[0]
    kept = kept_rows(waves)
    return pl.pallas_call(
        structure_kernel,
        out_shape=(
            jax.ShapeDtypeStruct((kept, 2 * atoms), jnp.bfloat16),
            pltpu.HBM((waves - kept, 2 * atoms), jnp.bfloat16),
            jax.ShapeDtypeStruct((pieces, waves // pieces, 2 * chans), jnp.bfloat16),
            jax.ShapeDtypeStruct((chans + 16, atoms), jnp.bfloat16),
        ),
        in_specs=[VMEM_SPEC] * 4 + [SMEM_SPEC],
        out_specs=(VMEM_SPEC, HBM_SPEC, VMEM_SPEC, ANY_SPEC),
        scratch_shapes=[
            pltpu.VMEM((waves, 16), jnp.bfloat16),
            pltpu.VMEM((16, atoms), jnp.bfloat16),
            pltpu.VMEM((waves - kept, 2 * atoms), jnp.bfloat16),
            pltpu.VMEM((chans + 16, atoms), jnp.bfloat16),
            pltpu.SemaphoreType.DMA((2, atoms // TILE)),
            pltpu.SemaphoreType.DMA,
        ],
        compiler_params=PARAMS,
        name="structure",
    )(kvec, coords, h, weight, count)


def spectral_kernel(arrived_ref, gain_ref, mixing_ref, out_ref):
    chans = mixing_ref.shape[0]
    factor = arrived_ref[0].astype(jnp.float32)
    for piece in range(1, arrived_ref.shape[0]):
        factor = factor + arrived_ref[piece].astype(jnp.float32)
    high = dict(precision=lax.Precision.HIGHEST, preferred_element_type=jnp.float32)
    mixing = mixing_ref[...]
    cos_part = jnp.dot(factor[:, :chans], mixing, **high)
    sin_part = jnp.dot(factor[:, chans:], mixing, **high)
    filtered = (jnp.concatenate([cos_part, sin_part], axis=1) * gain_ref[...]).astype(jnp.bfloat16)
    for piece in range(out_ref.shape[0]):
        out_ref[piece] = filtered


def spectral(arrived, gain, mixing):
    return pl.pallas_call(
        spectral_kernel,
        out_shape=jax.ShapeDtypeStruct(arrived.shape, jnp.bfloat16),
        in_specs=[VMEM_SPEC] * 3,
        out_specs=VMEM_SPEC,
        compiler_params=PARAMS,
        name="spectral",
    )(arrived, gain, mixing)


def potentials_kernel(filtered_ref, low_ref, high_in, out_ref, high_ref, sems):
    chans = out_ref.shape[1]
    pieces, _, width = out_ref.shape
    atoms = pieces * width
    kept = low_ref.shape[0]
    copies = []
    for piece in range(pieces):
        for half in range(2):
            span = pl.ds(half * atoms + piece * width, width)
            copy = pltpu.make_async_copy(high_in.at[:, span], high_ref.at[:, span], sems.at[half, piece])
            copy.start()
            copies.append(copy)
    parts = [
        (filtered_ref[:kept, :chans], low_ref, 0),
        (filtered_ref[:kept, chans:], low_ref, atoms),
        (filtered_ref[kept:, :chans], high_ref, 0),
        (filtered_ref[kept:, chans:], high_ref, atoms),
    ]
    for piece in range(pieces):
        start = piece * width
        copies[2 * piece].wait()
        copies[2 * piece + 1].wait()
        term = jnp.zeros((chans, width), jnp.float32)
        for part, place, base in parts:
            table = place[:, base + start : base + start + width]
            term = term + lax.dot_general(part, table, TN, preferred_element_type=jnp.float32)
        out_ref[piece] = (term * (1.0 / math.sqrt(K))).astype(jnp.bfloat16)


def potentials(filtered, low, high, pieces):
    chans = filtered.shape[1] // 2
    atoms = low.shape[1] // 2
    return pl.pallas_call(
        potentials_kernel,
        out_shape=jax.ShapeDtypeStruct((pieces, chans, atoms // pieces), jnp.bfloat16),
        in_specs=[VMEM_SPEC, VMEM_SPEC, HBM_SPEC],
        out_specs=VMEM_SPEC,
        scratch_shapes=[pltpu.VMEM(high.shape, jnp.bfloat16), pltpu.SemaphoreType.DMA((2, pieces))],
        compiler_params=PARAMS,
        name="potentials",
    )(filtered, low, pltpu.with_memory_space_constraint(high, pltpu.HBM))


def pairs_kernel(
    scale_x, regions, place_ref, idx_ref, live_ref, prev_in, own_in, next_in, h_in, after_in, out_ref,
    ext_ref, share_ref, pos_ref, own_ref, weights_ref, near_ref, sems,
):
    chans = h_in.shape[0]
    width = own_in.shape[1]
    nblocks = width // BLOCK
    slots = idx_ref.shape[1]
    count = out_ref.shape[1] // BLOCK
    here = place_ref[0]
    first = place_ref[1]
    copies = [
        pltpu.make_async_copy(source, ext_ref.at[:, pl.ds(at * width, width)], sems.at[at])
        for at, source in enumerate((prev_in, own_in, next_in))
    ]
    share = pl.ds(pl.multiple_of(first * BLOCK, BLOCK), count * BLOCK)
    copies.append(pltpu.make_async_copy(h_in.at[:, share], share_ref, sems.at[3]))
    for copy in copies:
        copy.start()
    for copy in copies:
        copy.wait()
    out_ref[:chans, :] = share_ref[...]
    pieces = ext_ref[chans : chans + 16, :].astype(jnp.float32)
    pos_ref[0:3, :] = (pieces[6:9] + pieces[3:6]) + pieces[0:3]
    for block in range(count):
        at = pl.multiple_of((nblocks + first + block) * BLOCK, BLOCK)
        columns = pos_ref[:, pl.ds(at, BLOCK)].T
        for axis in range(3):
            own_ref[block, axis] = jnp.broadcast_to(columns[:, axis : axis + 1], (BLOCK, BLOCK))
    exponent = -2.0 * math.log2(math.e)

    def slot_step(slot, carried):
        for block in range(count):
            entry = idx_ref[first + block, slot]
            offset = lax.rem(entry // nblocks - here + regions + 1, regions)
            at = pl.multiple_of((offset * nblocks + lax.rem(entry, nblocks)) * BLOCK, BLOCK)
            alive = live_ref[first + block, slot].astype(jnp.float32)
            near = pos_ref[:, pl.ds(at, BLOCK)]
            total = None
            for axis in range(3):
                diff = own_ref[block, axis] - near[axis : axis + 1, :]
                diff = diff - jnp.round(diff)
                term = diff * diff
                if axis == 0:
                    term = term * (scale_x * scale_x)
                total = term if total is None else total + term
            pair = jnp.exp2(total * exponent).astype(jnp.bfloat16)
            to = pl.multiple_of(slot * BLOCK, BLOCK)
            weights_ref[block, :, pl.ds(to, BLOCK)] = pair
            mapped = ext_ref[:chans, pl.ds(at, BLOCK)].astype(jnp.float32) * alive
            near_ref[block, :, pl.ds(to, BLOCK)] = mapped.astype(jnp.bfloat16)
        return carried

    lax.fori_loop(0, slots, slot_step, 0)
    for block in range(count):
        msg = lax.dot_general(near_ref[block], weights_ref[block], NT, preferred_element_type=jnp.float32)
        out_ref[chans:, block * BLOCK : (block + 1) * BLOCK] = (msg * MSG_SCALE).astype(jnp.bfloat16)


def pairs(place, neighbours, live_slots, prev, own, following, h, after, count, scale_x, regions):
    rows, width = own.shape
    chans = h.shape[0]
    slots = neighbours.shape[1]
    work = slots * count * BLOCK * BLOCK
    return pl.pallas_call(
        functools.partial(pairs_kernel, float(scale_x), regions),
        out_shape=jax.ShapeDtypeStruct((2 * chans, count * BLOCK), jnp.bfloat16),
        in_specs=[SMEM_SPEC] * 3 + [ANY_SPEC] * 5,
        out_specs=VMEM_SPEC,
        scratch_shapes=[
            pltpu.VMEM((rows, 3 * width), jnp.bfloat16),
            pltpu.VMEM((chans, count * BLOCK), jnp.bfloat16),
            pltpu.VMEM((8, 3 * width), jnp.float32),
            pltpu.VMEM((count, 3, BLOCK, BLOCK), jnp.float32),
            pltpu.VMEM((count, BLOCK, slots * BLOCK), jnp.bfloat16),
            pltpu.VMEM((count, chans, slots * BLOCK), jnp.bfloat16),
            pltpu.SemaphoreType.DMA((4,)),
        ],
        compiler_params=PARAMS,
        cost_estimate=pl.CostEstimate(
            flops=work * (2 * chans + 20), bytes_accessed=6 * rows * width, transcendentals=work
        ),
        name="pairs",
    )(place, neighbours, live_slots, prev, own, following, h, after)


def update_kernel(place_ref, count_ref, arrived_ref, known_ref, first_ref, second_ref, out_ref):
    potential = arrived_ref[0].astype(jnp.float32)
    for piece in range(1, arrived_ref.shape[0]):
        potential = potential + arrived_ref[piece].astype(jnp.float32)
    chans, share = potential.shape
    stacked = jnp.concatenate([known_ref[...], potential.astype(jnp.bfloat16)], axis=0)
    inner = lax.dot_general(first_ref[...], stacked, TN, preferred_element_type=jnp.float32)
    hidden = jax.nn.silu(inner).astype(jnp.bfloat16)
    h = known_ref[:chans, :].astype(jnp.float32)
    out = h + jnp.dot(second_ref[...], hidden, preferred_element_type=jnp.float32)
    atom = lax.broadcasted_iota(jnp.int32, (chans, share), 1) + place_ref[1] * BLOCK
    new = jnp.where(atom < count_ref[0] * BLOCK, out, 0.0).astype(jnp.bfloat16)
    for piece in range(out_ref.shape[0]):
        out_ref[piece] = new


def update(place, count, arrived, known, first_layer, second_layer):
    return pl.pallas_call(
        update_kernel,
        out_shape=jax.ShapeDtypeStruct(arrived.shape, jnp.bfloat16),
        in_specs=[SMEM_SPEC] * 2 + [VMEM_SPEC] * 4,
        out_specs=VMEM_SPEC,
        compiler_params=PARAMS,
        name="update",
    )(place, count, arrived, known, first_layer, second_layer)


def laid_out(pieces, dim):
    lengths = list(pieces.shape[1:])
    lengths[dim] *= pieces.shape[0]
    return jnp.moveaxis(pieces, 0, dim).reshape(lengths)


def from_others(pieces, axis):
    return lax.all_to_all(pieces, axis, 0, 0, tiled=True)


def local(
    features,
    coords,
    neighbours,
    live_slots,
    block_count,
    kvec,
    msg_weight,
    filter_weight,
    mlp_in,
    mlp_out,
):
    chans, width = features.shape
    nblocks = width // BLOCK
    regions = lax.axis_size("atoms")
    groups_waves = lax.axis_size("waves")
    here = lax.axis_index("atoms")
    per_group = nblocks // groups_waves
    first = lax.axis_index("waves") * per_group
    place = jnp.stack([here, first]).astype(jnp.int32)
    total = regions * width
    waves = kvec.shape[1]
    owned = waves // regions
    low, high, partial_factor, carry = structure(kvec, coords, features, msg_weight[0], block_count, regions)
    arrived = from_others(partial_factor, "atoms")
    prev = lax.ppermute(carry, "atoms", [(i, (i + 1) % regions) for i in range(regions)])
    following = lax.ppermute(carry, "atoms", [((i + 1) % regions, i) for i in range(regions)])
    kf = lax.dynamic_slice_in_dim(kvec, here * owned, owned, 1).astype(jnp.float32)
    kx = kf[0] / regions
    gain = GAIN_TOP / (4.0 + kx * kx + kf[1] * kf[1] + kf[2] * kf[2])
    gain_rows = jnp.broadcast_to(gain[:, None], (owned, 2 * chans))
    mixing = filter_weight[0] * (1.0 / math.sqrt(total))
    everyone = spectral(arrived, gain_rows, mixing)
    filtered = from_others(everyone, "atoms").reshape(waves, 2 * chans)
    known = pairs(
        place, neighbours.T, live_slots.T, prev, carry, following, features, everyone, per_group, regions, regions
    )
    partial_potential = potentials(filtered, low, high, groups_waves)
    potential = from_others(partial_potential, "waves")
    new = update(place, block_count, potential, known, mlp_in[0].T, mlp_out[0])
    return laid_out(from_others(new, "waves"), 1)


def solution(mesh):
    in_specs = (
        P(None, "atoms"),
        P(None, "atoms"),
        P(None, "atoms"),
        P(None, "atoms"),
        P("atoms"),
        P(None, "waves"),
        P(),
        P(),
        P(),
        P(),
    )
    out_specs = P(None, "atoms")
    return jax.shard_map(local, mesh=mesh, in_specs=in_specs, out_specs=out_specs, check_vma=False)
```

time: 97.2 us -> 91.2 us (0.938)
  starting transfers between devices: 35.3 us -> 18.6 us
  blocking collectives: 14.2 us -> 30.8 us
  matrix products: 6.46 us -> 0 us
  Pallas kernels: 11.2 us -> 17.2 us
  local copies, waits for them, and re-layouts: 7.8 us -> 3.93 us
  other arithmetic: 2.92 us -> 1.61 us
    all_to_all x1 -> x2, blocking collectives: 14.2 us -> 30.8 us  [from_others(): return lax.all_to_all(pieces, axis, 0, 0, tiled=True)]
    all_to_all x3 -> x2, starting transfers between devices: 29.6 us -> 17 us  [from_others(): return lax.all_to_all(pieces, axis, 0, 0, tiled=True)]
    all_to_all x3 -> x2, waiting for transfers between devices: 17.5 us -> 5.89 us  [from_others(): return lax.all_to_all(pieces, axis, 0, 0, tiled=True)]
    ppermute x4 -> x2, waiting for transfers between devices: 0.01 us -> 10.8 us  [the longest x1 7.99 us: local(): lax.ppermute(carry, 'atoms', [((i + 1) % regions, i) for i in range(regio...]
    dot_general x5 -> x0, matrix products: 6.46 us -> none  [the longest x1 3.03 us: short_step(): jnp.einsum('csbj,sbij->cbi', near, weights, preferred_element_type=jnp.fl...]
    pallas_call x1 -> x4, Pallas kernels: 7.32 us -> 13 us  [the longest x1 6.69 us: structure(): pl.pallas_call(structure_kernel, out_shape=(jax.ShapeDtypeStruct((kept, 2...]
    gather x5 -> x0, local copies, waits for them, and re-layouts: 4.51 us -> none  [the longest x1 1.33 us: short_step(): jnp.take(own3, blocks, axis=1)]
    ppermute x4 -> x2, starting transfers between devices: 5.67 us -> 1.6 us  [the longest x1 1.6 us: local(): lax.ppermute(carry, 'atoms', [((i + 1) % regions, i) for i in range(regio...]
  transfers between devices with their start and end apart: 7 -> 4, of which waited for: 2 -> 3; matrix products, arithmetic and copies ran while one was open for 16% -> 2% of each run, Pallas kernels for 8% -> 6%
where the time goes in v3:
time: 91.2 us; the launch traced here: 89.6 us
  blocking collectives  30.8 us (34%)
  starting transfers between devices  18.6 us (20%)
  Pallas kernels  17.2 us (19%)
  waiting for transfers between devices  16.7 us (18%)
  local copies, waits for them, and re-layouts  3.93 us (4%)
  other arithmetic  1.61 us (2%)
    all_to_all x2, blocking collectives, from_others(): return lax.all_to_all(pieces, axis, 0, 0, tiled=True)  30.8 us
    all_to_all x2, starting transfers between devices, from_others(): return lax.all_to_all(pieces, axis, 0, 0, tiled=True)  17 us
    ppermute x1, waiting for transfers between devices, local(): lax.ppermute(carry, 'atoms', [((i + 1) % regions, i) for i in range(regio...  7.99 us
    pallas_call x1, Pallas kernels, structure(): pl.pallas_call(structure_kernel, out_shape=(jax.ShapeDtypeStruct((kept, 2...  6.69 us
    all_to_all x2, waiting for transfers between devices, from_others(): return lax.all_to_all(pieces, axis, 0, 0, tiled=True)  5.89 us
    pallas_call x1, Pallas kernels, pairs(): pl.pallas_call(functools.partial(pairs_kernel, float(scale_x), regions),...  5.04 us
    pallas_call x1, Pallas kernels, potentials(): pl.pallas_call(potentials_kernel, out_shape=jax.ShapeDtypeStruct((pieces,...  4.27 us
    unnamed x18, local copies, waits for them, and re-layouts  3.14 us
  transfers between devices with their start and end apart: 4, of which 3 were waited for; matrix products, arithmetic and copies ran while one was open for 2% of the time, Pallas kernels for 6%

profile of v3, /device:TPU:32, one launch (start us, length us, event | category | flops | bytes accessed | tf_op | source)
XLA Modules:
  0.0 89.6 jit_solution(161214855204880453)
XLA Ops:
  0.7 0.0 copy-start
  0.7 0.9 %copy-done = bf16[64,2048]{1,0:T(8,128)(2,1)S(1)} copy-done((bf16[64,2048]{1,0:T(8,128)(2,1)S(1)}, bf16[64,2048]{1,0:T(8,128)(2,1)}, u32[]{:S(2)}) %copy-start) | copy-done | bytes 262168
  1.6 0.0 copy-start.3
  1.6 0.8 copy-done.3
  2.4 0.0 copy-start.4
  2.4 0.7 copy-done.4
  3.1 0.0 copy-start.6
  3.1 0.7 copy-done.6
  3.8 6.7 %structure.1 = (bf16[320,4096]{1,0:T(8,128)(2,1)S(1)}, bf16[192,4096]{1,0:T(8,128)(2,1)}, bf16[32,16,128]{2,1,0:T(8,128)(2,1)}, bf16[80,2048]{1,0:T(8,128)(2,1)S(1)}) custom-call(s32[3,512]{1,0:T(4,128)S(1)} %copy-done.6, f32[3,2048]{1,0:T(4,128)S(1)} %copy-done.3, bf16[64,2048]{1,0:T(8,128)(2,1)S(1)} %copy-done, bf16[64,64]{1,0:T(8,128)(2,1)S(1)} %bitcast.19, ...), custom_call_target="tpu_custom_call" | custom-call | tf_op jit(solution)/shard_map/structure/pallas_call | solution.py:120
  10.5 8.6 %all-to-all-start = ((bf16[32,16,128]{2,1,0:T(8,128)(2,1)}), bf16[32,16,128]{2,1,0:T(8,128)(2,1)S(1)}, u32[]{:S(2)}, u32[]{:S(2)}) async-start(bf16[32,16,128]{2,1,0:T(8,128)(2,1)} %get-tuple-element.9), calls=%async_computation | async-start | bytes 262144 | tf_op jit(solution)/shard_map/all_to_all | solution.py:331
  19.1 0.8 dynamic-slice_convert_fusion
  19.9 0.8 multiply_bitcast_fusion.mixing_ref
  20.7 5.9 %all-to-all-done.arrived_ref = bf16[32,16,128]{2,1,0:T(8,128)(2,1)S(1)} async-done(((bf16[32,16,128]{2,1,0:T(8,128)(2,1)}), bf16[32,16,128]{2,1,0:T(8,128)(2,1)S(1)}, u32[]{:S(2)}, u32[]{:S(2)}) %all-to-all-start) | async-done | bytes 131104 | tf_op jit(solution)/shard_map/all_to_all | solution.py:331
  26.6 0.1 broadcast_in_dim.2.gain_ref
  26.6 0.3 spectral.1.after_in
  27.0 12.1 %all_to_all.20 = bf16[32,16,128]{2,1,0:T(8,128)(2,1)S(1)} all-to-all(bf16[32,16,128]{2,1,0:T(8,128)(2,1)S(1)} %spectral.1.after_in), channel_id=1, replica_groups=mesh['atoms'=32,'waves'=8] {'atoms'}, dimensions={0} | all-to-all | bytes 262144 | tf_op jit(solution)/shard_map/all_to_all | solution.py:331
  39.1 0.0 copy-start.1
  39.1 0.0 copy-start.7
  39.1 0.0 copy-start.8
  39.1 0.0 copy-start.2
  39.1 0.0 copy-start.5
  39.1 4.3 %potentials.1 = bf16[8,64,256]{2,1,0:T(8,128)(2,1)} custom-call(bf16[512,128]{1,0:T(8,128)(2,1)S(1)} %bitcast.17, bf16[320,4096]{1,0:T(8,128)(2,1)S(1)} %get-tuple-element.10.low_ref, bf16[192,4096]{1,0:T(8,128)(2,1)} %get-tuple-element.11.high_in), custom_call_target="tpu_custom_call" | custom-call | tf_op jit(solution)/shard_map/potentials/pallas_call | solution.py:200
  43.4 8.4 %all-to-all-start.2 = ((bf16[8,64,256]{2,1,0:T(8,128)(2,1)}), bf16[8,64,256]{2,1,0:T(8,128)(2,1)S(1)}, u32[]{:S(2)}, u32[]{:S(2)}) async-start(bf16[8,64,256]{2,1,0:T(8,128)(2,1)} %potentials.1), calls=%async_computation.2 | async-start | bytes 524288 | tf_op jit(solution)/shard_map/all_to_all | solution.py:331
  51.8 1.6 %collective-permute-start.1 = (bf16[80,2048]{1,0:T(8,128)(2,1)S(1)}, bf16[80,2048]{1,0:T(8,128)(2,1)S(1)}, u32[]{:S(2)}, u32[]{:S(2)}) collective-permute-start(bf16[80,2048]{1,0:T(8,128)(2,1)S(1)} %get-tuple-element.12.own_in), channel_id=1, source_target_pairs={{8,0},{16,8},{24,16},{32,24},{40,32},{48,40},{56,48},{64,56},{72,6... | collective-permute-start | bytes 983048 | tf_op jit(solution)/shard_map/ppermute | solution.py:360
  53.4 0.0 collective-permute-start
  53.4 0.1 pad_add_fusion.place_ref
  53.5 8.0 %collective-permute-done.1.next_in = bf16[80,2048]{1,0:T(8,128)(2,1)S(1)} collective-permute-done((bf16[80,2048]{1,0:T(8,128)(2,1)S(1)}, bf16[80,2048]{1,0:T(8,128)(2,1)S(1)}, u32[]{:S(2)}, u32[]{:S(2)}) %collective-permute-start.1) | collective-permute-done | bytes 327712 | tf_op jit(solution)/shard_map/ppermute | solution.py:360
  61.4 2.8 %collective-permute-done.prev_in = bf16[80,2048]{1,0:T(8,128)(2,1)S(1)} collective-permute-done((bf16[80,2048]{1,0:T(8,128)(2,1)S(1)}, bf16[80,2048]{1,0:T(8,128)(2,1)S(1)}, u32[]{:S(2)}, u32[]{:S(2)}) %collective-permute-start) | collective-permute-done | bytes 327712 | tf_op jit(solution)/shard_map/ppermute | solution.py:359
  64.2 0.0 copy-done.1
  64.2 0.0 copy-done.7
  64.2 0.0 copy-done.8
  64.2 5.0 %pairs.1.known_ref = bf16[128,256]{1,0:T(8,128)(2,1)S(1)} custom-call(s32[2]{0:T(128)S(1)} %pad_add_fusion.place_ref, s32[16,27]{1,0:T(8,128)S(1)} %bitcast.21, s32[16,27]{1,0:T(8,128)S(1)} %bitcast.22, bf16[80,2048]{1,0:T(8,128)(2,1)S(1)} %collective-permute-done.prev_in, bf16[80,2048]{1,0:T(8,128)(2,1)S(1)} %get-tuple-element.12.own_in, ...), custom_call_target="tpu_custom_call" | custom-call | flops 130940928 | bytes 983040 | tf_op jit(solution)/shard_map/pairs/pallas_call | solution.py:275
  69.3 0.0 all-to-all-done.2.arrived_ref
  69.3 0.0 copy-done.2
  69.3 0.0 copy-done.5
  69.3 0.9 update.1
  70.2 18.7 %all_to_all.21 = bf16[8,64,256]{2,1,0:T(8,128)(2,1)S(1)} all-to-all(bf16[8,64,256]{2,1,0:T(8,128)(2,1)S(1)} %update.1), channel_id=1, replica_groups=mesh['atoms'=32,'waves'=8] {'waves'}, dimensions={0} | all-to-all | bytes 524288 | tf_op jit(solution)/shard_map/all_to_all | solution.py:331
  88.9 0.7 copy.12
  (1 shorter events, 0.0 us)
Async XLA Ops:
  0.7 1.0 %copy-start = (bf16[64,2048]{1,0:T(8,128)(2,1)S(1)}, bf16[64,2048]{1,0:T(8,128)(2,1)}, u32[]{:S(2)}) copy-start(bf16[64,2048]{1,0:T(8,128)(2,1)} %h_in.1) | copy-start | bytes 786436
  1.6 0.8 copy-start.3
  2.4 0.7 copy-start.4
  3.1 0.7 copy-start.6
  10.5 16.1 %all-to-all-start = ((bf16[32,16,128]{2,1,0:T(8,128)(2,1)}), bf16[32,16,128]{2,1,0:T(8,128)(2,1)S(1)}, u32[]{:S(2)}, u32[]{:S(2)}) async-start(bf16[32,16,128]{2,1,0:T(8,128)(2,1)} %get-tuple-element.9), calls=%async_computation | async-start | bytes 262144 | tf_op jit(solution)/shard_map/all_to_all | solution.py:331
  39.1 25.2 %copy-start.1 = (bf16[64,2048]{1,0:T(8,128)(2,1)S(1)}, bf16[64,2048]{1,0:T(8,128)(2,1)}, u32[]{:S(2)}) copy-start(bf16[64,2048]{1,0:T(8,128)(2,1)} %h_in.1) | copy-start | bytes 786436
  39.1 25.2 %copy-start.7 = (s32[27,16]{0,1:T(8,128)S(1)}, s32[27,16]{0,1:T(8,128)}, u32[]{:S(2)}) copy-start(s32[27,16]{0,1:T(8,128)} %param.12) | copy-start | bytes 5188
  39.1 25.2 %copy-start.8 = (s32[27,16]{0,1:T(8,128)S(1)}, s32[27,16]{0,1:T(8,128)}, u32[]{:S(2)}) copy-start(s32[27,16]{0,1:T(8,128)} %param.13) | copy-start | bytes 5188
  39.1 30.2 %copy-start.2 = (bf16[1,128,192]{1,2,0:T(8,128)(2,1)S(1)}, bf16[1,128,192]{1,2,0:T(8,128)(2,1)}, u32[]{:S(2)}) copy-start(bf16[1,128,192]{1,2,0:T(8,128)(2,1)} %param.18) | copy-start | bytes 147460
  39.1 30.2 %copy-start.5 = (bf16[1,64,128]{2,1,0:T(8,128)(2,1)S(1)}, bf16[1,64,128]{2,1,0:T(8,128)(2,1)}, u32[]{:S(2)}) copy-start(bf16[1,64,128]{2,1,0:T(8,128)(2,1)} %param.19) | copy-start | bytes 49156
  43.4 25.9 %all-to-all-start.2 = ((bf16[8,64,256]{2,1,0:T(8,128)(2,1)}), bf16[8,64,256]{2,1,0:T(8,128)(2,1)S(1)}, u32[]{:S(2)}, u32[]{:S(2)}) async-start(bf16[8,64,256]{2,1,0:T(8,128)(2,1)} %potentials.1), calls=%async_computation.2 | async-start | bytes 524288 | tf_op jit(solution)/shard_map/all_to_all | solution.py:331
  51.8 9.7 %collective-permute-start.1 = (bf16[80,2048]{1,0:T(8,128)(2,1)S(1)}, bf16[80,2048]{1,0:T(8,128)(2,1)S(1)}, u32[]{:S(2)}, u32[]{:S(2)}) collective-permute-start(bf16[80,2048]{1,0:T(8,128)(2,1)S(1)} %get-tuple-element.12.own_in), channel_id=1, source_target_pairs={{8,0},{16,8},{24,16},{32,24},{40,32},{48,40},{56,48},{64,56},{72,6... | collective-permute-start | bytes 983048 | tf_op jit(solution)/shard_map/ppermute | solution.py:360
  53.4 10.8 %collective-permute-start = (bf16[80,2048]{1,0:T(8,128)(2,1)S(1)}, bf16[80,2048]{1,0:T(8,128)(2,1)S(1)}, u32[]{:S(2)}, u32[]{:S(2)}) collective-permute-start(bf16[80,2048]{1,0:T(8,128)(2,1)S(1)} %get-tuple-element.12.own_in), channel_id=1, source_target_pairs={{0,8},{8,16},{16,24},{24,32},{32,40},{40,48},{48,56},{56,64},{64,7... | collective-permute-start | bytes 983048 | tf_op jit(solution)/shard_map/ppermute | solution.py:359

commit v4 on v3

v4 whole, which is shorter than its diff:
```python
import functools
import math

import jax
import jax.numpy as jnp
from jax import lax
from jax.experimental import pallas as pl
from jax.experimental.pallas import tpu as pltpu
from jax.sharding import PartitionSpec as P


K = 4096
BLOCK = 128

MSG_SCALE = 0.125
GAIN_TOP = 20.0
SIN_COEFS = (3.1415926401307073, -5.167710083507923, 2.5500775232148563, -0.5982912856211671, 0.07765766030589402)
COS_COEFS = (0.9999999532476085, -4.934792830619664, 4.058411352862771, -1.3318765680813944, 0.21968961109803095)
ROOT2 = math.sqrt(2.0)
TILE = 256
ROWS = 64
LIMIT = 16 * 2**20
VMEM_SPEC = pl.BlockSpec(memory_space=pltpu.VMEM)
SMEM_SPEC = pl.BlockSpec(memory_space=pltpu.SMEM)
ANY_SPEC = pl.BlockSpec(memory_space=pl.ANY)
HBM_SPEC = pl.BlockSpec(memory_space=pltpu.HBM)
PARAMS = pltpu.CompilerParams(vmem_limit_bytes=LIMIT)
NT = (((1,), (1,)), ((), ()))
TN = (((0,), (0,)), ((), ()))


def kept_rows(waves):
    return waves * 5 // 8


def horner(coefs, scale, u):
    value = coefs[-1] * scale
    for coef in coefs[-2::-1]:
        value = value * u + coef * scale
    return value


def phases_of(turns):
    r = turns - jnp.round(turns)
    u = r * r
    s = r * horner(SIN_COEFS, ROOT2, u)
    c = horner(COS_COEFS, ROOT2, u)
    return 1.0 - s * s, s * c


def three_pieces(values):
    first = values.astype(jnp.bfloat16)
    rest = values - first.astype(jnp.float32)
    second = rest.astype(jnp.bfloat16)
    third = (rest - second.astype(jnp.float32)).astype(jnp.bfloat16)
    return first.astype(jnp.float32), second.astype(jnp.float32), third.astype(jnp.float32)


def structure_kernel(
    scale, regions, place_ref, count_ref, kvec_in, coords_in, h_in, weight_in, mixing_in,
    low_ref, high_out, out_ref, carry_ref, gain_ref, mixing_ref,
    kvec_ref, coords_ref, h_ref, weight_ref, ka_ref, xs_ref, high_ref, in_sems, sems,
):
    waves = kvec_ref.shape[1]
    chans, atoms = h_ref.shape
    kept = low_ref.shape[0]
    owned = out_ref.shape[1]
    f32 = dict(preferred_element_type=jnp.float32)
    taken = [
        pltpu.make_async_copy(source, target, in_sems.at[at])
        for at, (source, target) in enumerate(
            (
                (kvec_in, kvec_ref),
                (coords_in, coords_ref),
                (h_in, h_ref),
                (weight_in, weight_ref),
                (mixing_in, mixing_ref),
            )
        )
    ]
    for copy in taken:
        copy.start()
    taken[0].wait()
    kf = kvec_ref[...].astype(jnp.float32)
    ka = jnp.concatenate([kf, kf, kf, jnp.zeros((7, waves), jnp.float32)], axis=0)
    ka_ref[...] = ka.T.astype(jnp.bfloat16)
    kx = kf[0:1] / regions
    gain = GAIN_TOP / (4.0 + kx * kx + kf[1:2] * kf[1:2] + kf[2:3] * kf[2:3])
    lane = lax.broadcasted_iota(jnp.int32, (owned, waves), 1)
    own = lane == lax.broadcasted_iota(jnp.int32, (owned, waves), 0) + place_ref[0] * owned
    mine = jnp.sum(jnp.where(own, jnp.broadcast_to(gain, (owned, waves)), 0.0), axis=1, keepdims=True)
    gain_ref[...] = jnp.broadcast_to(mine * scale, gain_ref.shape)
    taken[1].wait()
    first, second, third = three_pieces(coords_ref[...])
    xs = jnp.concatenate([first, second, third, jnp.zeros((7, atoms), jnp.float32)], axis=0)
    xs_ref[...] = xs.astype(jnp.bfloat16)
    gap = jnp.zeros((5, atoms), jnp.float32)
    spread = jnp.concatenate([first, gap, second, gap, third, gap], axis=0)
    carry_ref[chans:, :] = spread.astype(jnp.bfloat16)
    live_atoms = count_ref[0] * BLOCK
    low_sum = jnp.zeros((kept, 2 * chans), jnp.float32)
    high_sum = jnp.zeros((waves - kept, 2 * chans), jnp.float32)
    copies = []
    for start in range(0, atoms, TILE):
        cos_span = slice(start, start + TILE)
        sin_span = slice(atoms + start, atoms + start + TILE)
        xt = xs_ref[:, cos_span]
        for row in range(0, waves, ROWS):
            turns = jnp.dot(ka_ref[row : row + ROWS, :], xt, **f32)
            cosv, sinv = phases_of(turns)
            place, at = (low_ref, row) if row < kept else (high_ref, row - kept)
            place[at : at + ROWS, cos_span] = cosv.astype(jnp.bfloat16)
            place[at : at + ROWS, sin_span] = sinv.astype(jnp.bfloat16)
        for half in range(2):
            span = pl.ds(half * atoms + start, TILE)
            copy = pltpu.make_async_copy(high_ref.at[:, span], high_out.at[:, span], sems.at[half, start // TILE])
            copy.start()
            copies.append(copy)
        if start == 0:
            for copy in taken[2:]:
                copy.wait()
        carry_ref[:chans, cos_span] = jnp.dot(weight_ref[...], h_ref[:, cos_span], **f32).astype(jnp.bfloat16)
        atom = lax.broadcasted_iota(jnp.int32, (chans, TILE), 1) + start
        ht = jnp.where(atom < live_atoms, h_ref[:, cos_span].astype(jnp.float32), 0.0)
        zero = jnp.zeros_like(ht)
        hc = jnp.concatenate([ht, zero], axis=0).astype(jnp.bfloat16)
        hs = jnp.concatenate([zero, ht], axis=0).astype(jnp.bfloat16)
        low_sum = low_sum + lax.dot_general(low_ref[:, cos_span], hc, NT, **f32)
        low_sum = low_sum + lax.dot_general(low_ref[:, sin_span], hs, NT, **f32)
        high_sum = high_sum + lax.dot_general(high_ref[:, cos_span], hc, NT, **f32)
        high_sum = high_sum + lax.dot_general(high_ref[:, sin_span], hs, NT, **f32)
    out_ref[: kept // owned] = low_sum.astype(jnp.bfloat16).reshape(kept // owned, owned, 2 * chans)
    out_ref[kept // owned :] = high_sum.astype(jnp.bfloat16).reshape(-1, owned, 2 * chans)
    for copy in copies:
        copy.wait()


def in_hbm(*arrays):
    return tuple(pltpu.with_memory_space_constraint(array, pltpu.HBM) for array in arrays)


def structure(place, count, kvec, coords, h, weight, mixing, scale, regions):
    waves, atoms, chans = kvec.shape[1], coords.shape[1], h.shape[0]
    kept = kept_rows(waves)
    owned = waves // regions
    return pl.pallas_call(
        functools.partial(structure_kernel, scale, float(regions)),
        out_shape=(
            jax.ShapeDtypeStruct((kept, 2 * atoms), jnp.bfloat16),
            pltpu.HBM((waves - kept, 2 * atoms), jnp.bfloat16),
            jax.ShapeDtypeStruct((regions, owned, 2 * chans), jnp.bfloat16),
            jax.ShapeDtypeStruct((chans + 24, atoms), jnp.bfloat16),
            jax.ShapeDtypeStruct((owned, 2 * chans), jnp.float32),
            jax.ShapeDtypeStruct(mixing.shape, jnp.float32),
        ),
        in_specs=[SMEM_SPEC] * 2 + [HBM_SPEC] * 5,
        out_specs=(VMEM_SPEC, HBM_SPEC) + (VMEM_SPEC,) * 4,
        scratch_shapes=[
            pltpu.VMEM(kvec.shape, jnp.int32),
            pltpu.VMEM(coords.shape, jnp.float32),
            pltpu.VMEM(h.shape, jnp.bfloat16),
            pltpu.VMEM(weight.shape, jnp.bfloat16),
            pltpu.VMEM((waves, 16), jnp.bfloat16),
            pltpu.VMEM((16, atoms), jnp.bfloat16),
            pltpu.VMEM((waves - kept, 2 * atoms), jnp.bfloat16),
            pltpu.SemaphoreType.DMA((5,)),
            pltpu.SemaphoreType.DMA((2, atoms // TILE)),
        ],
        compiler_params=PARAMS,
        name="structure",
    )(place, count, *in_hbm(kvec, coords, h, weight, mixing))


def spectral_kernel(arrived_ref, gain_ref, mixing_ref, out_ref):
    chans = mixing_ref.shape[0]
    factor = arrived_ref[0].astype(jnp.float32)
    for piece in range(1, arrived_ref.shape[0]):
        factor = factor + arrived_ref[piece].astype(jnp.float32)
    high = dict(precision=lax.Precision.HIGHEST, preferred_element_type=jnp.float32)
    mixing = mixing_ref[...]
    cos_part = jnp.dot(factor[:, :chans], mixing, **high)
    sin_part = jnp.dot(factor[:, chans:], mixing, **high)
    filtered = (jnp.concatenate([cos_part, sin_part], axis=1) * gain_ref[...]).astype(jnp.bfloat16)
    for piece in range(out_ref.shape[0]):
        out_ref[piece] = filtered


def spectral(arrived, gain, mixing):
    return pl.pallas_call(
        spectral_kernel,
        out_shape=jax.ShapeDtypeStruct(arrived.shape, jnp.bfloat16),
        in_specs=[VMEM_SPEC] * 3,
        out_specs=VMEM_SPEC,
        compiler_params=PARAMS,
        name="spectral",
    )(arrived, gain, mixing)


def potentials_kernel(filtered_ref, low_ref, high_in, out_ref, high_ref, sum_ref, sems):
    chans = out_ref.shape[1]
    pieces, _, width = out_ref.shape
    atoms = pieces * width
    kept = low_ref.shape[0]
    copies = []
    for piece in range(pieces):
        for half in range(2):
            span = pl.ds(half * atoms + piece * width, width)
            copy = pltpu.make_async_copy(high_in.at[:, span], high_ref.at[:, span], sems.at[half, piece])
            copy.start()
            copies.append(copy)

    def term(rows, table, piece):
        cos_span = slice(piece * width, (piece + 1) * width)
        sin_span = slice(atoms + piece * width, atoms + (piece + 1) * width)
        f32 = dict(preferred_element_type=jnp.float32)
        return lax.dot_general(filtered_ref[rows, :chans], table[:, cos_span], TN, **f32) + lax.dot_general(
            filtered_ref[rows, chans:], table[:, sin_span], TN, **f32
        )

    for piece in range(pieces):
        sum_ref[piece] = term(slice(0, kept), low_ref, piece)
    for piece in range(pieces):
        copies[2 * piece].wait()
        copies[2 * piece + 1].wait()
        whole = sum_ref[piece] + term(slice(kept, filtered_ref.shape[0]), high_ref, piece)
        out_ref[piece] = (whole * (1.0 / math.sqrt(K))).astype(jnp.bfloat16)


def potentials(filtered, low, high, pieces):
    chans = filtered.shape[1] // 2
    atoms = low.shape[1] // 2
    return pl.pallas_call(
        potentials_kernel,
        out_shape=jax.ShapeDtypeStruct((pieces, chans, atoms // pieces), jnp.bfloat16),
        in_specs=[VMEM_SPEC, VMEM_SPEC, HBM_SPEC],
        out_specs=VMEM_SPEC,
        scratch_shapes=[
            pltpu.VMEM(high.shape, jnp.bfloat16),
            pltpu.VMEM((pieces, chans, atoms // pieces), jnp.float32),
            pltpu.SemaphoreType.DMA((2, pieces)),
        ],
        compiler_params=PARAMS,
        name="potentials",
    )(filtered, low, *in_hbm(high))


def pairs_kernel(
    scale_x, regions, place_ref, count_ref, idx_ref, live_ref, prev_in, own_in, next_in, h_in, first_in, second_in,
    inner_ref, share_ref, alive_ref, third_ref, second_ref,
    ext_ref, first_ref, pos_ref, own_ref, weights_ref, near_ref, sems,
):
    chans = h_in.shape[0]
    width = own_in.shape[1]
    nblocks = width // BLOCK
    slots = idx_ref.shape[1]
    count = share_ref.shape[1] // BLOCK
    here = place_ref[0]
    first = place_ref[1]
    share = pl.ds(pl.multiple_of(first * BLOCK, BLOCK), count * BLOCK)
    moves = [(source, ext_ref.at[:, pl.ds(at * width, width)]) for at, source in enumerate((prev_in, own_in, next_in))]
    moves += [(h_in.at[:, share], share_ref), (first_in, first_ref), (second_in, second_ref)]
    copies = [pltpu.make_async_copy(source, target, sems.at[at]) for at, (source, target) in enumerate(moves)]
    for copy in copies:
        copy.start()
    atom = lax.broadcasted_iota(jnp.int32, alive_ref.shape, 1) + first * BLOCK
    alive_ref[...] = jnp.where(atom < count_ref[0] * BLOCK, 1.0, 0.0)
    for copy in copies:
        copy.wait()
    pieces = [ext_ref[chans + 8 * at : chans + 8 * at + 8, :].astype(jnp.float32) for at in range(3)]
    pos_ref[...] = (pieces[2] + pieces[1]) + pieces[0]
    for block in range(count):
        at = pl.multiple_of((nblocks + first + block) * BLOCK, BLOCK)
        columns = pos_ref[:, pl.ds(at, BLOCK)].T
        for axis in range(3):
            own_ref[block, axis] = jnp.broadcast_to(columns[:, axis : axis + 1], (BLOCK, BLOCK))
    exponent = -2.0 * math.log2(math.e)

    def slot_step(slot, carried):
        for block in range(count):
            entry = idx_ref[first + block, slot]
            offset = lax.rem(entry // nblocks - here + regions + 1, regions)
            at = pl.multiple_of((offset * nblocks + lax.rem(entry, nblocks)) * BLOCK, BLOCK)
            used = live_ref[first + block, slot].astype(jnp.float32)
            near = pos_ref[:, pl.ds(at, BLOCK)]
            total = None
            for axis in range(3):
                diff = own_ref[block, axis] - near[axis : axis + 1, :]
                diff = diff - jnp.round(diff)
                term = diff * diff
                if axis == 0:
                    term = term * (scale_x * scale_x)
                total = term if total is None else total + term
            pair = jnp.exp2(total * exponent).astype(jnp.bfloat16)
            to = pl.multiple_of(slot * BLOCK, BLOCK)
            weights_ref[block, :, pl.ds(to, BLOCK)] = pair
            mapped = ext_ref[:chans, pl.ds(at, BLOCK)].astype(jnp.float32) * used
            near_ref[block, :, pl.ds(to, BLOCK)] = mapped.astype(jnp.bfloat16)
        return carried

    lax.fori_loop(0, slots, slot_step, 0)
    f32 = dict(preferred_element_type=jnp.float32)
    outer = first_ref[: 2 * chans, :]
    third_ref[...] = first_ref[2 * chans :, :].astype(jnp.float32).T.astype(jnp.bfloat16)
    for block in range(count):
        span = slice(block * BLOCK, (block + 1) * BLOCK)
        msg = lax.dot_general(near_ref[block], weights_ref[block], NT, **f32)
        msg = (msg * MSG_SCALE).astype(jnp.bfloat16)
        known = jnp.concatenate([share_ref[:, span], msg], axis=0)
        inner_ref[:, span] = lax.dot_general(outer, known, TN, **f32)


def pairs(place, live_blocks, neighbours, live_slots, prev, own, following, h, first, second, count, regions):
    rows, width = own.shape
    chans = h.shape[0]
    hidden = first.shape[1]
    slots = neighbours.shape[1]
    share = count * BLOCK
    work = slots * share * BLOCK
    return pl.pallas_call(
        functools.partial(pairs_kernel, float(regions), regions),
        out_shape=(
            jax.ShapeDtypeStruct((hidden, share), jnp.float32),
            jax.ShapeDtypeStruct((chans, share), jnp.bfloat16),
            jax.ShapeDtypeStruct((8, share), jnp.float32),
            jax.ShapeDtypeStruct((hidden, chans), jnp.bfloat16),
            jax.ShapeDtypeStruct(second.shape, jnp.bfloat16),
        ),
        in_specs=[SMEM_SPEC] * 4 + [ANY_SPEC] * 3 + [HBM_SPEC] * 3,
        out_specs=(VMEM_SPEC,) * 5,
        scratch_shapes=[
            pltpu.VMEM((rows, 3 * width), jnp.bfloat16),
            pltpu.VMEM(first.shape, jnp.bfloat16),
            pltpu.VMEM((8, 3 * width), jnp.float32),
            pltpu.VMEM((count, 3, BLOCK, BLOCK), jnp.float32),
            pltpu.VMEM((count, BLOCK, slots * BLOCK), jnp.bfloat16),
            pltpu.VMEM((count, chans, slots * BLOCK), jnp.bfloat16),
            pltpu.SemaphoreType.DMA((6,)),
        ],
        compiler_params=PARAMS,
        cost_estimate=pl.CostEstimate(
            flops=work * (2 * chans + 20), bytes_accessed=6 * rows * width, transcendentals=work
        ),
        name="pairs",
    )(place, live_blocks, neighbours, live_slots, prev, own, following, *in_hbm(h, first, second))


def update_kernel(arrived_ref, inner_ref, share_ref, alive_ref, third_ref, second_ref, out_ref):
    potential = arrived_ref[0].astype(jnp.float32)
    for piece in range(1, arrived_ref.shape[0]):
        potential = potential + arrived_ref[piece].astype(jnp.float32)
    f32 = dict(preferred_element_type=jnp.float32)
    inner = inner_ref[...] + jnp.dot(third_ref[...], potential.astype(jnp.bfloat16), **f32)
    hidden = jax.nn.silu(inner).astype(jnp.bfloat16)
    out = share_ref[...].astype(jnp.float32) + jnp.dot(second_ref[...], hidden, **f32)
    new = jnp.where(alive_ref[0:1, :] > 0.0, out, 0.0).astype(jnp.bfloat16)
    for piece in range(out_ref.shape[0]):
        out_ref[piece] = new


def update(arrived, known):
    return pl.pallas_call(
        update_kernel,
        out_shape=jax.ShapeDtypeStruct(arrived.shape, jnp.bfloat16),
        in_specs=[VMEM_SPEC] * 6,
        out_specs=VMEM_SPEC,
        compiler_params=PARAMS,
        name="update",
    )(arrived, *known)


def laid_out(pieces, dim):
    lengths = list(pieces.shape[1:])
    lengths[dim] *= pieces.shape[0]
    return jnp.moveaxis(pieces, 0, dim).reshape(lengths)


def from_others(pieces, axis):
    return lax.all_to_all(pieces, axis, 0, 0, tiled=True)


def local(
    features,
    coords,
    neighbours,
    live_slots,
    block_count,
    kvec,
    msg_weight,
    filter_weight,
    mlp_in,
    mlp_out,
):
    chans, width = features.shape
    nblocks = width // BLOCK
    regions = lax.axis_size("atoms")
    groups_waves = lax.axis_size("waves")
    here = lax.axis_index("atoms")
    per_group = nblocks // groups_waves
    first = lax.axis_index("waves") * per_group
    place = jnp.stack([here, first]).astype(jnp.int32)
    total = regions * width
    waves = kvec.shape[1]
    low, high, partial_factor, carry, gain_rows, mixing = structure(
        place, block_count, kvec, coords, features, msg_weight[0], filter_weight[0], 1.0 / math.sqrt(total), regions
    )
    arrived = from_others(partial_factor, "atoms")
    prev = lax.ppermute(carry, "atoms", [(i, (i + 1) % regions) for i in range(regions)])
    following = lax.ppermute(carry, "atoms", [((i + 1) % regions, i) for i in range(regions)])
    everyone = spectral(arrived, gain_rows, mixing)
    filtered = from_others(everyone, "atoms").reshape(waves, 2 * chans)
    partial_potential = potentials(filtered, low, high, groups_waves)
    potential = from_others(partial_potential, "waves")
    known = pairs(
        place, block_count, neighbours.T, live_slots.T, prev, carry, following,
        features, mlp_in[0].T, mlp_out[0], per_group, regions,
    )
    new = update(potential, known)
    return laid_out(from_others(new, "waves"), 1)


def solution(mesh):
    in_specs = (
        P(None, "atoms"),
        P(None, "atoms"),
        P(None, "atoms"),
        P(None, "atoms"),
        P("atoms"),
        P(None, "waves"),
        P(),
        P(),
        P(),
        P(),
    )
    out_specs = P(None, "atoms")
    return jax.shard_map(local, mesh=mesh, in_specs=in_specs, out_specs=out_specs, check_vma=False)
```

time: 91.2 us -> 89.2 us (0.978)
  blocking collectives: 30.8 us -> 46.3 us
  starting transfers between devices: 18.6 us -> 10 us
  waiting for transfers between devices: 16.7 us -> 11.5 us
  local copies, waits for them, and re-layouts: 3.93 us -> 0.73 us
  other arithmetic: 1.61 us -> 0.08 us
  Pallas kernels: 17.2 us -> 18.5 us
    all_to_all x2 -> x3, blocking collectives: 30.8 us -> 46.3 us  [from_others(): return lax.all_to_all(pieces, axis, 0, 0, tiled=True)]
    all_to_all x2 -> x1, starting transfers between devices: 17 us -> 8.41 us  [from_others(): return lax.all_to_all(pieces, axis, 0, 0, tiled=True)]
    all_to_all x2 -> x1, waiting for transfers between devices: 5.89 us -> 0.01 us  [from_others(): return lax.all_to_all(pieces, axis, 0, 0, tiled=True)]
    unnamed x18 -> x4, local copies, waits for them, and re-layouts: 3.14 us -> 0.01 us
    pallas_call x2, Pallas kernels: 11.7 us -> 13.7 us  [the longest x1 7.32 us: structure(): pl.pallas_call(functools.partial(structure_kernel, scale, float(regions))...]
  transfers between devices with their start and end apart: 4 -> 3, of which waited for: 3 -> 2; matrix products, arithmetic and copies ran while one was open for 2% -> 0% of each run, Pallas kernels for 6% -> 7%
where the time goes in v4:
time: 89.2 us; the launch traced here: 87.8 us
  blocking collectives  46.3 us (52%)
  Pallas kernels  18.5 us (21%)
  waiting for transfers between devices  11.5 us (13%)
  starting transfers between devices  10 us (11%)
    all_to_all x3, blocking collectives, from_others(): return lax.all_to_all(pieces, axis, 0, 0, tiled=True)  46.3 us
    ppermute x1, waiting for transfers between devices, local(): lax.ppermute(carry, 'atoms', [((i + 1) % regions, i) for i in range(regio...  8.42 us
    all_to_all x1, starting transfers between devices, from_others(): return lax.all_to_all(pieces, axis, 0, 0, tiled=True)  8.41 us
    pallas_call x1, Pallas kernels, structure(): pl.pallas_call(functools.partial(structure_kernel, scale, float(regions))...  7.32 us
    pallas_call x1, Pallas kernels, pairs(): pl.pallas_call(functools.partial(pairs_kernel, float(regions), regions),...  6.33 us
    pallas_call x1, Pallas kernels, potentials(): pl.pallas_call(potentials_kernel, out_shape=jax.ShapeDtypeStruct((pieces,...  4.16 us
    ppermute x1, waiting for transfers between devices, local(): lax.ppermute(carry, 'atoms', [(i, (i + 1) % regions) for i in range(regio...  3.07 us
  transfers between devices with their start and end apart: 3, of which 2 were waited for; matrix products, arithmetic and copies ran while one was open for 0% of the time, Pallas kernels for 7%

profile of v4, /device:TPU:32, one launch (start us, length us, event | category | flops | bytes accessed | tf_op | source)
XLA Modules:
  0.0 87.8 jit_solution(1575215122298259931)
XLA Ops:
  0.7 0.1 pad_add_fusion.place_ref
  0.7 7.3 %structure.1 = (bf16[320,4096]{1,0:T(8,128)(2,1)S(1)}, bf16[192,4096]{1,0:T(8,128)(2,1)}, bf16[32,16,128]{2,1,0:T(8,128)(2,1)S(1)}, bf16[88,2048]{1,0:T(8,128)(2...) custom-call(s32[2]{0:T(128)S(1)} %pad_add_fusion.place_ref, s32[1]{0:T(128)S(6)} %copy.13.count_ref, ...), custom_call_target="tpu_custom_call" | custom-call | tf_op jit(solution)/shard_map/structure/pallas_call | solution.py:146
  8.1 15.9 %all_to_all.20.arrived_ref = bf16[32,16,128]{2,1,0:T(8,128)(2,1)S(1)} all-to-all(bf16[32,16,128]{2,1,0:T(8,128)(2,1)S(1)} %get-tuple-element.16), channel_id=1, replica_groups=mesh['atoms'=32,'waves'=8] {'atoms'}, dimensions={0} | all-to-all | bytes 262144 | tf_op jit(solution)/shard_map/all_to_all | solution.py:378
  23.9 0.3 spectral.1
  24.3 12.1 %all_to_all.21 = bf16[32,16,128]{2,1,0:T(8,128)(2,1)S(1)} all-to-all(bf16[32,16,128]{2,1,0:T(8,128)(2,1)S(1)} %spectral.1), channel_id=1, replica_groups=mesh['atoms'=32,'waves'=8] {'atoms'}, dimensions={0} | all-to-all | bytes 262144 | tf_op jit(solution)/shard_map/all_to_all | solution.py:378
  36.4 0.0 copy-start
  36.4 0.0 copy-start.1
  36.4 4.2 %potentials.1 = bf16[8,64,256]{2,1,0:T(8,128)(2,1)} custom-call(bf16[512,128]{1,0:T(8,128)(2,1)S(1)} %bitcast.14, bf16[320,4096]{1,0:T(8,128)(2,1)S(1)} %get-tuple-element.19.low_ref, bf16[192,4096]{1,0:T(8,128)(2,1)} %get-tuple-element.20.high_in), custom_call_target="tpu_custom_call" | custom-call | tf_op jit(solution)/shard_map/potentials/pallas_call | solution.py:232
  40.5 8.4 %all-to-all-start.2 = ((bf16[8,64,256]{2,1,0:T(8,128)(2,1)}), bf16[8,64,256]{2,1,0:T(8,128)(2,1)S(1)}, u32[]{:S(2)}, u32[]{:S(2)}) async-start(bf16[8,64,256]{2,1,0:T(8,128)(2,1)} %potentials.1), calls=%async_computation.2 | async-start | bytes 524288 | tf_op jit(solution)/shard_map/all_to_all | solution.py:378
  48.9 1.6 %collective-permute-start.1 = (bf16[88,2048]{1,0:T(8,128)(2,1)S(1)}, bf16[88,2048]{1,0:T(8,128)(2,1)S(1)}, u32[]{:S(2)}, u32[]{:S(2)}) collective-permute-start(bf16[88,2048]{1,0:T(8,128)(2,1)S(1)} %get-tuple-element.21.own_in), channel_id=1, source_target_pairs={{8,0},{16,8},{24,16},{32,24},{40,32},{48,40},{56,48},{64,56},{72,6... | collective-permute-start | bytes 1081352 | tf_op jit(solution)/shard_map/ppermute | solution.py:408
  50.5 0.0 collective-permute-start
  50.5 8.4 %collective-permute-done.1.next_in = bf16[88,2048]{1,0:T(8,128)(2,1)S(1)} collective-permute-done((bf16[88,2048]{1,0:T(8,128)(2,1)S(1)}, bf16[88,2048]{1,0:T(8,128)(2,1)S(1)}, u32[]{:S(2)}, u32[]{:S(2)}) %collective-permute-start.1) | collective-permute-done | bytes 360480 | tf_op jit(solution)/shard_map/ppermute | solution.py:408
  59.0 3.1 %collective-permute-done.prev_in = bf16[88,2048]{1,0:T(8,128)(2,1)S(1)} collective-permute-done((bf16[88,2048]{1,0:T(8,128)(2,1)S(1)}, bf16[88,2048]{1,0:T(8,128)(2,1)S(1)}, u32[]{:S(2)}, u32[]{:S(2)}) %collective-permute-start) | collective-permute-done | bytes 360480 | tf_op jit(solution)/shard_map/ppermute | solution.py:407
  62.0 0.0 copy-done
  62.0 0.0 copy-done.1
  62.0 6.3 %pairs.1 = (f32[128,256]{1,0:T(8,128)S(1)}, bf16[64,256]{1,0:T(8,128)(2,1)S(1)}, f32[8,256]{1,0:T(8,128)S(1)}, bf16[128,64]{1,0:T(8,128)(2,1)S(1)}, bf16[64,128]{1,0:T(8,128)(2,1)S(1)}) custom-call(s32[2]{0:T(128)S(1)} %pad_add_fusion.place_ref, s32[1]{0:T(128)S(6)} %copy.13.count_ref, s32[16,27]{1,0:T(8,128)S(1)} %bitcast.15, s32[16,27]{1,0:T(8,128)S(1)} %bitcast.16, ...), custom_call_target="tpu_custom_call" | custom-call | flops 130940928 | bytes 1081344 | tf_op jit(solution)/shard_map/pairs/pallas_call | solution.py:319
  68.4 0.0 all-to-all-done.2.arrived_ref
  68.4 0.3 update.1
  68.7 18.4 %all_to_all.22 = bf16[8,64,256]{2,1,0:T(8,128)(2,1)S(1)} all-to-all(bf16[8,64,256]{2,1,0:T(8,128)(2,1)S(1)} %update.1), channel_id=1, replica_groups=mesh['atoms'=32,'waves'=8] {'waves'}, dimensions={0} | all-to-all | bytes 524288 | tf_op jit(solution)/shard_map/all_to_all | solution.py:378
  87.1 0.7 copy.12
Async XLA Ops:
  36.4 25.7 %copy-start = (s32[27,16]{0,1:T(8,128)S(1)}, s32[27,16]{0,1:T(8,128)}, u32[]{:S(2)}) copy-start(s32[27,16]{0,1:T(8,128)} %param.12) | copy-start | bytes 5188
  36.4 25.7 %copy-start.1 = (s32[27,16]{0,1:T(8,128)S(1)}, s32[27,16]{0,1:T(8,128)}, u32[]{:S(2)}) copy-start(s32[27,16]{0,1:T(8,128)} %param.13) | copy-start | bytes 5188
  40.5 27.8 %all-to-all-start.2 = ((bf16[8,64,256]{2,1,0:T(8,128)(2,1)}), bf16[8,64,256]{2,1,0:T(8,128)(2,1)S(1)}, u32[]{:S(2)}, u32[]{:S(2)}) async-start(bf16[8,64,256]{2,1,0:T(8,128)(2,1)} %potentials.1), calls=%async_computation.2 | async-start | bytes 524288 | tf_op jit(solution)/shard_map/all_to_all | solution.py:378
  48.9 10.0 %collective-permute-start.1 = (bf16[88,2048]{1,0:T(8,128)(2,1)S(1)}, bf16[88,2048]{1,0:T(8,128)(2,1)S(1)}, u32[]{:S(2)}, u32[]{:S(2)}) collective-permute-start(bf16[88,2048]{1,0:T(8,128)(2,1)S(1)} %get-tuple-element.21.own_in), channel_id=1, source_target_pairs={{8,0},{16,8},{24,16},{32,24},{40,32},{48,40},{56,48},{64,56},{72,6... | collective-permute-start | bytes 1081352 | tf_op jit(solution)/shard_map/ppermute | solution.py:408
  50.5 11.5 %collective-permute-start = (bf16[88,2048]{1,0:T(8,128)(2,1)S(1)}, bf16[88,2048]{1,0:T(8,128)(2,1)S(1)}, u32[]{:S(2)}, u32[]{:S(2)}) collective-permute-start(bf16[88,2048]{1,0:T(8,128)(2,1)S(1)} %get-tuple-element.21.own_in), channel_id=1, source_target_pairs={{0,8},{8,16},{16,24},{24,32},{32,40},{40,48},{48,56},{56,64},{64,7... | collective-permute-start | bytes 1081352 | tf_op jit(solution)/shard_map/ppermute | solution.py:407

commit v5 on v4

--- a/solution.py
+++ b/solution.py
@@ -14,7 +14,7 @@
 
 MSG_SCALE = 0.125
 GAIN_TOP = 20.0
-SIN_COEFS = (3.1415926401307073, -5.167710083507923, 2.5500775232148563, -0.5982912856211671, 0.07765766030589402)
+SIN_COEFS = (3.1415902702069918, -5.167406733272337, 2.5440105185033337, -0.5594624554679438)
 COS_COEFS = (0.9999999532476085, -4.934792830619664, 4.058411352862771, -1.3318765680813944, 0.21968961109803095)
 ROOT2 = math.sqrt(2.0)
 TILE = 256
@@ -30,7 +30,7 @@
 
 
 def kept_rows(waves):
-    return waves * 5 // 8
+    return waves * 3 // 4
 
 
 def horner(coefs, scale, u):
@@ -58,8 +58,8 @@
 
 def structure_kernel(
     scale, regions, place_ref, count_ref, kvec_in, coords_in, h_in, weight_in, mixing_in,
-    low_ref, high_out, out_ref, carry_ref, gain_ref, mixing_ref,
-    kvec_ref, coords_ref, h_ref, weight_ref, ka_ref, xs_ref, high_ref, in_sems, sems,
+    low_ref, high_out, out_ref, carry_out, gain_ref, mixing_ref,
+    kvec_ref, coords_ref, h_ref, weight_ref, ka_ref, masked_ref, high_ref, carry_ref, in_sems, sems,
 ):
     waves = kvec_ref.shape[1]
     chans, atoms = h_ref.shape
@@ -82,7 +82,8 @@
         copy.start()
     taken[0].wait()
     kf = kvec_ref[...].astype(jnp.float32)
-    ka = jnp.concatenate([kf, kf, kf, jnp.zeros((7, waves), jnp.float32)], axis=0)
+    ahead, behind = jnp.zeros((3, waves), jnp.float32), jnp.zeros((2, waves), jnp.float32)
+    ka = jnp.concatenate([part for axis in range(3) for part in (ahead, *(-kf[axis : axis + 1],) * 3, behind)], axis=0)
     ka_ref[...] = ka.T.astype(jnp.bfloat16)
     kx = kf[0:1] / regions
     gain = GAIN_TOP / (4.0 + kx * kx + kf[1:2] * kf[1:2] + kf[2:3] * kf[2:3])
@@ -91,46 +92,54 @@
     mine = jnp.sum(jnp.where(own, jnp.broadcast_to(gain, (owned, waves)), 0.0), axis=1, keepdims=True)
     gain_ref[...] = jnp.broadcast_to(mine * scale, gain_ref.shape)
     taken[1].wait()
-    first, second, third = three_pieces(coords_ref[...])
-    xs = jnp.concatenate([first, second, third, jnp.zeros((7, atoms), jnp.float32)], axis=0)
-    xs_ref[...] = xs.astype(jnp.bfloat16)
-    gap = jnp.zeros((5, atoms), jnp.float32)
-    spread = jnp.concatenate([first, gap, second, gap, third, gap], axis=0)
-    carry_ref[chans:, :] = spread.astype(jnp.bfloat16)
+    pieces = three_pieces(coords_ref[...])
+    ones, gap = jnp.ones((3, atoms), jnp.float32), jnp.zeros((2, atoms), jnp.float32)
+    for axis in range(3):
+        rows = jnp.concatenate([ones, *(-piece[axis : axis + 1] for piece in pieces), gap], axis=0)
+        carry_ref[chans + 8 * axis : chans + 8 * axis + 8, :] = rows.astype(jnp.bfloat16)
+    for copy in taken[2:]:
+        copy.wait()
     live_atoms = count_ref[0] * BLOCK
-    low_sum = jnp.zeros((kept, 2 * chans), jnp.float32)
-    high_sum = jnp.zeros((waves - kept, 2 * chans), jnp.float32)
+    atom = lax.broadcasted_iota(jnp.int32, (chans, atoms), 1)
+    masked_ref[...] = jnp.where(atom < live_atoms, h_ref[...].astype(jnp.float32), 0.0).astype(jnp.bfloat16)
+    zero = jnp.zeros((chans, TILE), jnp.bfloat16)
+    sums = {}
+
+    def add_up(place, at, row, start):
+        ht = masked_ref[:, start : start + TILE]
+        cosv = place[at : at + ROWS, start : start + TILE]
+        sinv = place[at : at + ROWS, atoms + start : atoms + start + TILE]
+        term = lax.dot_general(cosv, jnp.concatenate([ht, zero], axis=0), NT, **f32)
+        term = term + lax.dot_general(sinv, jnp.concatenate([zero, ht], axis=0), NT, **f32)
+        sums[row] = term if start == 0 else sums[row] + term
+        if start + TILE == atoms:
+            whole = sums.pop(row).astype(jnp.bfloat16)
+            out_ref[row // owned : (row + ROWS) // owned] = whole.reshape(ROWS // owned, owned, 2 * chans)
+
+    pending = []
     copies = []
-    for start in range(0, atoms, TILE):
-        cos_span = slice(start, start + TILE)
-        sin_span = slice(atoms + start, atoms + start + TILE)
-        xt = xs_ref[:, cos_span]
-        for row in range(0, waves, ROWS):
-            turns = jnp.dot(ka_ref[row : row + ROWS, :], xt, **f32)
+    for row in [*range(kept, waves, ROWS), *range(0, kept, ROWS)]:
+        place, at = (low_ref, row) if row < kept else (high_ref, row - kept)
+        if row == 0:
+            copies = [
+                pltpu.make_async_copy(high_ref, high_out, sems.at[0]),
+                pltpu.make_async_copy(carry_ref, carry_out, sems.at[1]),
+            ]
+            for copy in copies:
+                copy.start()
+        for start in range(0, atoms, TILE):
+            cos_span = slice(start, start + TILE)
+            sin_span = slice(atoms + start, atoms + start + TILE)
+            turns = jnp.dot(ka_ref[row : row + ROWS, :], carry_ref[chans:, cos_span], **f32)
             cosv, sinv = phases_of(turns)
-            place, at = (low_ref, row) if row < kept else (high_ref, row - kept)
             place[at : at + ROWS, cos_span] = cosv.astype(jnp.bfloat16)
             place[at : at + ROWS, sin_span] = sinv.astype(jnp.bfloat16)
-        for half in range(2):
-            span = pl.ds(half * atoms + start, TILE)
-            copy = pltpu.make_async_copy(high_ref.at[:, span], high_out.at[:, span], sems.at[half, start // TILE])
-            copy.start()
-            copies.append(copy)
-        if start == 0:
-            for copy in taken[2:]:
-                copy.wait()
-        carry_ref[:chans, cos_span] = jnp.dot(weight_ref[...], h_ref[:, cos_span], **f32).astype(jnp.bfloat16)
-        atom = lax.broadcasted_iota(jnp.int32, (chans, TILE), 1) + start
-        ht = jnp.where(atom < live_atoms, h_ref[:, cos_span].astype(jnp.float32), 0.0)
-        zero = jnp.zeros_like(ht)
-        hc = jnp.concatenate([ht, zero], axis=0).astype(jnp.bfloat16)
-        hs = jnp.concatenate([zero, ht], axis=0).astype(jnp.bfloat16)
-        low_sum = low_sum + lax.dot_general(low_ref[:, cos_span], hc, NT, **f32)
-        low_sum = low_sum + lax.dot_general(low_ref[:, sin_span], hs, NT, **f32)
-        high_sum = high_sum + lax.dot_general(high_ref[:, cos_span], hc, NT, **f32)
-        high_sum = high_sum + lax.dot_general(high_ref[:, sin_span], hs, NT, **f32)
-    out_ref[: kept // owned] = low_sum.astype(jnp.bfloat16).reshape(kept // owned, owned, 2 * chans)
-    out_ref[kept // owned :] = high_sum.astype(jnp.bfloat16).reshape(-1, owned, 2 * chans)
+            if row == kept:
+                carry_ref[:chans, cos_span] = jnp.dot(weight_ref[...], h_ref[:, cos_span], **f32).astype(jnp.bfloat16)
+            pending.append((place, at, row, start))
+            if len(pending) > 1:
+                add_up(*pending.pop(0))
+    add_up(*pending.pop(0))
     for copy in copies:
         copy.wait()
 
@@ -149,22 +158,23 @@
             jax.ShapeDtypeStruct((kept, 2 * atoms), jnp.bfloat16),
             pltpu.HBM((waves - kept, 2 * atoms), jnp.bfloat16),
             jax.ShapeDtypeStruct((regions, owned, 2 * chans), jnp.bfloat16),
-            jax.ShapeDtypeStruct((chans + 24, atoms), jnp.bfloat16),
+            pltpu.HBM((chans + 24, atoms), jnp.bfloat16),
             jax.ShapeDtypeStruct((owned, 2 * chans), jnp.float32),
             jax.ShapeDtypeStruct(mixing.shape, jnp.float32),
         ),
         in_specs=[SMEM_SPEC] * 2 + [HBM_SPEC] * 5,
-        out_specs=(VMEM_SPEC, HBM_SPEC) + (VMEM_SPEC,) * 4,
+        out_specs=(VMEM_SPEC, HBM_SPEC, VMEM_SPEC, HBM_SPEC, VMEM_SPEC, VMEM_SPEC),
         scratch_shapes=[
             pltpu.VMEM(kvec.shape, jnp.int32),
             pltpu.VMEM(coords.shape, jnp.float32),
             pltpu.VMEM(h.shape, jnp.bfloat16),
             pltpu.VMEM(weight.shape, jnp.bfloat16),
-            pltpu.VMEM((waves, 16), jnp.bfloat16),
-            pltpu.VMEM((16, atoms), jnp.bfloat16),
+            pltpu.VMEM((waves, 24), jnp.bfloat16),
+            pltpu.VMEM(h.shape, jnp.bfloat16),
             pltpu.VMEM((waves - kept, 2 * atoms), jnp.bfloat16),
+            pltpu.VMEM((chans + 24, atoms), jnp.bfloat16),
             pltpu.SemaphoreType.DMA((5,)),
-            pltpu.SemaphoreType.DMA((2, atoms // TILE)),
+            pltpu.SemaphoreType.DMA((2,)),
         ],
         compiler_params=PARAMS,
         name="structure",
@@ -196,33 +206,28 @@
     )(arrived, gain, mixing)
 
 
-def potentials_kernel(filtered_ref, low_ref, high_in, out_ref, high_ref, sum_ref, sems):
+def potentials_kernel(filtered_ref, low_ref, high_in, out_ref, high_ref, across_ref, sum_ref, sem):
     chans = out_ref.shape[1]
     pieces, _, width = out_ref.shape
     atoms = pieces * width
-    kept = low_ref.shape[0]
-    copies = []
-    for piece in range(pieces):
-        for half in range(2):
-            span = pl.ds(half * atoms + piece * width, width)
-            copy = pltpu.make_async_copy(high_in.at[:, span], high_ref.at[:, span], sems.at[half, piece])
-            copy.start()
-            copies.append(copy)
+    kept, waves = low_ref.shape[0], filtered_ref.shape[0]
+    copy = pltpu.make_async_copy(high_in, high_ref, sem)
+    copy.start()
+    across_ref[...] = filtered_ref[...].astype(jnp.float32).T.astype(jnp.bfloat16)
 
     def term(rows, table, piece):
         cos_span = slice(piece * width, (piece + 1) * width)
         sin_span = slice(atoms + piece * width, atoms + (piece + 1) * width)
         f32 = dict(preferred_element_type=jnp.float32)
-        return lax.dot_general(filtered_ref[rows, :chans], table[:, cos_span], TN, **f32) + lax.dot_general(
-            filtered_ref[rows, chans:], table[:, sin_span], TN, **f32
+        return jnp.dot(across_ref[:chans, rows], table[:, cos_span], **f32) + jnp.dot(
+            across_ref[chans:, rows], table[:, sin_span], **f32
         )
 
     for piece in range(pieces):
         sum_ref[piece] = term(slice(0, kept), low_ref, piece)
+    copy.wait()
     for piece in range(pieces):
-        copies[2 * piece].wait()
-        copies[2 * piece + 1].wait()
-        whole = sum_ref[piece] + term(slice(kept, filtered_ref.shape[0]), high_ref, piece)
+        whole = sum_ref[piece] + term(slice(kept, waves), high_ref, piece)
         out_ref[piece] = (whole * (1.0 / math.sqrt(K))).astype(jnp.bfloat16)
 
 
@@ -236,8 +241,9 @@
         out_specs=VMEM_SPEC,
         scratch_shapes=[
             pltpu.VMEM(high.shape, jnp.bfloat16),
+            pltpu.VMEM((2 * chans, filtered.shape[0]), jnp.bfloat16),
             pltpu.VMEM((pieces, chans, atoms // pieces), jnp.float32),
-            pltpu.SemaphoreType.DMA((2, pieces)),
+            pltpu.SemaphoreType.DMA,
         ],
         compiler_params=PARAMS,
         name="potentials",
@@ -245,9 +251,9 @@
 
 
 def pairs_kernel(
-    scale_x, regions, place_ref, count_ref, idx_ref, live_ref, prev_in, own_in, next_in, h_in, first_in, second_in,
+    scale_x, regions, unroll, place_ref, count_ref, idx_ref, live_ref, prev_in, next_in, own_in, h_in, first_in, second_in,
     inner_ref, share_ref, alive_ref, third_ref, second_ref,
-    ext_ref, first_ref, pos_ref, own_ref, weights_ref, near_ref, sems,
+    ext_ref, first_ref, own_ref, pos_ref, weights_ref, near_ref, sum_ref, sems,
 ):
     chans = h_in.shape[0]
     width = own_in.shape[1]
@@ -266,45 +272,65 @@
     alive_ref[...] = jnp.where(atom < count_ref[0] * BLOCK, 1.0, 0.0)
     for copy in copies:
         copy.wait()
-    pieces = [ext_ref[chans + 8 * at : chans + 8 * at + 8, :].astype(jnp.float32) for at in range(3)]
-    pos_ref[...] = (pieces[2] + pieces[1]) + pieces[0]
+    f32 = dict(preferred_element_type=jnp.float32)
+    column = lax.broadcasted_iota(jnp.int32, (8, 8), 1)
+    pick = jnp.where((column >= 3) & (column < 6), 1.0, 0.0).astype(jnp.bfloat16)
+    row = lax.broadcasted_iota(jnp.int32, (8, BLOCK), 0)
+    lead = jnp.where(row < 3, 1.0, 0.0).astype(jnp.bfloat16)
+    for axis in range(3):
+        rows = slice(chans + 8 * axis, chans + 8 * axis + 8)
+        for start in range(0, 3 * width, 4 * BLOCK):
+            span = slice(start, start + 4 * BLOCK)
+            pos_ref[axis, :, span] = jnp.dot(pick, ext_ref[rows, span], **f32)
     for block in range(count):
         at = pl.multiple_of((nblocks + first + block) * BLOCK, BLOCK)
-        columns = pos_ref[:, pl.ds(at, BLOCK)].T
         for axis in range(3):
-            own_ref[block, axis] = jnp.broadcast_to(columns[:, axis : axis + 1], (BLOCK, BLOCK))
+            rows = ext_ref[chans + 8 * axis : chans + 8 * axis + 8, pl.ds(at, BLOCK)].astype(jnp.float32)
+            swapped = jnp.concatenate([-rows[3:6], rows[0:3], rows[6:8]], axis=0)
+            own_ref[block, axis] = jnp.dot(swapped.T.astype(jnp.bfloat16), lead, **f32)
+        sum_ref[block] = jnp.zeros((chans, BLOCK), jnp.float32)
+        weights_ref[block] = jnp.zeros(weights_ref.shape[1:], jnp.bfloat16)
+        near_ref[block] = jnp.zeros(near_ref.shape[1:], jnp.bfloat16)
     exponent = -2.0 * math.log2(math.e)
-
-    def slot_step(slot, carried):
+    part_rows = 16
+
+    def add_up(block):
+        sum_ref[block] += lax.dot_general(near_ref[block], weights_ref[block], NT, **f32)
+
+    def slots_step(step, carried):
         for block in range(count):
-            entry = idx_ref[first + block, slot]
-            offset = lax.rem(entry // nblocks - here + regions + 1, regions)
-            at = pl.multiple_of((offset * nblocks + lax.rem(entry, nblocks)) * BLOCK, BLOCK)
-            used = live_ref[first + block, slot].astype(jnp.float32)
-            near = pos_ref[:, pl.ds(at, BLOCK)]
-            total = None
-            for axis in range(3):
-                diff = own_ref[block, axis] - near[axis : axis + 1, :]
-                diff = diff - jnp.round(diff)
-                term = diff * diff
-                if axis == 0:
-                    term = term * (scale_x * scale_x)
-                total = term if total is None else total + term
-            pair = jnp.exp2(total * exponent).astype(jnp.bfloat16)
-            to = pl.multiple_of(slot * BLOCK, BLOCK)
-            weights_ref[block, :, pl.ds(to, BLOCK)] = pair
-            mapped = ext_ref[:chans, pl.ds(at, BLOCK)].astype(jnp.float32) * used
-            near_ref[block, :, pl.ds(to, BLOCK)] = mapped.astype(jnp.bfloat16)
+            add_up(block)
+        for block in range(count):
+            for part in range(unroll):
+                slot = step * unroll + part
+                entry = idx_ref[first + block, slot]
+                where = jnp.bitwise_and(entry + (regions + 1 - here) * nblocks, regions * nblocks - 1)
+                span = pl.ds(pl.multiple_of(where * BLOCK, BLOCK), BLOCK)
+                to = slice(part * BLOCK, (part + 1) * BLOCK)
+                used = live_ref[first + block, slot].astype(jnp.float32)
+                mapped = ext_ref[:chans, span].astype(jnp.float32) * used
+                near_ref[block, :, to] = mapped.astype(jnp.bfloat16)
+                minus = [jnp.tile(pos_ref[axis, :, span], (part_rows // 8, 1)) for axis in range(3)]
+                for start in range(0, BLOCK, part_rows):
+                    rows = slice(start, start + part_rows)
+                    total = None
+                    for axis in range(3):
+                        diff = own_ref[block, axis, rows, :] + minus[axis]
+                        diff = diff - jnp.round(diff)
+                        term = diff * diff
+                        if axis == 0:
+                            term = term * (scale_x * scale_x)
+                        total = term if total is None else total + term
+                    weights_ref[block, rows, to] = jnp.exp2(total * exponent).astype(jnp.bfloat16)
         return carried
 
-    lax.fori_loop(0, slots, slot_step, 0)
-    f32 = dict(preferred_element_type=jnp.float32)
+    lax.fori_loop(0, slots // unroll, slots_step, 0)
     outer = first_ref[: 2 * chans, :]
     third_ref[...] = first_ref[2 * chans :, :].astype(jnp.float32).T.astype(jnp.bfloat16)
     for block in range(count):
+        add_up(block)
         span = slice(block * BLOCK, (block + 1) * BLOCK)
-        msg = lax.dot_general(near_ref[block], weights_ref[block], NT, **f32)
-        msg = (msg * MSG_SCALE).astype(jnp.bfloat16)
+        msg = (sum_ref[block] * MSG_SCALE).astype(jnp.bfloat16)
         known = jnp.concatenate([share_ref[:, span], msg], axis=0)
         inner_ref[:, span] = lax.dot_general(outer, known, TN, **f32)
 
@@ -316,8 +342,9 @@
     slots = neighbours.shape[1]
     share = count * BLOCK
     work = slots * share * BLOCK
+    unroll = 3 if slots % 3 == 0 else 1
     return pl.pallas_call(
-        functools.partial(pairs_kernel, float(regions), regions),
+        functools.partial(pairs_kernel, float(regions), regions, unroll),
         out_shape=(
             jax.ShapeDtypeStruct((hidden, share), jnp.float32),
             jax.ShapeDtypeStruct((chans, share), jnp.bfloat16),
@@ -325,15 +352,16 @@
             jax.ShapeDtypeStruct((hidden, chans), jnp.bfloat16),
             jax.ShapeDtypeStruct(second.shape, jnp.bfloat16),
         ),
-        in_specs=[SMEM_SPEC] * 4 + [ANY_SPEC] * 3 + [HBM_SPEC] * 3,
+        in_specs=[SMEM_SPEC] * 4 + [ANY_SPEC] * 2 + [HBM_SPEC] * 4,
         out_specs=(VMEM_SPEC,) * 5,
         scratch_shapes=[
             pltpu.VMEM((rows, 3 * width), jnp.bfloat16),
             pltpu.VMEM(first.shape, jnp.bfloat16),
-            pltpu.VMEM((8, 3 * width), jnp.float32),
             pltpu.VMEM((count, 3, BLOCK, BLOCK), jnp.float32),
-            pltpu.VMEM((count, BLOCK, slots * BLOCK), jnp.bfloat16),
-            pltpu.VMEM((count, chans, slots * BLOCK), jnp.bfloat16),
+            pltpu.VMEM((3, 8, 3 * width), jnp.float32),
+            pltpu.VMEM((count, BLOCK, unroll * BLOCK), jnp.bfloat16),
+            pltpu.VMEM((count, chans, unroll * BLOCK), jnp.bfloat16),
+            pltpu.VMEM((count, chans, BLOCK), jnp.float32),
             pltpu.SemaphoreType.DMA((6,)),
         ],
         compiler_params=PARAMS,
@@ -341,7 +369,7 @@
             flops=work * (2 * chans + 20), bytes_accessed=6 * rows * width, transcendentals=work
         ),
         name="pairs",
-    )(place, live_blocks, neighbours, live_slots, prev, own, following, *in_hbm(h, first, second))
+    )(place, live_blocks, neighbours, live_slots, prev, following, *in_hbm(own, h, first, second))
 
 
 def update_kernel(arrived_ref, inner_ref, share_ref, alive_ref, third_ref, second_ref, out_ref):

time: 89.2 us -> 86.7 us (0.972)
  Pallas kernels: 18.5 us -> 15.8 us
    pallas_call x1, Pallas kernels: 4.16 us -> 2.25 us  [potentials(): pl.pallas_call(potentials_kernel, out_shape=jax.ShapeDtypeStruct((pieces,...]
where the time goes in v5:
time: 86.7 us; the launch traced here: 85.3 us
  blocking collectives  46.4 us (54%)
  Pallas kernels  15.8 us (18%)
  waiting for transfers between devices  11.4 us (13%)
  starting transfers between devices  10.1 us (12%)
    all_to_all x3, blocking collectives, from_others(): return lax.all_to_all(pieces, axis, 0, 0, tiled=True)  46.4 us
    all_to_all x1, starting transfers between devices, from_others(): return lax.all_to_all(pieces, axis, 0, 0, tiled=True)  8.41 us
    ppermute x1, waiting for transfers between devices, local(): lax.ppermute(carry, 'atoms', [((i + 1) % regions, i) for i in range(regio...  8.33 us
    pallas_call x1, Pallas kernels, structure(): pl.pallas_call(functools.partial(structure_kernel, scale, float(regions))...  6.75 us
    pallas_call x1, Pallas kernels, pairs(): pl.pallas_call(functools.partial(pairs_kernel, float(regions), regions, u...  6.15 us
    ppermute x1, waiting for transfers between devices, local(): lax.ppermute(carry, 'atoms', [(i, (i + 1) % regions) for i in range(regio...  3.07 us
    pallas_call x1, Pallas kernels, potentials(): pl.pallas_call(potentials_kernel, out_shape=jax.ShapeDtypeStruct((pieces,...  2.25 us
  transfers between devices with their start and end apart: 3, of which 2 were waited for; matrix products, arithmetic and copies ran while one was open for 0% of the time, Pallas kernels for 7%

profile of v5, /device:TPU:32, one launch (start us, length us, event | category | flops | bytes accessed | tf_op | source)
XLA Modules:
  0.0 85.3 jit_solution(8473155606551879496)
XLA Ops:
  0.7 0.1 pad_add_fusion.place_ref
  0.7 0.0 copy-start
  0.7 0.0 copy-start.1
  0.7 6.7 %structure.1 = (bf16[384,4096]{1,0:T(8,128)(2,1)S(1)}, bf16[128,4096]{1,0:T(8,128)(2,1)}, bf16[32,16,128]{2,1,0:T(8,128)(2,1)S(1)}, bf16[88,2048]{1,0:T(8,128)(2...) custom-call(s32[2]{0:T(128)S(1)} %pad_add_fusion.place_ref, s32[1]{0:T(128)S(6)} %copy.13.count_ref, s32[3,512]{1,0:T(4,128)} %kvec_in.1, ...), custom_call_target="tpu_custom_call" | custom-call | tf_op jit(solution)/shard_map/structure/pallas_call | solution.py:155
  7.5 0.0 copy-start.2
  7.5 16.0 %all_to_all.20.arrived_ref = bf16[32,16,128]{2,1,0:T(8,128)(2,1)S(1)} all-to-all(bf16[32,16,128]{2,1,0:T(8,128)(2,1)S(1)} %get-tuple-element.16), channel_id=1, replica_groups=mesh['atoms'=32,'waves'=8] {'atoms'}, dimensions={0} | all-to-all | bytes 262144 | tf_op jit(solution)/shard_map/all_to_all | solution.py:406
  23.5 0.3 spectral.1
  23.8 12.1 %all_to_all.21 = bf16[32,16,128]{2,1,0:T(8,128)(2,1)S(1)} all-to-all(bf16[32,16,128]{2,1,0:T(8,128)(2,1)S(1)} %spectral.1), channel_id=1, replica_groups=mesh['atoms'=32,'waves'=8] {'atoms'}, dimensions={0} | all-to-all | bytes 262144 | tf_op jit(solution)/shard_map/all_to_all | solution.py:406
  35.9 2.2 %potentials.1 = bf16[8,64,256]{2,1,0:T(8,128)(2,1)} custom-call(bf16[512,128]{1,0:T(8,128)(2,1)S(1)} %bitcast.14, bf16[384,4096]{1,0:T(8,128)(2,1)S(1)} %get-tuple-element.19.low_ref, bf16[128,4096]{1,0:T(8,128)(2,1)} %get-tuple-element.20.high_in), custom_call_target="tpu_custom_call" | custom-call | tf_op jit(solution)/shard_map/potentials/pallas_call | solution.py:237
  38.2 8.4 %all-to-all-start.2 = ((bf16[8,64,256]{2,1,0:T(8,128)(2,1)}), bf16[8,64,256]{2,1,0:T(8,128)(2,1)S(1)}, u32[]{:S(2)}, u32[]{:S(2)}) async-start(bf16[8,64,256]{2,1,0:T(8,128)(2,1)} %potentials.1), calls=%async_computation.2 | async-start | bytes 524288 | tf_op jit(solution)/shard_map/all_to_all | solution.py:406
  46.6 0.0 copy-done.2
  46.6 1.7 %collective-permute-start.1 = (bf16[88,2048]{1,0:T(8,128)(2,1)S(1)}, bf16[88,2048]{1,0:T(8,128)(2,1)S(1)}, u32[]{:S(2)}, u32[]{:S(2)}) collective-permute-start(bf16[88,2048]{1,0:T(8,128)(2,1)S(1)} %copy-done.2), channel_id=1, source_target_pairs={{8,0},{16,8},{24,16},{32,24},{40,32},{48,40},{56,48},{64,56},{72,6... | collective-permute-start | bytes 1081352 | tf_op jit(solution)/shard_map/ppermute | solution.py:436
  48.3 0.0 collective-permute-start
  48.3 8.3 %collective-permute-done.1.next_in = bf16[88,2048]{1,0:T(8,128)(2,1)S(1)} collective-permute-done((bf16[88,2048]{1,0:T(8,128)(2,1)S(1)}, bf16[88,2048]{1,0:T(8,128)(2,1)S(1)}, u32[]{:S(2)}, u32[]{:S(2)}) %collective-permute-start.1) | collective-permute-done | bytes 360480 | tf_op jit(solution)/shard_map/ppermute | solution.py:436
  56.6 3.1 %collective-permute-done.prev_in = bf16[88,2048]{1,0:T(8,128)(2,1)S(1)} collective-permute-done((bf16[88,2048]{1,0:T(8,128)(2,1)S(1)}, bf16[88,2048]{1,0:T(8,128)(2,1)S(1)}, u32[]{:S(2)}, u32[]{:S(2)}) %collective-permute-start) | collective-permute-done | bytes 360480 | tf_op jit(solution)/shard_map/ppermute | solution.py:435
  59.7 0.0 copy-done
  59.7 0.0 copy-done.1
  59.7 6.2 %pairs.1 = (f32[128,256]{1,0:T(8,128)S(1)}, bf16[64,256]{1,0:T(8,128)(2,1)S(1)}, f32[8,256]{1,0:T(8,128)S(1)}, bf16[128,64]{1,0:T(8,128)(2,1)S(1)}, bf16[64,128]{1,0:T(8,128)(2,1)S(1)}) custom-call(s32[2]{0:T(128)S(1)} %pad_add_fusion.place_ref, s32[1]{0:T(128)S(6)} %copy.13.count_ref, s32[16,27]{1,0:T(8,128)S(1)} %bitcast.15, s32[16,27]{1,0:T(8,128)S(1)} %bitcast.16, ...), custom_call_target="tpu_custom_call" | custom-call | flops 130940928 | bytes 1081344 | tf_op jit(solution)/shard_map/pairs/pallas_call | solution.py:346
  65.9 0.0 all-to-all-done.2.arrived_ref
  65.9 0.3 update.1
  66.2 18.4 %all_to_all.22 = bf16[8,64,256]{2,1,0:T(8,128)(2,1)S(1)} all-to-all(bf16[8,64,256]{2,1,0:T(8,128)(2,1)S(1)} %update.1), channel_id=1, replica_groups=mesh['atoms'=32,'waves'=8] {'waves'}, dimensions={0} | all-to-all | bytes 524288 | tf_op jit(solution)/shard_map/all_to_all | solution.py:406
  84.6 0.7 copy.12
Async XLA Ops:
  0.7 59.0 %copy-start = (s32[27,16]{0,1:T(8,128)S(1)}, s32[27,16]{0,1:T(8,128)}, u32[]{:S(2)}) copy-start(s32[27,16]{0,1:T(8,128)} %param.12) | copy-start | bytes 5188
  0.7 59.0 %copy-start.1 = (s32[27,16]{0,1:T(8,128)S(1)}, s32[27,16]{0,1:T(8,128)}, u32[]{:S(2)}) copy-start(s32[27,16]{0,1:T(8,128)} %param.13) | copy-start | bytes 5188
  7.5 39.1 %copy-start.2 = (bf16[88,2048]{1,0:T(8,128)(2,1)S(1)}, bf16[88,2048]{1,0:T(8,128)(2,1)}, u32[]{:S(2)}) copy-start(bf16[88,2048]{1,0:T(8,128)(2,1)} %get-tuple-element.21.own_in) | copy-start | bytes 1081348
  38.2 27.7 %all-to-all-start.2 = ((bf16[8,64,256]{2,1,0:T(8,128)(2,1)}), bf16[8,64,256]{2,1,0:T(8,128)(2,1)S(1)}, u32[]{:S(2)}, u32[]{:S(2)}) async-start(bf16[8,64,256]{2,1,0:T(8,128)(2,1)} %potentials.1), calls=%async_computation.2 | async-start | bytes 524288 | tf_op jit(solution)/shard_map/all_to_all | solution.py:406
  46.6 10.0 %collective-permute-start.1 = (bf16[88,2048]{1,0:T(8,128)(2,1)S(1)}, bf16[88,2048]{1,0:T(8,128)(2,1)S(1)}, u32[]{:S(2)}, u32[]{:S(2)}) collective-permute-start(bf16[88,2048]{1,0:T(8,128)(2,1)S(1)} %copy-done.2), channel_id=1, source_target_pairs={{8,0},{16,8},{24,16},{32,24},{40,32},{48,40},{56,48},{64,56},{72,6... | collective-permute-start | bytes 1081352 | tf_op jit(solution)/shard_map/ppermute | solution.py:436
  48.3 11.4 %collective-permute-start = (bf16[88,2048]{1,0:T(8,128)(2,1)S(1)}, bf16[88,2048]{1,0:T(8,128)(2,1)S(1)}, u32[]{:S(2)}, u32[]{:S(2)}) collective-permute-start(bf16[88,2048]{1,0:T(8,128)(2,1)S(1)} %copy-done.2), channel_id=1, source_target_pairs={{0,8},{8,16},{16,24},{24,32},{32,40},{40,48},{48,56},{56,64},{64,7... | collective-permute-start | bytes 1081352 | tf_op jit(solution)/shard_map/ppermute | solution.py:435

commit v6 on v5

--- a/solution.py
+++ b/solution.py
@@ -14,11 +14,10 @@
 
 MSG_SCALE = 0.125
 GAIN_TOP = 20.0
-SIN_COEFS = (3.1415902702069918, -5.167406733272337, 2.5440105185033337, -0.5594624554679438)
-COS_COEFS = (0.9999999532476085, -4.934792830619664, 4.058411352862771, -1.3318765680813944, 0.21968961109803095)
-ROOT2 = math.sqrt(2.0)
+ALPHA = 8.0**0.25
+SIN_COEFS = tuple(ALPHA / math.sqrt(2.0) * c for c in (2.221430356581745, -0.9131746556274619, 0.10983828651966959))
 TILE = 256
-ROWS = 64
+ROWS = 128
 LIMIT = 16 * 2**20
 VMEM_SPEC = pl.BlockSpec(memory_space=pltpu.VMEM)
 SMEM_SPEC = pl.BlockSpec(memory_space=pltpu.SMEM)
@@ -33,19 +32,13 @@
     return waves * 3 // 4
 
 
-def horner(coefs, scale, u):
-    value = coefs[-1] * scale
-    for coef in coefs[-2::-1]:
-        value = value * u + coef * scale
-    return value
-
-
 def phases_of(turns):
     r = turns - jnp.round(turns)
     u = r * r
-    s = r * horner(SIN_COEFS, ROOT2, u)
-    c = horner(COS_COEFS, ROOT2, u)
-    return 1.0 - s * s, s * c
+    s = r * ((SIN_COEFS[2] * u + SIN_COEFS[1]) * u + SIN_COEFS[0])
+    q = s * s
+    w = math.sqrt(8.0) - q
+    return 1.0 - q * w, (s * (w * lax.rsqrt(w))) * (math.sqrt(2.0) - q)
 
 
 def three_pieces(values):
@@ -263,14 +256,17 @@
     here = place_ref[0]
     first = place_ref[1]
     share = pl.ds(pl.multiple_of(first * BLOCK, BLOCK), count * BLOCK)
-    moves = [(source, ext_ref.at[:, pl.ds(at * width, width)]) for at, source in enumerate((prev_in, own_in, next_in))]
+    moves = []
+    for rows in (pl.ds(chans, ext_ref.shape[0] - chans), pl.ds(0, chans)):
+        for at, source in enumerate((prev_in, own_in, next_in)):
+            moves.append((source.at[rows, :], ext_ref.at[rows, pl.ds(at * width, width)]))
     moves += [(h_in.at[:, share], share_ref), (first_in, first_ref), (second_in, second_ref)]
     copies = [pltpu.make_async_copy(source, target, sems.at[at]) for at, (source, target) in enumerate(moves)]
     for copy in copies:
         copy.start()
     atom = lax.broadcasted_iota(jnp.int32, alive_ref.shape, 1) + first * BLOCK
     alive_ref[...] = jnp.where(atom < count_ref[0] * BLOCK, 1.0, 0.0)
-    for copy in copies:
+    for copy in copies[:3]:
         copy.wait()
     f32 = dict(preferred_element_type=jnp.float32)
     column = lax.broadcasted_iota(jnp.int32, (8, 8), 1)
@@ -291,6 +287,8 @@
         sum_ref[block] = jnp.zeros((chans, BLOCK), jnp.float32)
         weights_ref[block] = jnp.zeros(weights_ref.shape[1:], jnp.bfloat16)
         near_ref[block] = jnp.zeros(near_ref.shape[1:], jnp.bfloat16)
+    for copy in copies[3:6]:
+        copy.wait()
     exponent = -2.0 * math.log2(math.e)
     part_rows = 16
 
@@ -325,6 +323,8 @@
         return carried
 
     lax.fori_loop(0, slots // unroll, slots_step, 0)
+    for copy in copies[6:]:
+        copy.wait()
     outer = first_ref[: 2 * chans, :]
     third_ref[...] = first_ref[2 * chans :, :].astype(jnp.float32).T.astype(jnp.bfloat16)
     for block in range(count):
@@ -362,7 +362,7 @@
             pltpu.VMEM((count, BLOCK, unroll * BLOCK), jnp.bfloat16),
             pltpu.VMEM((count, chans, unroll * BLOCK), jnp.bfloat16),
             pltpu.VMEM((count, chans, BLOCK), jnp.float32),
-            pltpu.SemaphoreType.DMA((6,)),
+            pltpu.SemaphoreType.DMA((9,)),
         ],
         compiler_params=PARAMS,
         cost_estimate=pl.CostEstimate(

time: 86.7 us -> 85.9 us (level)
  no operation moved by 1% of the time
where the time goes in v6:
time: 85.9 us; the launch traced here: 84.5 us
  blocking collectives  46.4 us (54%)
  Pallas kernels  15 us (17%)
  waiting for transfers between devices  11.4 us (13%)
  starting transfers between devices  10.1 us (12%)
    all_to_all x3, blocking collectives, from_others(): return lax.all_to_all(pieces, axis, 0, 0, tiled=True)  46.4 us
    all_to_all x1, starting transfers between devices, from_others(): return lax.all_to_all(pieces, axis, 0, 0, tiled=True)  8.41 us
    ppermute x1, waiting for transfers between devices, local(): lax.ppermute(carry, 'atoms', [((i + 1) % regions, i) for i in range(regio...  8.33 us
    pallas_call x1, Pallas kernels, pairs(): pl.pallas_call(functools.partial(pairs_kernel, float(regions), regions, u...  6.12 us
    pallas_call x1, Pallas kernels, structure(): pl.pallas_call(functools.partial(structure_kernel, scale, float(regions))...  5.98 us
    ppermute x1, waiting for transfers between devices, local(): lax.ppermute(carry, 'atoms', [(i, (i + 1) % regions) for i in range(regio...  3.07 us
    pallas_call x1, Pallas kernels, potentials(): pl.pallas_call(potentials_kernel, out_shape=jax.ShapeDtypeStruct((pieces,...  2.25 us
  transfers between devices with their start and end apart: 3, of which 2 were waited for; matrix products, arithmetic and copies ran while one was open for 0% of the time, Pallas kernels for 7%

profile of v6, /device:TPU:32, one launch (start us, length us, event | category | flops | bytes accessed | tf_op | source)
XLA Modules:
  0.0 84.5 jit_solution(3506845372736083860)
XLA Ops:
  0.7 0.1 pad_add_fusion.place_ref
  0.7 0.0 copy-start
  0.7 0.0 copy-start.1
  0.7 6.0 %structure.1 = (bf16[384,4096]{1,0:T(8,128)(2,1)S(1)}, bf16[128,4096]{1,0:T(8,128)(2,1)}, bf16[32,16,128]{2,1,0:T(8,128)(2,1)S(1)}, bf16[88,2048]{1,0:T(8,128)(2...) custom-call(s32[2]{0:T(128)S(1)} %pad_add_fusion.place_ref, s32[1]{0:T(128)S(6)} %copy.13.count_ref, s32[3,512]{1,0:T(4,128)} %kvec_in.1, ...), custom_call_target="tpu_custom_call" | custom-call | tf_op jit(solution)/shard_map/structure/pallas_call | solution.py:148
  6.7 0.0 copy-start.2
  6.7 16.0 %all_to_all.20.arrived_ref = bf16[32,16,128]{2,1,0:T(8,128)(2,1)S(1)} all-to-all(bf16[32,16,128]{2,1,0:T(8,128)(2,1)S(1)} %get-tuple-element.16), channel_id=1, replica_groups=mesh['atoms'=32,'waves'=8] {'atoms'}, dimensions={0} | all-to-all | bytes 262144 | tf_op jit(solution)/shard_map/all_to_all | solution.py:406
  22.7 0.3 spectral.1
  23.1 12.1 %all_to_all.21 = bf16[32,16,128]{2,1,0:T(8,128)(2,1)S(1)} all-to-all(bf16[32,16,128]{2,1,0:T(8,128)(2,1)S(1)} %spectral.1), channel_id=1, replica_groups=mesh['atoms'=32,'waves'=8] {'atoms'}, dimensions={0} | all-to-all | bytes 262144 | tf_op jit(solution)/shard_map/all_to_all | solution.py:406
  35.2 2.2 %potentials.1 = bf16[8,64,256]{2,1,0:T(8,128)(2,1)} custom-call(bf16[512,128]{1,0:T(8,128)(2,1)S(1)} %bitcast.14, bf16[384,4096]{1,0:T(8,128)(2,1)S(1)} %get-tuple-element.19.low_ref, bf16[128,4096]{1,0:T(8,128)(2,1)} %get-tuple-element.20.high_in), custom_call_target="tpu_custom_call" | custom-call | tf_op jit(solution)/shard_map/potentials/pallas_call | solution.py:230
  37.4 8.4 %all-to-all-start.2 = ((bf16[8,64,256]{2,1,0:T(8,128)(2,1)}), bf16[8,64,256]{2,1,0:T(8,128)(2,1)S(1)}, u32[]{:S(2)}, u32[]{:S(2)}) async-start(bf16[8,64,256]{2,1,0:T(8,128)(2,1)} %potentials.1), calls=%async_computation.2 | async-start | bytes 524288 | tf_op jit(solution)/shard_map/all_to_all | solution.py:406
  45.8 0.0 copy-done.2
  45.8 1.7 %collective-permute-start.1 = (bf16[88,2048]{1,0:T(8,128)(2,1)S(1)}, bf16[88,2048]{1,0:T(8,128)(2,1)S(1)}, u32[]{:S(2)}, u32[]{:S(2)}) collective-permute-start(bf16[88,2048]{1,0:T(8,128)(2,1)S(1)} %copy-done.2), channel_id=1, source_target_pairs={{8,0},{16,8},{24,16},{32,24},{40,32},{48,40},{56,48},{64,56},{72,6... | collective-permute-start | bytes 1081352 | tf_op jit(solution)/shard_map/ppermute | solution.py:436
  47.5 0.0 collective-permute-start
  47.5 8.3 %collective-permute-done.1.next_in = bf16[88,2048]{1,0:T(8,128)(2,1)S(1)} collective-permute-done((bf16[88,2048]{1,0:T(8,128)(2,1)S(1)}, bf16[88,2048]{1,0:T(8,128)(2,1)S(1)}, u32[]{:S(2)}, u32[]{:S(2)}) %collective-permute-start.1) | collective-permute-done | bytes 360480 | tf_op jit(solution)/shard_map/ppermute | solution.py:436
  55.9 3.1 %collective-permute-done.prev_in = bf16[88,2048]{1,0:T(8,128)(2,1)S(1)} collective-permute-done((bf16[88,2048]{1,0:T(8,128)(2,1)S(1)}, bf16[88,2048]{1,0:T(8,128)(2,1)S(1)}, u32[]{:S(2)}, u32[]{:S(2)}) %collective-permute-start) | collective-permute-done | bytes 360480 | tf_op jit(solution)/shard_map/ppermute | solution.py:435
  58.9 0.0 copy-done
  58.9 0.0 copy-done.1
  58.9 6.1 %pairs.1 = (f32[128,256]{1,0:T(8,128)S(1)}, bf16[64,256]{1,0:T(8,128)(2,1)S(1)}, f32[8,256]{1,0:T(8,128)S(1)}, bf16[128,64]{1,0:T(8,128)(2,1)S(1)}, bf16[64,128]{1,0:T(8,128)(2,1)S(1)}) custom-call(s32[2]{0:T(128)S(1)} %pad_add_fusion.place_ref, s32[1]{0:T(128)S(6)} %copy.13.count_ref, s32[16,27]{1,0:T(8,128)S(1)} %bitcast.15, s32[16,27]{1,0:T(8,128)S(1)} %bitcast.16, ...), custom_call_target="tpu_custom_call" | custom-call | flops 130940928 | bytes 1081344 | tf_op jit(solution)/shard_map/pairs/pallas_call | solution.py:346
  65.0 0.0 all-to-all-done.2.arrived_ref
  65.1 0.3 update.1
  65.4 18.4 %all_to_all.22 = bf16[8,64,256]{2,1,0:T(8,128)(2,1)S(1)} all-to-all(bf16[8,64,256]{2,1,0:T(8,128)(2,1)S(1)} %update.1), channel_id=1, replica_groups=mesh['atoms'=32,'waves'=8] {'waves'}, dimensions={0} | all-to-all | bytes 524288 | tf_op jit(solution)/shard_map/all_to_all | solution.py:406
  83.8 0.7 copy.12
Async XLA Ops:
  0.7 58.2 %copy-start = (s32[27,16]{0,1:T(8,128)S(1)}, s32[27,16]{0,1:T(8,128)}, u32[]{:S(2)}) copy-start(s32[27,16]{0,1:T(8,128)} %param.12) | copy-start | bytes 5188
  0.7 58.2 %copy-start.1 = (s32[27,16]{0,1:T(8,128)S(1)}, s32[27,16]{0,1:T(8,128)}, u32[]{:S(2)}) copy-start(s32[27,16]{0,1:T(8,128)} %param.13) | copy-start | bytes 5188
  6.7 39.1 %copy-start.2 = (bf16[88,2048]{1,0:T(8,128)(2,1)S(1)}, bf16[88,2048]{1,0:T(8,128)(2,1)}, u32[]{:S(2)}) copy-start(bf16[88,2048]{1,0:T(8,128)(2,1)} %get-tuple-element.21.own_in) | copy-start | bytes 1081348
  37.4 27.6 %all-to-all-start.2 = ((bf16[8,64,256]{2,1,0:T(8,128)(2,1)}), bf16[8,64,256]{2,1,0:T(8,128)(2,1)S(1)}, u32[]{:S(2)}, u32[]{:S(2)}) async-start(bf16[8,64,256]{2,1,0:T(8,128)(2,1)} %potentials.1), calls=%async_computation.2 | async-start | bytes 524288 | tf_op jit(solution)/shard_map/all_to_all | solution.py:406
  45.8 10.0 %collective-permute-start.1 = (bf16[88,2048]{1,0:T(8,128)(2,1)S(1)}, bf16[88,2048]{1,0:T(8,128)(2,1)S(1)}, u32[]{:S(2)}, u32[]{:S(2)}) collective-permute-start(bf16[88,2048]{1,0:T(8,128)(2,1)S(1)} %copy-done.2), channel_id=1, source_target_pairs={{8,0},{16,8},{24,16},{32,24},{40,32},{48,40},{56,48},{64,56},{72,6... | collective-permute-start | bytes 1081352 | tf_op jit(solution)/shard_map/ppermute | solution.py:436
  47.5 11.4 %collective-permute-start = (bf16[88,2048]{1,0:T(8,128)(2,1)S(1)}, bf16[88,2048]{1,0:T(8,128)(2,1)S(1)}, u32[]{:S(2)}, u32[]{:S(2)}) collective-permute-start(bf16[88,2048]{1,0:T(8,128)(2,1)S(1)} %copy-done.2), channel_id=1, source_target_pairs={{0,8},{8,16},{16,24},{24,32},{32,40},{40,48},{48,56},{56,64},{64,7... | collective-permute-start | bytes 1081352 | tf_op jit(solution)/shard_map/ppermute | solution.py:435

commit v7 on v6

--- a/solution.py
+++ b/solution.py
@@ -75,8 +75,8 @@
         copy.start()
     taken[0].wait()
     kf = kvec_ref[...].astype(jnp.float32)
-    ahead, behind = jnp.zeros((3, waves), jnp.float32), jnp.zeros((2, waves), jnp.float32)
-    ka = jnp.concatenate([part for axis in range(3) for part in (ahead, *(-kf[axis : axis + 1],) * 3, behind)], axis=0)
+    behind = jnp.zeros((5, waves), jnp.float32)
+    ka = jnp.concatenate([-kf, behind] * 3, axis=0)
     ka_ref[...] = ka.T.astype(jnp.bfloat16)
     kx = kf[0:1] / regions
     gain = GAIN_TOP / (4.0 + kx * kx + kf[1:2] * kf[1:2] + kf[2:3] * kf[2:3])
@@ -85,11 +85,10 @@
     mine = jnp.sum(jnp.where(own, jnp.broadcast_to(gain, (owned, waves)), 0.0), axis=1, keepdims=True)
     gain_ref[...] = jnp.broadcast_to(mine * scale, gain_ref.shape)
     taken[1].wait()
-    pieces = three_pieces(coords_ref[...])
-    ones, gap = jnp.ones((3, atoms), jnp.float32), jnp.zeros((2, atoms), jnp.float32)
-    for axis in range(3):
-        rows = jnp.concatenate([ones, *(-piece[axis : axis + 1] for piece in pieces), gap], axis=0)
-        carry_ref[chans + 8 * axis : chans + 8 * axis + 8, :] = rows.astype(jnp.bfloat16)
+    gap = jnp.zeros((5, atoms), jnp.float32)
+    for at, piece in enumerate(three_pieces(-coords_ref[...])):
+        rows = jnp.concatenate([piece, gap], axis=0)
+        carry_ref[chans + 8 * at : chans + 8 * at + 8, :] = rows.astype(jnp.bfloat16)
     for copy in taken[2:]:
         copy.wait()
     live_atoms = count_ref[0] * BLOCK
@@ -199,13 +198,21 @@
     )(arrived, gain, mixing)
 
 
-def potentials_kernel(filtered_ref, low_ref, high_in, out_ref, high_ref, across_ref, sum_ref, sem):
+def potentials_kernel(
+    filtered_ref, low_ref, high_in, prev_in, next_in, own_in,
+    out_ref, pos_ref, high_ref, rows_ref, across_ref, sum_ref, sems,
+):
     chans = out_ref.shape[1]
     pieces, _, width = out_ref.shape
     atoms = pieces * width
     kept, waves = low_ref.shape[0], filtered_ref.shape[0]
-    copy = pltpu.make_async_copy(high_in, high_ref, sem)
-    copy.start()
+    region = own_in.shape[1]
+    moves = [(high_in, high_ref)]
+    for at, source in enumerate((prev_in, own_in, next_in)):
+        moves.append((source.at[pl.ds(chans, 24), :], rows_ref.at[:, pl.ds(at * region, region)]))
+    copies = [pltpu.make_async_copy(source, target, sems.at[at]) for at, (source, target) in enumerate(moves)]
+    for copy in copies:
+        copy.start()
     across_ref[...] = filtered_ref[...].astype(jnp.float32).T.astype(jnp.bfloat16)
 
     def term(rows, table, piece):
@@ -218,126 +225,128 @@
 
     for piece in range(pieces):
         sum_ref[piece] = term(slice(0, kept), low_ref, piece)
-    copy.wait()
+    for copy in copies:
+        copy.wait()
+    parts = [rows_ref[8 * at : 8 * at + 8, :].astype(jnp.float32) for at in range(3)]
+    pos_ref[...] = (parts[2] + parts[1]) + parts[0]
     for piece in range(pieces):
         whole = sum_ref[piece] + term(slice(kept, waves), high_ref, piece)
         out_ref[piece] = (whole * (1.0 / math.sqrt(K))).astype(jnp.bfloat16)
 
 
-def potentials(filtered, low, high, pieces):
+def potentials(filtered, low, high, prev, following, own, pieces):
     chans = filtered.shape[1] // 2
     atoms = low.shape[1] // 2
     return pl.pallas_call(
         potentials_kernel,
-        out_shape=jax.ShapeDtypeStruct((pieces, chans, atoms // pieces), jnp.bfloat16),
-        in_specs=[VMEM_SPEC, VMEM_SPEC, HBM_SPEC],
-        out_specs=VMEM_SPEC,
+        out_shape=(
+            jax.ShapeDtypeStruct((pieces, chans, atoms // pieces), jnp.bfloat16),
+            jax.ShapeDtypeStruct((8, 3 * atoms), jnp.float32),
+        ),
+        in_specs=[VMEM_SPEC, VMEM_SPEC, HBM_SPEC, ANY_SPEC, ANY_SPEC, HBM_SPEC],
+        out_specs=(VMEM_SPEC, VMEM_SPEC),
         scratch_shapes=[
             pltpu.VMEM(high.shape, jnp.bfloat16),
+            pltpu.VMEM((24, 3 * atoms), jnp.bfloat16),
             pltpu.VMEM((2 * chans, filtered.shape[0]), jnp.bfloat16),
             pltpu.VMEM((pieces, chans, atoms // pieces), jnp.float32),
-            pltpu.SemaphoreType.DMA,
+            pltpu.SemaphoreType.DMA((4,)),
         ],
         compiler_params=PARAMS,
         name="potentials",
-    )(filtered, low, *in_hbm(high))
+    )(filtered, low, *in_hbm(high), prev, following, *in_hbm(own))
 
 
 def pairs_kernel(
-    scale_x, regions, unroll, place_ref, count_ref, idx_ref, live_ref, prev_in, next_in, own_in, h_in, first_in, second_in,
+    scale_x, regions, unroll, place_ref, count_ref, idx_ref, live_ref, pos_ref,
+    prev_in, next_in, own_in, h_in, first_in, second_in,
     inner_ref, share_ref, alive_ref, third_ref, second_ref,
-    ext_ref, first_ref, own_ref, pos_ref, weights_ref, near_ref, sum_ref, sems,
+    ext_ref, first_ref, own_ref, weights_ref, near_ref, sum_ref, sems,
 ):
-    chans = h_in.shape[0]
-    width = own_in.shape[1]
+    chans, width = h_in.shape
     nblocks = width // BLOCK
     slots = idx_ref.shape[1]
     count = share_ref.shape[1] // BLOCK
     here = place_ref[0]
     first = place_ref[1]
+    f32 = dict(preferred_element_type=jnp.float32)
     share = pl.ds(pl.multiple_of(first * BLOCK, BLOCK), count * BLOCK)
     moves = []
-    for rows in (pl.ds(chans, ext_ref.shape[0] - chans), pl.ds(0, chans)):
-        for at, source in enumerate((prev_in, own_in, next_in)):
-            moves.append((source.at[rows, :], ext_ref.at[rows, pl.ds(at * width, width)]))
+    for at, source in enumerate((prev_in, own_in, next_in)):
+        moves.append((source.at[pl.ds(0, chans), :], ext_ref.at[:, pl.ds(at * width, width)]))
     moves += [(h_in.at[:, share], share_ref), (first_in, first_ref), (second_in, second_ref)]
     copies = [pltpu.make_async_copy(source, target, sems.at[at]) for at, (source, target) in enumerate(moves)]
     for copy in copies:
         copy.start()
     atom = lax.broadcasted_iota(jnp.int32, alive_ref.shape, 1) + first * BLOCK
     alive_ref[...] = jnp.where(atom < count_ref[0] * BLOCK, 1.0, 0.0)
+    for block in range(count):
+        at = pl.multiple_of((nblocks + first + block) * BLOCK, BLOCK)
+        columns = -pos_ref[:, pl.ds(at, BLOCK)].T
+        for axis in range(3):
+            own_ref[block, axis] = jnp.broadcast_to(columns[:, axis : axis + 1], (BLOCK, BLOCK))
+        sum_ref[block] = jnp.zeros((chans, BLOCK), jnp.float32)
+    exponent = -2.0 * math.log2(math.e)
+    part_rows = 16
+
+    def span_of(block, slot):
+        entry = idx_ref[first + block, slot]
+        where = jnp.bitwise_and(entry + (regions + 1 - here) * nblocks, regions * nblocks - 1)
+        return pl.ds(pl.multiple_of(where * BLOCK, BLOCK), BLOCK)
+
+    def weigh(block, step):
+        for part in range(unroll):
+            span = span_of(block, step * unroll + part)
+            to = slice(part * BLOCK, (part + 1) * BLOCK)
+            minus = [jnp.broadcast_to(pos_ref[axis : axis + 1, span], (part_rows, BLOCK)) for axis in range(3)]
+            for start in range(0, BLOCK, part_rows):
+                rows = slice(start, start + part_rows)
+                total = None
+                for axis in range(3):
+                    diff = own_ref[block, axis, rows, :] + minus[axis]
+                    diff = diff - jnp.round(diff)
+                    term = diff * diff
+                    if axis == 0:
+                        term = term * (scale_x * scale_x)
+                    total = term if total is None else total + term
+                weights_ref[block, rows, to] = jnp.exp2(total * exponent).astype(jnp.bfloat16)
+
+    def add_up(block, step):
+        for part in range(unroll):
+            slot = step * unroll + part
+            used = live_ref[first + block, slot].astype(jnp.float32)
+            mapped = ext_ref[:, span_of(block, slot)].astype(jnp.float32) * used
+            near_ref[block, :, part * BLOCK : (part + 1) * BLOCK] = mapped.astype(jnp.bfloat16)
+        sum_ref[block] += lax.dot_general(near_ref[block], weights_ref[block], NT, **f32)
+
+    steps = slots // unroll
+    for block in range(count):
+        weigh(block, 0)
     for copy in copies[:3]:
         copy.wait()
-    f32 = dict(preferred_element_type=jnp.float32)
-    column = lax.broadcasted_iota(jnp.int32, (8, 8), 1)
-    pick = jnp.where((column >= 3) & (column < 6), 1.0, 0.0).astype(jnp.bfloat16)
-    row = lax.broadcasted_iota(jnp.int32, (8, BLOCK), 0)
-    lead = jnp.where(row < 3, 1.0, 0.0).astype(jnp.bfloat16)
-    for axis in range(3):
-        rows = slice(chans + 8 * axis, chans + 8 * axis + 8)
-        for start in range(0, 3 * width, 4 * BLOCK):
-            span = slice(start, start + 4 * BLOCK)
-            pos_ref[axis, :, span] = jnp.dot(pick, ext_ref[rows, span], **f32)
-    for block in range(count):
-        at = pl.multiple_of((nblocks + first + block) * BLOCK, BLOCK)
-        for axis in range(3):
-            rows = ext_ref[chans + 8 * axis : chans + 8 * axis + 8, pl.ds(at, BLOCK)].astype(jnp.float32)
-            swapped = jnp.concatenate([-rows[3:6], rows[0:3], rows[6:8]], axis=0)
-            own_ref[block, axis] = jnp.dot(swapped.T.astype(jnp.bfloat16), lead, **f32)
-        sum_ref[block] = jnp.zeros((chans, BLOCK), jnp.float32)
-        weights_ref[block] = jnp.zeros(weights_ref.shape[1:], jnp.bfloat16)
-        near_ref[block] = jnp.zeros(near_ref.shape[1:], jnp.bfloat16)
-    for copy in copies[3:6]:
-        copy.wait()
-    exponent = -2.0 * math.log2(math.e)
-    part_rows = 16
-
-    def add_up(block):
-        sum_ref[block] += lax.dot_general(near_ref[block], weights_ref[block], NT, **f32)
 
     def slots_step(step, carried):
         for block in range(count):
-            add_up(block)
-        for block in range(count):
-            for part in range(unroll):
-                slot = step * unroll + part
-                entry = idx_ref[first + block, slot]
-                where = jnp.bitwise_and(entry + (regions + 1 - here) * nblocks, regions * nblocks - 1)
-                span = pl.ds(pl.multiple_of(where * BLOCK, BLOCK), BLOCK)
-                to = slice(part * BLOCK, (part + 1) * BLOCK)
-                used = live_ref[first + block, slot].astype(jnp.float32)
-                mapped = ext_ref[:chans, span].astype(jnp.float32) * used
-                near_ref[block, :, to] = mapped.astype(jnp.bfloat16)
-                minus = [jnp.tile(pos_ref[axis, :, span], (part_rows // 8, 1)) for axis in range(3)]
-                for start in range(0, BLOCK, part_rows):
-                    rows = slice(start, start + part_rows)
-                    total = None
-                    for axis in range(3):
-                        diff = own_ref[block, axis, rows, :] + minus[axis]
-                        diff = diff - jnp.round(diff)
-                        term = diff * diff
-                        if axis == 0:
-                            term = term * (scale_x * scale_x)
-                        total = term if total is None else total + term
-                    weights_ref[block, rows, to] = jnp.exp2(total * exponent).astype(jnp.bfloat16)
+            add_up(block, step - 1)
+            weigh(block, step)
         return carried
 
-    lax.fori_loop(0, slots // unroll, slots_step, 0)
-    for copy in copies[6:]:
+    lax.fori_loop(1, steps, slots_step, 0)
+    for block in range(count):
+        add_up(block, steps - 1)
+    for copy in copies[3:]:
         copy.wait()
     outer = first_ref[: 2 * chans, :]
     third_ref[...] = first_ref[2 * chans :, :].astype(jnp.float32).T.astype(jnp.bfloat16)
     for block in range(count):
-        add_up(block)
         span = slice(block * BLOCK, (block + 1) * BLOCK)
         msg = (sum_ref[block] * MSG_SCALE).astype(jnp.bfloat16)
         known = jnp.concatenate([share_ref[:, span], msg], axis=0)
         inner_ref[:, span] = lax.dot_general(outer, known, TN, **f32)
 
 
-def pairs(place, live_blocks, neighbours, live_slots, prev, own, following, h, first, second, count, regions):
-    rows, width = own.shape
-    chans = h.shape[0]
+def pairs(place, live_blocks, neighbours, live_slots, positions, prev, own, following, h, first, second, count, regions):
+    chans, width = h.shape
     hidden = first.shape[1]
     slots = neighbours.shape[1]
     share = count * BLOCK
@@ -352,24 +361,23 @@
             jax.ShapeDtypeStruct((hidden, chans), jnp.bfloat16),
             jax.ShapeDtypeStruct(second.shape, jnp.bfloat16),
         ),
-        in_specs=[SMEM_SPEC] * 4 + [ANY_SPEC] * 2 + [HBM_SPEC] * 4,
+        in_specs=[SMEM_SPEC] * 4 + [VMEM_SPEC] + [ANY_SPEC] * 2 + [HBM_SPEC] * 4,
         out_specs=(VMEM_SPEC,) * 5,
         scratch_shapes=[
-            pltpu.VMEM((rows, 3 * width), jnp.bfloat16),
+            pltpu.VMEM((chans, 3 * width), jnp.bfloat16),
             pltpu.VMEM(first.shape, jnp.bfloat16),
             pltpu.VMEM((count, 3, BLOCK, BLOCK), jnp.float32),
-            pltpu.VMEM((3, 8, 3 * width), jnp.float32),
             pltpu.VMEM((count, BLOCK, unroll * BLOCK), jnp.bfloat16),
             pltpu.VMEM((count, chans, unroll * BLOCK), jnp.bfloat16),
             pltpu.VMEM((count, chans, BLOCK), jnp.float32),
-            pltpu.SemaphoreType.DMA((9,)),
+            pltpu.SemaphoreType.DMA((6,)),
         ],
         compiler_params=PARAMS,
         cost_estimate=pl.CostEstimate(
-            flops=work * (2 * chans + 20), bytes_accessed=6 * rows * width, transcendentals=work
+            flops=work * (2 * chans + 20), bytes_accessed=6 * chans * width, transcendentals=work
         ),
         name="pairs",
-    )(place, live_blocks, neighbours, live_slots, prev, following, *in_hbm(own, h, first, second))
+    )(place, live_blocks, neighbours, live_slots, positions, prev, following, *in_hbm(own, h, first, second))
 
 
 def update_kernel(arrived_ref, inner_ref, share_ref, alive_ref, third_ref, second_ref, out_ref):
@@ -436,10 +444,10 @@
     following = lax.ppermute(carry, "atoms", [((i + 1) % regions, i) for i in range(regions)])
     everyone = spectral(arrived, gain_rows, mixing)
     filtered = from_others(everyone, "atoms").reshape(waves, 2 * chans)
-    partial_potential = potentials(filtered, low, high, groups_waves)
+    partial_potential, positions = potentials(filtered, low, high, prev, following, carry, groups_waves)
     potential = from_others(partial_potential, "waves")
     known = pairs(
-        place, block_count, neighbours.T, live_slots.T, prev, carry, following,
+        place, block_count, neighbours.T, live_slots.T, positions, prev, carry, following,
         features, mlp_in[0].T, mlp_out[0], per_group, regions,
     )
     new = update(potential, known)

time: 85.9 us -> 79.2 us (0.922); the launches traced: 84.5 us -> 78.7 us
  blocking collectives: 46.4 us -> 15.1 us
  starting transfers between devices: 10.1 us -> 25.1 us
  waiting for transfers between devices: 11.4 us -> 20.7 us
  Pallas kernels: 15 us -> 16.2 us
    all_to_all x3 -> x1, blocking collectives: 46.4 us -> 15.1 us  [from_others(): return lax.all_to_all(pieces, axis, 0, 0, tiled=True)]
    all_to_all x1 -> x3, waiting for transfers between devices: 0.01 us -> 20.7 us  [from_others(): return lax.all_to_all(pieces, axis, 0, 0, tiled=True)]
    all_to_all x1 -> x3, starting transfers between devices: 8.41 us -> 22.7 us  [from_others(): return lax.all_to_all(pieces, axis, 0, 0, tiled=True)]
    ppermute x1, waiting for transfers between devices: 8.33 us -> 0.01 us  [local(): lax.ppermute(carry, 'atoms', [((i + 1) % regions, i) for i in range(regio...]
    ppermute x1, waiting for transfers between devices: 3.07 us -> 0.01 us  [local(): lax.ppermute(carry, 'atoms', [(i, (i + 1) % regions) for i in range(regio...]
  transfers between devices with their start and end apart: 3 -> 5, of which waited for: 2 -> 3; matrix products, arithmetic and copies ran while one was open for 0% -> 0% of each run, Pallas kernels for 7% -> 9%
where the time goes in v7:
time: 79.2 us; the launch traced here: 78.7 us
  starting transfers between devices  25.1 us (32%)
  waiting for transfers between devices  20.7 us (26%)
  Pallas kernels  16.2 us (20%)
  blocking collectives  15.1 us (19%)
    all_to_all x3, starting transfers between devices, from_others(): return lax.all_to_all(pieces, axis, 0, 0, tiled=True)  22.7 us
    all_to_all x3, waiting for transfers between devices, from_others(): return lax.all_to_all(pieces, axis, 0, 0, tiled=True)  20.7 us
    all_to_all x1, blocking collectives, from_others(): return lax.all_to_all(pieces, axis, 0, 0, tiled=True)  15.1 us
    pallas_call x1, Pallas kernels, structure(): pl.pallas_call(functools.partial(structure_kernel, scale, float(regions))...  6.66 us
    pallas_call x1, Pallas kernels, pairs(): pl.pallas_call(functools.partial(pairs_kernel, float(regions), regions, u...  5.83 us
    ppermute x1, starting transfers between devices, local(): lax.ppermute(carry, 'atoms', [((i + 1) % regions, i) for i in range(regio...  2.47 us
    pallas_call x1, Pallas kernels, potentials(): pl.pallas_call(potentials_kernel, out_shape=(jax.ShapeDtypeStruct((pieces...  2.36 us
  transfers between devices with their start and end apart: 5, of which 3 were waited for; matrix products, arithmetic and copies ran while one was open for 0% of the time, Pallas kernels for 9%

profile of v7, /device:TPU:32, one launch (start us, length us, event | category | flops | bytes accessed | tf_op | source)
XLA Modules:
  0.0 78.7 jit_solution(13051905491082974434)
XLA Ops:
  0.7 0.1 pad_add_fusion.place_ref
  0.7 6.7 %structure.1 = (bf16[384,4096]{1,0:T(8,128)(2,1)S(1)}, bf16[128,4096]{1,0:T(8,128)(2,1)}, bf16[32,16,128]{2,1,0:T(8,128)(2,1)}, bf16[88,2048]{1,0:T(8,128)(2,1)}...) custom-call(s32[2]{0:T(128)S(1)} %pad_add_fusion.place_ref, s32[1]{0:T(128)S(6)} %copy.13.count_ref, s32[3,512]{1,0:T(4,128)} %kvec_in.1, ...), custom_call_target="tpu_custom_call" | custom-call | tf_op jit(solution)/shard_map/structure/pallas_call | solution.py:147
  7.4 8.6 %all-to-all-start = ((bf16[32,16,128]{2,1,0:T(8,128)(2,1)}), bf16[32,16,128]{2,1,0:T(8,128)(2,1)S(1)}, u32[]{:S(2)}, u32[]{:S(2)}) async-start(bf16[32,16,128]{2,1,0:T(8,128)(2,1)} %get-tuple-element.18), calls=%async_computation | async-start | bytes 262144 | tf_op jit(solution)/shard_map/all_to_all | solution.py:414
  16.0 2.5 %collective-permute-start.1 = (bf16[88,2048]{1,0:T(8,128)(2,1)}, bf16[88,2048]{1,0:T(8,128)(2,1)}, u32[]{:S(2)}, u32[]{:S(2)}) collective-permute-start(bf16[88,2048]{1,0:T(8,128)(2,1)} %get-tuple-element.23.own_in), channel_id=1, source_target_pairs={{8,0},{16,8},{24,16},{32,24},{40,32},{48,40},{56,48},{64,56},{72,6... | collective-permute-start | bytes 1081352 | tf_op jit(solution)/shard_map/ppermute | solution.py:444
  18.5 0.0 collective-permute-start
  18.5 5.0 %all-to-all-done.arrived_ref = bf16[32,16,128]{2,1,0:T(8,128)(2,1)S(1)} async-done(((bf16[32,16,128]{2,1,0:T(8,128)(2,1)}), bf16[32,16,128]{2,1,0:T(8,128)(2,1)S(1)}, u32[]{:S(2)}, u32[]{:S(2)}) %all-to-all-start) | async-done | bytes 131104 | tf_op jit(solution)/shard_map/all_to_all | solution.py:414
  23.5 1.0 %spectral.1 = bf16[32,16,128]{2,1,0:T(8,128)(2,1)} custom-call(bf16[32,16,128]{2,1,0:T(8,128)(2,1)S(1)} %all-to-all-done.arrived_ref, f32[16,128]{1,0:T(8,128)S(1)} %get-tuple-element.19.gain_ref, f32[64,64]{1,0:T(8,128)S(1)} %get-tuple-element.20.mixing_ref), custom_call_target="tpu_custom_call" | custom-call | tf_op jit(solution)/shard_map/spectral/pallas_call | solution.py:191
  24.5 0.0 copy-start
  24.5 0.0 copy-start.1
  24.5 5.6 %all-to-all-start.1 = ((bf16[32,16,128]{2,1,0:T(8,128)(2,1)}), bf16[32,16,128]{2,1,0:T(8,128)(2,1)S(1)}, u32[]{:S(2)}, u32[]{:S(2)}) async-start(bf16[32,16,128]{2,1,0:T(8,128)(2,1)} %spectral.1), calls=%async_computation.1 | async-start | bytes 262144 | tf_op jit(solution)/shard_map/all_to_all | solution.py:414
  30.1 0.0 collective-permute-done.1.next_in
  30.1 0.0 collective-permute-done.prev_in
  30.1 7.4 %all-to-all-done.1 = bf16[32,16,128]{2,1,0:T(8,128)(2,1)S(1)} async-done(((bf16[32,16,128]{2,1,0:T(8,128)(2,1)}), bf16[32,16,128]{2,1,0:T(8,128)(2,1)S(1)}, u32[]{:S(2)}, u32[]{:S(2)}) %all-to-all-start.1) | async-done | bytes 131104 | tf_op jit(solution)/shard_map/all_to_all | solution.py:414
  37.5 2.4 %potentials.1 = (bf16[8,64,256]{2,1,0:T(8,128)(2,1)}, f32[8,6144]{1,0:T(8,128)S(1)}) custom-call(bf16[512,128]{1,0:T(8,128)(2,1)S(1)} %bitcast.14, bf16[384,4096]{1,0:T(8,128)(2,1)S(1)} %get-tuple-element.21.low_ref, bf16[128,4096]{1,0:T(8,128)(2,1)} %get-tuple-element.22.high_in, bf16[88,2048]{1,0:T(8,128)(2,1)} %collective-permute-done.prev_in, ...), custom_call_target="tpu_custom_call" | custom-call | tf_op jit(solution)/shard_map/potentials/pallas_call | solution.py:240
  39.9 8.4 %all-to-all-start.2 = ((bf16[8,64,256]{2,1,0:T(8,128)(2,1)}), bf16[8,64,256]{2,1,0:T(8,128)(2,1)S(1)}, u32[]{:S(2)}, u32[]{:S(2)}) async-start(bf16[8,64,256]{2,1,0:T(8,128)(2,1)} %get-tuple-element.24), calls=%async_computation.2 | async-start | bytes 524288 | tf_op jit(solution)/shard_map/all_to_all | solution.py:414
  48.3 0.0 copy-done
  48.3 0.0 copy-done.1
  48.3 5.8 %pairs.1 = (f32[128,256]{1,0:T(8,128)S(1)}, bf16[64,256]{1,0:T(8,128)(2,1)S(1)}, f32[8,256]{1,0:T(8,128)S(1)}, bf16[128,64]{1,0:T(8,128)(2,1)S(1)}, bf16[64,128]{1,0:T(8,128)(2,1)S(1)}) custom-call(s32[2]{0:T(128)S(1)} %pad_add_fusion.place_ref, s32[1]{0:T(128)S(6)} %copy.13.count_ref, s32[16,27]{1,0:T(8,128)S(1)} %bitcast.15, s32[16,27]{1,0:T(8,128)S(1)} %bitcast.16, ...), custom_call_target="tpu_custom_call" | custom-call | flops 130940928 | bytes 786432 | tf_op jit(solution)/shard_map/pairs/pallas_call | solution.py:355
  54.2 8.4 %all-to-all-done.2.arrived_ref = bf16[8,64,256]{2,1,0:T(8,128)(2,1)S(1)} async-done(((bf16[8,64,256]{2,1,0:T(8,128)(2,1)}), bf16[8,64,256]{2,1,0:T(8,128)(2,1)S(1)}, u32[]{:S(2)}, u32[]{:S(2)}) %all-to-all-start.2) | async-done | bytes 262176 | tf_op jit(solution)/shard_map/all_to_all | solution.py:414
  62.5 0.3 update.1
  62.9 15.1 %all_to_all.20 = bf16[8,64,256]{2,1,0:T(8,128)(2,1)S(1)} all-to-all(bf16[8,64,256]{2,1,0:T(8,128)(2,1)S(1)} %update.1), channel_id=1, replica_groups=mesh['atoms'=32,'waves'=8] {'waves'}, dimensions={0} | all-to-all | bytes 524288 | tf_op jit(solution)/shard_map/all_to_all | solution.py:414
  78.0 0.7 copy.12
Async XLA Ops:
  7.4 16.1 %all-to-all-start = ((bf16[32,16,128]{2,1,0:T(8,128)(2,1)}), bf16[32,16,128]{2,1,0:T(8,128)(2,1)S(1)}, u32[]{:S(2)}, u32[]{:S(2)}) async-start(bf16[32,16,128]{2,1,0:T(8,128)(2,1)} %get-tuple-element.18), calls=%async_computation | async-start | bytes 262144 | tf_op jit(solution)/shard_map/all_to_all | solution.py:414
  16.0 14.1 %collective-permute-start.1 = (bf16[88,2048]{1,0:T(8,128)(2,1)}, bf16[88,2048]{1,0:T(8,128)(2,1)}, u32[]{:S(2)}, u32[]{:S(2)}) collective-permute-start(bf16[88,2048]{1,0:T(8,128)(2,1)} %get-tuple-element.23.own_in), channel_id=1, source_target_pairs={{8,0},{16,8},{24,16},{32,24},{40,32},{48,40},{56,48},{64,56},{72,6... | collective-permute-start | bytes 1081352 | tf_op jit(solution)/shard_map/ppermute | solution.py:444
  18.5 11.6 %collective-permute-start = (bf16[88,2048]{1,0:T(8,128)(2,1)}, bf16[88,2048]{1,0:T(8,128)(2,1)}, u32[]{:S(2)}, u32[]{:S(2)}) collective-permute-start(bf16[88,2048]{1,0:T(8,128)(2,1)} %get-tuple-element.23.own_in), channel_id=1, source_target_pairs={{0,8},{8,16},{16,24},{24,32},{32,40},{40,48},{48,56},{56,64},{64,7... | collective-permute-start | bytes 1081352 | tf_op jit(solution)/shard_map/ppermute | solution.py:443
  24.5 23.8 %copy-start = (s32[27,16]{0,1:T(8,128)S(1)}, s32[27,16]{0,1:T(8,128)}, u32[]{:S(2)}) copy-start(s32[27,16]{0,1:T(8,128)} %param.12) | copy-start | bytes 5188
  24.5 23.8 %copy-start.1 = (s32[27,16]{0,1:T(8,128)S(1)}, s32[27,16]{0,1:T(8,128)}, u32[]{:S(2)}) copy-start(s32[27,16]{0,1:T(8,128)} %param.13) | copy-start | bytes 5188
  24.5 13.0 %all-to-all-start.1 = ((bf16[32,16,128]{2,1,0:T(8,128)(2,1)}), bf16[32,16,128]{2,1,0:T(8,128)(2,1)S(1)}, u32[]{:S(2)}, u32[]{:S(2)}) async-start(bf16[32,16,128]{2,1,0:T(8,128)(2,1)} %spectral.1), calls=%async_computation.1 | async-start | bytes 262144 | tf_op jit(solution)/shard_map/all_to_all | solution.py:414
  39.9 22.6 %all-to-all-start.2 = ((bf16[8,64,256]{2,1,0:T(8,128)(2,1)}), bf16[8,64,256]{2,1,0:T(8,128)(2,1)S(1)}, u32[]{:S(2)}, u32[]{:S(2)}) async-start(bf16[8,64,256]{2,1,0:T(8,128)(2,1)} %get-tuple-element.24), calls=%async_computation.2 | async-start | bytes 524288 | tf_op jit(solution)/shard_map/all_to_all | solution.py:414

commit v8 on v6

--- a/solution.py
+++ b/solution.py
@@ -51,13 +51,16 @@
 
 def structure_kernel(
     scale, regions, place_ref, count_ref, kvec_in, coords_in, h_in, weight_in, mixing_in,
-    low_ref, high_out, out_ref, carry_out, gain_ref, mixing_ref,
-    kvec_ref, coords_ref, h_ref, weight_ref, ka_ref, masked_ref, high_ref, carry_ref, in_sems, sems,
+    low_ref, high_out, kept_ref, sent_ref, carry_out, gain_ref, mixing_ref,
+    kvec_ref, coords_ref, h_ref, weight_ref, ka_ref, masked_ref, high_ref, carry_ref, whole_ref, gains_ref, in_sems, sems,
 ):
     waves = kvec_ref.shape[1]
     chans, atoms = h_ref.shape
     kept = low_ref.shape[0]
-    owned = out_ref.shape[1]
+    half = kept_ref.shape[0]
+    core = jnp.bitwise_and(place_ref[0], 1)
+    mine = pl.ds(pl.multiple_of(core * half, half), half)
+    theirs = pl.ds(pl.multiple_of((1 - core) * half, half), half)
     f32 = dict(preferred_element_type=jnp.float32)
     taken = [
         pltpu.make_async_copy(source, target, in_sems.at[at])
@@ -80,10 +83,9 @@
     ka_ref[...] = ka.T.astype(jnp.bfloat16)
     kx = kf[0:1] / regions
     gain = GAIN_TOP / (4.0 + kx * kx + kf[1:2] * kf[1:2] + kf[2:3] * kf[2:3])
-    lane = lax.broadcasted_iota(jnp.int32, (owned, waves), 1)
-    own = lane == lax.broadcasted_iota(jnp.int32, (owned, waves), 0) + place_ref[0] * owned
-    mine = jnp.sum(jnp.where(own, jnp.broadcast_to(gain, (owned, waves)), 0.0), axis=1, keepdims=True)
-    gain_ref[...] = jnp.broadcast_to(mine * scale, gain_ref.shape)
+    columns = jnp.broadcast_to(gain * scale, (8, waves)).T
+    gains_ref[...] = jnp.broadcast_to(columns[:, 0:1], gains_ref.shape)
+    gain_ref[...] = gains_ref[mine, :]
     taken[1].wait()
     pieces = three_pieces(coords_ref[...])
     ones, gap = jnp.ones((3, atoms), jnp.float32), jnp.zeros((2, atoms), jnp.float32)
@@ -106,8 +108,7 @@
         term = term + lax.dot_general(sinv, jnp.concatenate([zero, ht], axis=0), NT, **f32)
         sums[row] = term if start == 0 else sums[row] + term
         if start + TILE == atoms:
-            whole = sums.pop(row).astype(jnp.bfloat16)
-            out_ref[row // owned : (row + ROWS) // owned] = whole.reshape(ROWS // owned, owned, 2 * chans)
+            whole_ref[row : row + ROWS, :] = sums.pop(row)
 
     pending = []
     copies = []
@@ -133,6 +134,8 @@
             if len(pending) > 1:
                 add_up(*pending.pop(0))
     add_up(*pending.pop(0))
+    kept_ref[...] = whole_ref[mine, :]
+    sent_ref[...] = whole_ref[theirs, :].astype(jnp.bfloat16)
     for copy in copies:
         copy.wait()
 
@@ -144,19 +147,19 @@
 def structure(place, count, kvec, coords, h, weight, mixing, scale, regions):
     waves, atoms, chans = kvec.shape[1], coords.shape[1], h.shape[0]
     kept = kept_rows(waves)
-    owned = waves // regions
     return pl.pallas_call(
         functools.partial(structure_kernel, scale, float(regions)),
         out_shape=(
             jax.ShapeDtypeStruct((kept, 2 * atoms), jnp.bfloat16),
             pltpu.HBM((waves - kept, 2 * atoms), jnp.bfloat16),
-            jax.ShapeDtypeStruct((regions, owned, 2 * chans), jnp.bfloat16),
+            jax.ShapeDtypeStruct((waves // 2, 2 * chans), jnp.float32),
+            jax.ShapeDtypeStruct((waves // 2, 2 * chans), jnp.bfloat16),
             pltpu.HBM((chans + 24, atoms), jnp.bfloat16),
-            jax.ShapeDtypeStruct((owned, 2 * chans), jnp.float32),
+            jax.ShapeDtypeStruct((waves // 2, 2 * chans), jnp.float32),
             jax.ShapeDtypeStruct(mixing.shape, jnp.float32),
         ),
         in_specs=[SMEM_SPEC] * 2 + [HBM_SPEC] * 5,
-        out_specs=(VMEM_SPEC, HBM_SPEC, VMEM_SPEC, HBM_SPEC, VMEM_SPEC, VMEM_SPEC),
+        out_specs=(VMEM_SPEC, HBM_SPEC, VMEM_SPEC, VMEM_SPEC, HBM_SPEC, VMEM_SPEC, VMEM_SPEC),
         scratch_shapes=[
             pltpu.VMEM(kvec.shape, jnp.int32),
             pltpu.VMEM(coords.shape, jnp.float32),
@@ -166,6 +169,8 @@
             pltpu.VMEM(h.shape, jnp.bfloat16),
             pltpu.VMEM((waves - kept, 2 * atoms), jnp.bfloat16),
             pltpu.VMEM((chans + 24, atoms), jnp.bfloat16),
+            pltpu.VMEM((waves, 2 * chans), jnp.float32),
+            pltpu.VMEM((waves, 2 * chans), jnp.float32),
             pltpu.SemaphoreType.DMA((5,)),
             pltpu.SemaphoreType.DMA((2,)),
         ],
@@ -174,38 +179,40 @@
     )(place, count, *in_hbm(kvec, coords, h, weight, mixing))
 
 
-def spectral_kernel(arrived_ref, gain_ref, mixing_ref, out_ref):
+def spectral_kernel(kept_ref, arrived_ref, gain_ref, mixing_ref, out_ref):
     chans = mixing_ref.shape[0]
-    factor = arrived_ref[0].astype(jnp.float32)
-    for piece in range(1, arrived_ref.shape[0]):
-        factor = factor + arrived_ref[piece].astype(jnp.float32)
+    factor = kept_ref[...] + arrived_ref[...].astype(jnp.float32)
     high = dict(precision=lax.Precision.HIGHEST, preferred_element_type=jnp.float32)
     mixing = mixing_ref[...]
     cos_part = jnp.dot(factor[:, :chans], mixing, **high)
     sin_part = jnp.dot(factor[:, chans:], mixing, **high)
-    filtered = (jnp.concatenate([cos_part, sin_part], axis=1) * gain_ref[...]).astype(jnp.bfloat16)
-    for piece in range(out_ref.shape[0]):
-        out_ref[piece] = filtered
-
-
-def spectral(arrived, gain, mixing):
+    out_ref[...] = (jnp.concatenate([cos_part, sin_part], axis=1) * gain_ref[...]).astype(jnp.bfloat16)
+
+
+def spectral(kept, arrived, gain, mixing):
     return pl.pallas_call(
         spectral_kernel,
         out_shape=jax.ShapeDtypeStruct(arrived.shape, jnp.bfloat16),
-        in_specs=[VMEM_SPEC] * 3,
+        in_specs=[VMEM_SPEC] * 4,
         out_specs=VMEM_SPEC,
         compiler_params=PARAMS,
         name="spectral",
-    )(arrived, gain, mixing)
-
-
-def potentials_kernel(filtered_ref, low_ref, high_in, out_ref, high_ref, across_ref, sum_ref, sem):
+    )(kept, arrived, gain, mixing)
+
+
+def potentials_kernel(
+    place_ref, own_ref, other_ref, low_ref, high_in, out_ref, filtered_ref, high_ref, across_ref, sum_ref, sem,
+):
     chans = out_ref.shape[1]
     pieces, _, width = out_ref.shape
     atoms = pieces * width
     kept, waves = low_ref.shape[0], filtered_ref.shape[0]
     copy = pltpu.make_async_copy(high_in, high_ref, sem)
     copy.start()
+    half = own_ref.shape[0]
+    core = jnp.bitwise_and(place_ref[0], 1)
+    filtered_ref[pl.ds(pl.multiple_of(core * half, half), half), :] = own_ref[...]
+    filtered_ref[pl.ds(pl.multiple_of((1 - core) * half, half), half), :] = other_ref[...]
     across_ref[...] = filtered_ref[...].astype(jnp.float32).T.astype(jnp.bfloat16)
 
     def term(rows, table, piece):
@@ -224,23 +231,25 @@
         out_ref[piece] = (whole * (1.0 / math.sqrt(K))).astype(jnp.bfloat16)
 
 
-def potentials(filtered, low, high, pieces):
-    chans = filtered.shape[1] // 2
+def potentials(place, own, other, low, high, pieces):
+    chans = own.shape[1] // 2
+    waves = 2 * own.shape[0]
     atoms = low.shape[1] // 2
     return pl.pallas_call(
         potentials_kernel,
         out_shape=jax.ShapeDtypeStruct((pieces, chans, atoms // pieces), jnp.bfloat16),
-        in_specs=[VMEM_SPEC, VMEM_SPEC, HBM_SPEC],
+        in_specs=[SMEM_SPEC, VMEM_SPEC, VMEM_SPEC, VMEM_SPEC, HBM_SPEC],
         out_specs=VMEM_SPEC,
         scratch_shapes=[
+            pltpu.VMEM((waves, 2 * chans), jnp.bfloat16),
             pltpu.VMEM(high.shape, jnp.bfloat16),
-            pltpu.VMEM((2 * chans, filtered.shape[0]), jnp.bfloat16),
+            pltpu.VMEM((2 * chans, waves), jnp.bfloat16),
             pltpu.VMEM((pieces, chans, atoms // pieces), jnp.float32),
             pltpu.SemaphoreType.DMA,
         ],
         compiler_params=PARAMS,
         name="potentials",
-    )(filtered, low, *in_hbm(high))
+    )(place, own, other, low, *in_hbm(high))
 
 
 def pairs_kernel(
@@ -402,6 +411,16 @@
     return jnp.moveaxis(pieces, 0, dim).reshape(lengths)
 
 
+def shifted(cells, regions, groups, step):
+    pairs_of = []
+    for region in range(regions):
+        to = region + step
+        turned = 0 if 0 <= to < regions else groups // 2
+        for group in range(groups):
+            pairs_of.append((region * groups + group, to % regions * groups + (group ^ turned)))
+    return lax.ppermute(cells, ("atoms", "waves"), pairs_of)
+
+
 def from_others(pieces, axis):
     return lax.all_to_all(pieces, axis, 0, 0, tiled=True)
 
@@ -418,7 +437,7 @@
     mlp_in,
     mlp_out,
 ):
-    chans, width = features.shape
+    _, width = features.shape
     nblocks = width // BLOCK
     regions = lax.axis_size("atoms")
     groups_waves = lax.axis_size("waves")
@@ -427,16 +446,20 @@
     first = lax.axis_index("waves") * per_group
     place = jnp.stack([here, first]).astype(jnp.int32)
     total = regions * width
-    waves = kvec.shape[1]
-    low, high, partial_factor, carry, gain_rows, mixing = structure(
+    low, high, factor, sent, carry, gain_rows, mixing = structure(
         place, block_count, kvec, coords, features, msg_weight[0], filter_weight[0], 1.0 / math.sqrt(total), regions
     )
-    arrived = from_others(partial_factor, "atoms")
-    prev = lax.ppermute(carry, "atoms", [(i, (i + 1) % regions) for i in range(regions)])
-    following = lax.ppermute(carry, "atoms", [((i + 1) % regions, i) for i in range(regions)])
-    everyone = spectral(arrived, gain_rows, mixing)
-    filtered = from_others(everyone, "atoms").reshape(waves, 2 * chans)
-    partial_potential = potentials(filtered, low, high, groups_waves)
+    exchanges = (1, 2, 6, 8, 24)
+    for step, flip in enumerate(exchanges):
+        arrived = lax.ppermute(sent, "atoms", [(i, i ^ flip) for i in range(regions)])
+        if step + 1 < len(exchanges):
+            factor = factor + arrived.astype(jnp.float32)
+            sent = factor.astype(jnp.bfloat16)
+    prev = shifted(carry, regions, groups_waves, 1)
+    following = shifted(carry, regions, groups_waves, -1)
+    filtered = spectral(factor, arrived, gain_rows, mixing)
+    other = lax.ppermute(filtered, "atoms", [(i, i ^ 1) for i in range(regions)])
+    partial_potential = potentials(place, filtered, other, low, high, groups_waves)
     potential = from_others(partial_potential, "waves")
     known = pairs(
         place, block_count, neighbours.T, live_slots.T, prev, carry, following,

time: 85.9 us -> 83 us (0.966); the launches traced: 84.5 us -> 82.7 us
  blocking collectives: 46.4 us -> 18.2 us
  starting transfers between devices: 10.1 us -> 23.3 us
  waiting for transfers between devices: 11.4 us -> 23.7 us
    all_to_all x3 -> x1, blocking collectives: 46.4 us -> 18.2 us  [from_others(): return lax.all_to_all(pieces, axis, 0, 0, tiled=True)]
    ppermute x2 -> x8, waiting for transfers between devices: 11.4 us -> 23.7 us  [the longest x5 11.5 us: local(): lax.ppermute(sent, 'atoms', [(i, i ^ flip) for i in range(regions)])]
    ppermute x2 -> x8, starting transfers between devices: 1.68 us -> 13.1 us  [the longest x5 8.41 us: local(): lax.ppermute(sent, 'atoms', [(i, i ^ flip) for i in range(regions)])]
    all_to_all x1, starting transfers between devices: 8.41 us -> 10.2 us  [from_others(): return lax.all_to_all(pieces, axis, 0, 0, tiled=True)]
  transfers between devices with their start and end apart: 3 -> 9, of which waited for: 2 -> 8; matrix products, arithmetic and copies ran while one was open for 0% -> 0% of each run, Pallas kernels for 7% -> 7%
where the time goes in v8:
time: 83 us; the launch traced here: 82.7 us
  waiting for transfers between devices  23.7 us (29%)
  starting transfers between devices  23.3 us (28%)
  blocking collectives  18.2 us (22%)
  Pallas kernels  15.8 us (19%)
    all_to_all x1, blocking collectives, from_others(): return lax.all_to_all(pieces, axis, 0, 0, tiled=True)  18.2 us
    ppermute x5, waiting for transfers between devices, local(): lax.ppermute(sent, 'atoms', [(i, i ^ flip) for i in range(regions)])  11.5 us
    ppermute x2, waiting for transfers between devices, shifted(): return lax.ppermute(cells, ('atoms', 'waves'), pairs_of)  10.9 us
    all_to_all x1, starting transfers between devices, from_others(): return lax.all_to_all(pieces, axis, 0, 0, tiled=True)  10.2 us
    ppermute x5, starting transfers between devices, local(): lax.ppermute(sent, 'atoms', [(i, i ^ flip) for i in range(regions)])  8.41 us
    pallas_call x1, Pallas kernels, pairs(): pl.pallas_call(functools.partial(pairs_kernel, float(regions), regions, u...  6.11 us
    pallas_call x1, Pallas kernels, structure(): pl.pallas_call(functools.partial(structure_kernel, scale, float(regions))...  6.11 us
    ppermute x2, starting transfers between devices, shifted(): return lax.ppermute(cells, ('atoms', 'waves'), pairs_of)  4.56 us
  transfers between devices with their start and end apart: 9, of which 8 were waited for; matrix products, arithmetic and copies ran while one was open for 0% of the time, Pallas kernels for 7%

profile of v8, /device:TPU:32, one launch (start us, length us, event | category | flops | bytes accessed | tf_op | source)
XLA Modules:
  0.0 82.7 jit_solution(4752678705410199715)
XLA Ops:
  0.7 0.1 pad_add_fusion.place_ref
  0.7 6.1 %structure.1 = (bf16[384,4096]{1,0:T(8,128)(2,1)S(1)}, bf16[128,4096]{1,0:T(8,128)(2,1)}, f32[256,128]{1,0:T(8,128)S(1)}, bf16[256,128]{1,0:T(8,128)(2,1)S(1)}, ...) custom-call(s32[2]{0:T(128)S(1)} %pad_add_fusion.place_ref, s32[1]{0:T(128)S(6)} %copy.13.count_ref, ...), custom_call_target="tpu_custom_call" | custom-call | tf_op jit(solution)/shard_map/structure/pallas_call | solution.py:150
  6.9 0.1 collective-permute-start
  7.0 1.2 %collective-permute-done = bf16[256,128]{1,0:T(8,128)(2,1)S(1)} collective-permute-done((bf16[256,128]{1,0:T(8,128)(2,1)S(1)}, bf16[256,128]{1,0:T(8,128)(2,1)S(1)}, u32[]{:S(2)}, u32[]{:S(2)}) %collective-permute-start) | collective-permute-done | bytes 65568 | tf_op jit(solution)/shard_map/ppermute | solution.py:454
  8.2 1.6 %collective-permute-start.1 = (bf16[256,128]{1,0:T(8,128)(2,1)S(1)}, bf16[256,128]{1,0:T(8,128)(2,1)S(1)}, u32[]{:S(2)}, u32[]{:S(2)}) collective-permute-start(bf16[256,128]{1,0:T(8,128)(2,1)S(1)} %fusion), channel_id=1, source_target_pairs={{0,16},{8,24},{16,0},{24,8},{32,48},{40,56},{48,32},{56,40},{64,80... | collective-permute-start | bytes 196616 | tf_op jit(solution)/shard_map/ppermute | solution.py:454
  9.8 2.8 %collective-permute-done.1 = bf16[256,128]{1,0:T(8,128)(2,1)S(1)} collective-permute-done((bf16[256,128]{1,0:T(8,128)(2,1)S(1)}, bf16[256,128]{1,0:T(8,128)(2,1)S(1)}, u32[]{:S(2)}, u32[]{:S(2)}) %collective-permute-start.1) | collective-permute-done | bytes 65568 | tf_op jit(solution)/shard_map/ppermute | solution.py:454
  12.6 2.8 %collective-permute-start.2 = (bf16[256,128]{1,0:T(8,128)(2,1)S(1)}, bf16[256,128]{1,0:T(8,128)(2,1)S(1)}, u32[]{:S(2)}, u32[]{:S(2)}) collective-permute-start(bf16[256,128]{1,0:T(8,128)(2,1)S(1)} %fusion.2), channel_id=1, source_target_pairs={{0,48},{8,56},{16,32},{24,40},{32,16},{40,24},{48,0},{56,8},{64,11... | collective-permute-start | bytes 196616 | tf_op jit(solution)/shard_map/ppermute | solution.py:454
  15.4 2.7 %collective-permute-done.2 = bf16[256,128]{1,0:T(8,128)(2,1)S(1)} collective-permute-done((bf16[256,128]{1,0:T(8,128)(2,1)S(1)}, bf16[256,128]{1,0:T(8,128)(2,1)S(1)}, u32[]{:S(2)}, u32[]{:S(2)}) %collective-permute-start.2) | collective-permute-done | bytes 65568 | tf_op jit(solution)/shard_map/ppermute | solution.py:454
  18.2 0.0 copy-start.2
  18.2 0.0 copy-start
  18.2 0.0 copy-start.1
  18.2 1.9 %collective-permute-start.3 = (bf16[256,128]{1,0:T(8,128)(2,1)S(1)}, bf16[256,128]{1,0:T(8,128)(2,1)S(1)}, u32[]{:S(2)}, u32[]{:S(2)}) collective-permute-start(bf16[256,128]{1,0:T(8,128)(2,1)S(1)} %fusion.1), channel_id=1, source_target_pairs={{0,64},{8,72},{16,80},{24,88},{32,96},{40,104},{48,112},{56,120},{... | collective-permute-start | bytes 196616 | tf_op jit(solution)/shard_map/ppermute | solution.py:454
  20.1 2.5 %collective-permute-done.3 = bf16[256,128]{1,0:T(8,128)(2,1)S(1)} collective-permute-done((bf16[256,128]{1,0:T(8,128)(2,1)S(1)}, bf16[256,128]{1,0:T(8,128)(2,1)S(1)}, u32[]{:S(2)}, u32[]{:S(2)}) %collective-permute-start.3) | collective-permute-done | bytes 65568 | tf_op jit(solution)/shard_map/ppermute | solution.py:454
  22.7 2.0 %collective-permute-start.4 = (bf16[256,128]{1,0:T(8,128)(2,1)S(1)}, bf16[256,128]{1,0:T(8,128)(2,1)S(1)}, u32[]{:S(2)}, u32[]{:S(2)}) collective-permute-start(bf16[256,128]{1,0:T(8,128)(2,1)S(1)} %get-tuple-element.29), channel_id=1, source_target_pairs={{0,192},{8,200},{16,208},{24,216},{32,224},{40,232},{48,240},{56,2... | collective-permute-start | bytes 196616 | tf_op jit(solution)/shard_map/ppermute | solution.py:454
  24.7 2.4 %collective-permute-done.4.arrived_ref = bf16[256,128]{1,0:T(8,128)(2,1)S(1)} collective-permute-done((bf16[256,128]{1,0:T(8,128)(2,1)S(1)}, bf16[256,128]{1,0:T(8,128)(2,1)S(1)}, u32[]{:S(2)}, u32[]{:S(2)}) %collective-permute-start.4) | collective-permute-done | bytes 65568 | tf_op jit(solution)/shard_map/ppermute | solution.py:454
  27.0 0.5 spectral.1.own_ref
  27.5 0.1 collective-permute-start.5
  27.6 1.2 %collective-permute-done.5.other_ref = bf16[256,128]{1,0:T(8,128)(2,1)S(1)} collective-permute-done((bf16[256,128]{1,0:T(8,128)(2,1)S(1)}, bf16[256,128]{1,0:T(8,128)(2,1)S(1)}, u32[]{:S(2)}, u32[]{:S(2)}) %collective-permute-start.5) | collective-permute-done | bytes 65568 | tf_op jit(solution)/shard_map/ppermute | solution.py:461
  28.8 2.8 %potentials.1 = bf16[8,64,256]{2,1,0:T(8,128)(2,1)} custom-call(s32[2]{0:T(128)S(1)} %pad_add_fusion.place_ref, bf16[256,128]{1,0:T(8,128)(2,1)S(1)} %spectral.1.own_ref, bf16[256,128]{1,0:T(8,128)(2,1)S(1)} %collective-permute-done.5.other_ref, bf16[384,4096]{1,0:T(8,128)(2,1)S(1)} %get-tuple-element.21.low_ref, bf16[128,4096]{1,0:T(8,128)(2,1)} %get-tuple-element.22.high_in), custom_call_target="tpu_custom_call" | custom-call | tf_op jit(solution)/shard_map/potentials/pallas_call | solution.py:238
  31.6 10.2 %all-to-all-start = ((bf16[8,64,256]{2,1,0:T(8,128)(2,1)}), bf16[8,64,256]{2,1,0:T(8,128)(2,1)S(1)}, u32[]{:S(2)}, u32[]{:S(2)}) async-start(bf16[8,64,256]{2,1,0:T(8,128)(2,1)} %potentials.1), calls=%async_computation | async-start | bytes 524288 | tf_op jit(solution)/shard_map/all_to_all | solution.py:425
  41.8 0.0 copy-done.2
  41.8 4.6 %collective-permute-start.7 = (bf16[88,2048]{1,0:T(8,128)(2,1)S(1)}, bf16[88,2048]{1,0:T(8,128)(2,1)S(1)}, u32[]{:S(2)}, u32[]{:S(2)}) collective-permute-start(bf16[88,2048]{1,0:T(8,128)(2,1)S(1)} %copy-done.2), channel_id=1, source_target_pairs={{0,252},{1,253},{2,254},{3,255},{4,248},{5,249},{6,250},{7,251},{8... | collective-permute-start | bytes 1081352 | tf_op jit(solution)/shard_map/ppermute | solution.py:421
  46.4 0.0 collective-permute-start.6
  46.4 5.4 %collective-permute-done.7.next_in = bf16[88,2048]{1,0:T(8,128)(2,1)S(1)} collective-permute-done((bf16[88,2048]{1,0:T(8,128)(2,1)S(1)}, bf16[88,2048]{1,0:T(8,128)(2,1)S(1)}, u32[]{:S(2)}, u32[]{:S(2)}) %collective-permute-start.7) | collective-permute-done | bytes 360480 | tf_op jit(solution)/shard_map/ppermute | solution.py:421
  51.8 5.5 %collective-permute-done.6.prev_in = bf16[88,2048]{1,0:T(8,128)(2,1)S(1)} collective-permute-done((bf16[88,2048]{1,0:T(8,128)(2,1)S(1)}, bf16[88,2048]{1,0:T(8,128)(2,1)S(1)}, u32[]{:S(2)}, u32[]{:S(2)}) %collective-permute-start.6) | collective-permute-done | bytes 360480 | tf_op jit(solution)/shard_map/ppermute | solution.py:421
  57.3 0.0 copy-done
  57.3 0.0 copy-done.1
  57.3 6.1 %pairs.1 = (f32[128,256]{1,0:T(8,128)S(1)}, bf16[64,256]{1,0:T(8,128)(2,1)S(1)}, f32[8,256]{1,0:T(8,128)S(1)}, bf16[128,64]{1,0:T(8,128)(2,1)S(1)}, bf16[64,128]{1,0:T(8,128)(2,1)S(1)}) custom-call(s32[2]{0:T(128)S(1)} %pad_add_fusion.place_ref, s32[1]{0:T(128)S(6)} %copy.13.count_ref, s32[16,27]{1,0:T(8,128)S(1)} %bitcast.13, s32[16,27]{1,0:T(8,128)S(1)} %bitcast.14, ...), custom_call_target="tpu_custom_call" | custom-call | flops 130940928 | bytes 1081344 | tf_op jit(solution)/shard_map/pairs/pallas_call | solution.py:355
  63.4 0.0 all-to-all-done.arrived_ref
  63.5 0.3 update.1
  63.8 18.2 %all_to_all.10 = bf16[8,64,256]{2,1,0:T(8,128)(2,1)S(1)} all-to-all(bf16[8,64,256]{2,1,0:T(8,128)(2,1)S(1)} %update.1), channel_id=1, replica_groups=mesh['atoms'=32,'waves'=8] {'waves'}, dimensions={0} | all-to-all | bytes 524288 | tf_op jit(solution)/shard_map/all_to_all | solution.py:425
  82.0 0.7 copy.12
  (4 shorter events, 0.1 us)
Async XLA Ops:
  6.9 1.3 %collective-permute-start = (bf16[256,128]{1,0:T(8,128)(2,1)S(1)}, bf16[256,128]{1,0:T(8,128)(2,1)S(1)}, u32[]{:S(2)}, u32[]{:S(2)}) collective-permute-start(bf16[256,128]{1,0:T(8,128)(2,1)S(1)} %get-tuple-element.18), channel_id=1, source_target_pairs={{0,8},{8,0},{16,24},{24,16},{32,40},{40,32},{48,56},{56,48},{64,72... | collective-permute-start | bytes 196616 | tf_op jit(solution)/shard_map/ppermute | solution.py:454
  8.2 4.4 %collective-permute-start.1 = (bf16[256,128]{1,0:T(8,128)(2,1)S(1)}, bf16[256,128]{1,0:T(8,128)(2,1)S(1)}, u32[]{:S(2)}, u32[]{:S(2)}) collective-permute-start(bf16[256,128]{1,0:T(8,128)(2,1)S(1)} %fusion), channel_id=1, source_target_pairs={{0,16},{8,24},{16,0},{24,8},{32,48},{40,56},{48,32},{56,40},{64,80... | collective-permute-start | bytes 196616 | tf_op jit(solution)/shard_map/ppermute | solution.py:454
  12.6 5.6 %collective-permute-start.2 = (bf16[256,128]{1,0:T(8,128)(2,1)S(1)}, bf16[256,128]{1,0:T(8,128)(2,1)S(1)}, u32[]{:S(2)}, u32[]{:S(2)}) collective-permute-start(bf16[256,128]{1,0:T(8,128)(2,1)S(1)} %fusion.2), channel_id=1, source_target_pairs={{0,48},{8,56},{16,32},{24,40},{32,16},{40,24},{48,0},{56,8},{64,11... | collective-permute-start | bytes 196616 | tf_op jit(solution)/shard_map/ppermute | solution.py:454
  18.2 23.6 %copy-start.2 = (bf16[88,2048]{1,0:T(8,128)(2,1)S(1)}, bf16[88,2048]{1,0:T(8,128)(2,1)}, u32[]{:S(2)}) copy-start(bf16[88,2048]{1,0:T(8,128)(2,1)} %get-tuple-element.23.own_in) | copy-start | bytes 1081348
  18.2 39.1 %copy-start = (s32[27,16]{0,1:T(8,128)S(1)}, s32[27,16]{0,1:T(8,128)}, u32[]{:S(2)}) copy-start(s32[27,16]{0,1:T(8,128)} %param.12) | copy-start | bytes 5188
  18.2 39.1 %copy-start.1 = (s32[27,16]{0,1:T(8,128)S(1)}, s32[27,16]{0,1:T(8,128)}, u32[]{:S(2)}) copy-start(s32[27,16]{0,1:T(8,128)} %param.13) | copy-start | bytes 5188
  18.2 4.4 %collective-permute-start.3 = (bf16[256,128]{1,0:T(8,128)(2,1)S(1)}, bf16[256,128]{1,0:T(8,128)(2,1)S(1)}, u32[]{:S(2)}, u32[]{:S(2)}) collective-permute-start(bf16[256,128]{1,0:T(8,128)(2,1)S(1)} %fusion.1), channel_id=1, source_target_pairs={{0,64},{8,72},{16,80},{24,88},{32,96},{40,104},{48,112},{56,120},{... | collective-permute-start | bytes 196616 | tf_op jit(solution)/shard_map/ppermute | solution.py:454
  22.7 4.4 %collective-permute-start.4 = (bf16[256,128]{1,0:T(8,128)(2,1)S(1)}, bf16[256,128]{1,0:T(8,128)(2,1)S(1)}, u32[]{:S(2)}, u32[]{:S(2)}) collective-permute-start(bf16[256,128]{1,0:T(8,128)(2,1)S(1)} %get-tuple-element.29), channel_id=1, source_target_pairs={{0,192},{8,200},{16,208},{24,216},{32,224},{40,232},{48,240},{56,2... | collective-permute-start | bytes 196616 | tf_op jit(solution)/shard_map/ppermute | solution.py:454
  27.5 1.3 %collective-permute-start.5 = (bf16[256,128]{1,0:T(8,128)(2,1)S(1)}, bf16[256,128]{1,0:T(8,128)(2,1)S(1)}, u32[]{:S(2)}, u32[]{:S(2)}) collective-permute-start(bf16[256,128]{1,0:T(8,128)(2,1)S(1)} %spectral.1.own_ref), channel_id=1, source_target_pairs={{0,8},{8,0},{16,24},{24,16},{32,40},{40,32},{48,56},{56,48},{64,72... | collective-permute-start | bytes 196616 | tf_op jit(solution)/shard_map/ppermute | solution.py:461
  31.6 31.8 %all-to-all-start = ((bf16[8,64,256]{2,1,0:T(8,128)(2,1)}), bf16[8,64,256]{2,1,0:T(8,128)(2,1)S(1)}, u32[]{:S(2)}, u32[]{:S(2)}) async-start(bf16[8,64,256]{2,1,0:T(8,128)(2,1)} %potentials.1), calls=%async_computation | async-start | bytes 524288 | tf_op jit(solution)/shard_map/all_to_all | solution.py:425
  41.8 10.0 %collective-permute-start.7 = (bf16[88,2048]{1,0:T(8,128)(2,1)S(1)}, bf16[88,2048]{1,0:T(8,128)(2,1)S(1)}, u32[]{:S(2)}, u32[]{:S(2)}) collective-permute-start(bf16[88,2048]{1,0:T(8,128)(2,1)S(1)} %copy-done.2), channel_id=1, source_target_pairs={{0,252},{1,253},{2,254},{3,255},{4,248},{5,249},{6,250},{7,251},{8... | collective-permute-start | bytes 1081352 | tf_op jit(solution)/shard_map/ppermute | solution.py:421
  46.4 10.9 %collective-permute-start.6 = (bf16[88,2048]{1,0:T(8,128)(2,1)S(1)}, bf16[88,2048]{1,0:T(8,128)(2,1)S(1)}, u32[]{:S(2)}, u32[]{:S(2)}) collective-permute-start(bf16[88,2048]{1,0:T(8,128)(2,1)S(1)} %copy-done.2), channel_id=1, source_target_pairs={{0,8},{1,9},{2,10},{3,11},{4,12},{5,13},{6,14},{7,15},{8,16},{9,17... | collective-permute-start | bytes 1081352 | tf_op jit(solution)/shard_map/ppermute | solution.py:421

commit v9 on v8

--- a/solution.py
+++ b/solution.py
@@ -449,9 +449,9 @@
     low, high, factor, sent, carry, gain_rows, mixing = structure(
         place, block_count, kvec, coords, features, msg_weight[0], filter_weight[0], 1.0 / math.sqrt(total), regions
     )
-    exchanges = (1, 2, 6, 8, 24)
-    for step, flip in enumerate(exchanges):
-        arrived = lax.ppermute(sent, "atoms", [(i, i ^ flip) for i in range(regions)])
+    exchanges = ((1, 1), (2, 8), (6, 24), (8, 2), (24, 6))
+    for step, flips in enumerate(exchanges):
+        arrived = lax.ppermute(sent, "atoms", [(i, i ^ flips[i % 2]) for i in range(regions)])
         if step + 1 < len(exchanges):
             factor = factor + arrived.astype(jnp.float32)
             sent = factor.astype(jnp.bfloat16)

time: 83 us -> 83 us (level)
  no operation moved by 1% of the time
where the time goes in v9:
time: 83 us; the launch traced here: 82.7 us
  waiting for transfers between devices  23.7 us (29%)
  starting transfers between devices  23.3 us (28%)
  blocking collectives  18.2 us (22%)
  Pallas kernels  15.8 us (19%)
    all_to_all x1, blocking collectives, from_others(): return lax.all_to_all(pieces, axis, 0, 0, tiled=True)  18.2 us
    ppermute x5, waiting for transfers between devices, local(): lax.ppermute(sent, 'atoms', [(i, i ^ flips[i % 2]) for i in range(regions)])  11.5 us
    ppermute x2, waiting for transfers between devices, shifted(): return lax.ppermute(cells, ('atoms', 'waves'), pairs_of)  10.9 us
    all_to_all x1, starting transfers between devices, from_others(): return lax.all_to_all(pieces, axis, 0, 0, tiled=True)  10.2 us
    ppermute x5, starting transfers between devices, local(): lax.ppermute(sent, 'atoms', [(i, i ^ flips[i % 2]) for i in range(regions)])  8.41 us
    pallas_call x1, Pallas kernels, pairs(): pl.pallas_call(functools.partial(pairs_kernel, float(regions), regions, u...  6.11 us
    pallas_call x1, Pallas kernels, structure(): pl.pallas_call(functools.partial(structure_kernel, scale, float(regions))...  6.11 us
    ppermute x2, starting transfers between devices, shifted(): return lax.ppermute(cells, ('atoms', 'waves'), pairs_of)  4.56 us
  transfers between devices with their start and end apart: 9, of which 8 were waited for; matrix products, arithmetic and copies ran while one was open for 0% of the time, Pallas kernels for 7%

profile of v9, /device:TPU:32, one launch (start us, length us, event | category | flops | bytes accessed | tf_op | source)
XLA Modules:
  0.0 82.7 jit_solution(11779761615097726935)
XLA Ops:
  0.7 0.1 pad_add_fusion.place_ref
  0.7 6.1 %structure.1 = (bf16[384,4096]{1,0:T(8,128)(2,1)S(1)}, bf16[128,4096]{1,0:T(8,128)(2,1)}, f32[256,128]{1,0:T(8,128)S(1)}, bf16[256,128]{1,0:T(8,128)(2,1)S(1)}, ...) custom-call(s32[2]{0:T(128)S(1)} %pad_add_fusion.place_ref, s32[1]{0:T(128)S(6)} %copy.13.count_ref, ...), custom_call_target="tpu_custom_call" | custom-call | tf_op jit(solution)/shard_map/structure/pallas_call | solution.py:150
  6.9 0.1 collective-permute-start
  7.0 1.2 %collective-permute-done = bf16[256,128]{1,0:T(8,128)(2,1)S(1)} collective-permute-done((bf16[256,128]{1,0:T(8,128)(2,1)S(1)}, bf16[256,128]{1,0:T(8,128)(2,1)S(1)}, u32[]{:S(2)}, u32[]{:S(2)}) %collective-permute-start) | collective-permute-done | bytes 65568 | tf_op jit(solution)/shard_map/ppermute | solution.py:454
  8.2 1.6 %collective-permute-start.1 = (bf16[256,128]{1,0:T(8,128)(2,1)S(1)}, bf16[256,128]{1,0:T(8,128)(2,1)S(1)}, u32[]{:S(2)}, u32[]{:S(2)}) collective-permute-start(bf16[256,128]{1,0:T(8,128)(2,1)S(1)} %fusion), channel_id=1, source_target_pairs={{0,16},{8,72},{16,0},{24,88},{32,48},{40,104},{48,32},{56,120},{64... | collective-permute-start | bytes 196616 | tf_op jit(solution)/shard_map/ppermute | solution.py:454
  9.8 2.8 %collective-permute-done.1 = bf16[256,128]{1,0:T(8,128)(2,1)S(1)} collective-permute-done((bf16[256,128]{1,0:T(8,128)(2,1)S(1)}, bf16[256,128]{1,0:T(8,128)(2,1)S(1)}, u32[]{:S(2)}, u32[]{:S(2)}) %collective-permute-start.1) | collective-permute-done | bytes 65568 | tf_op jit(solution)/shard_map/ppermute | solution.py:454
  12.6 2.8 %collective-permute-start.2 = (bf16[256,128]{1,0:T(8,128)(2,1)S(1)}, bf16[256,128]{1,0:T(8,128)(2,1)S(1)}, u32[]{:S(2)}, u32[]{:S(2)}) collective-permute-start(bf16[256,128]{1,0:T(8,128)(2,1)S(1)} %fusion.2), channel_id=1, source_target_pairs={{0,48},{8,200},{16,32},{24,216},{32,16},{40,232},{48,0},{56,248},{... | collective-permute-start | bytes 196616 | tf_op jit(solution)/shard_map/ppermute | solution.py:454
  15.4 2.7 %collective-permute-done.2 = bf16[256,128]{1,0:T(8,128)(2,1)S(1)} collective-permute-done((bf16[256,128]{1,0:T(8,128)(2,1)S(1)}, bf16[256,128]{1,0:T(8,128)(2,1)S(1)}, u32[]{:S(2)}, u32[]{:S(2)}) %collective-permute-start.2) | collective-permute-done | bytes 65568 | tf_op jit(solution)/shard_map/ppermute | solution.py:454
  18.2 0.0 copy-start.2
  18.2 0.0 copy-start
  18.2 0.0 copy-start.1
  18.2 1.9 %collective-permute-start.3 = (bf16[256,128]{1,0:T(8,128)(2,1)S(1)}, bf16[256,128]{1,0:T(8,128)(2,1)S(1)}, u32[]{:S(2)}, u32[]{:S(2)}) collective-permute-start(bf16[256,128]{1,0:T(8,128)(2,1)S(1)} %fusion.1), channel_id=1, source_target_pairs={{0,64},{8,24},{16,80},{24,8},{32,96},{40,56},{48,112},{56,40},{64,... | collective-permute-start | bytes 196616 | tf_op jit(solution)/shard_map/ppermute | solution.py:454
  20.1 2.5 %collective-permute-done.3 = bf16[256,128]{1,0:T(8,128)(2,1)S(1)} collective-permute-done((bf16[256,128]{1,0:T(8,128)(2,1)S(1)}, bf16[256,128]{1,0:T(8,128)(2,1)S(1)}, u32[]{:S(2)}, u32[]{:S(2)}) %collective-permute-start.3) | collective-permute-done | bytes 65568 | tf_op jit(solution)/shard_map/ppermute | solution.py:454
  22.7 2.0 %collective-permute-start.4 = (bf16[256,128]{1,0:T(8,128)(2,1)S(1)}, bf16[256,128]{1,0:T(8,128)(2,1)S(1)}, u32[]{:S(2)}, u32[]{:S(2)}) collective-permute-start(bf16[256,128]{1,0:T(8,128)(2,1)S(1)} %get-tuple-element.29), channel_id=1, source_target_pairs={{0,192},{8,56},{16,208},{24,40},{32,224},{40,24},{48,240},{56,8},{... | collective-permute-start | bytes 196616 | tf_op jit(solution)/shard_map/ppermute | solution.py:454
  24.7 2.4 %collective-permute-done.4.arrived_ref = bf16[256,128]{1,0:T(8,128)(2,1)S(1)} collective-permute-done((bf16[256,128]{1,0:T(8,128)(2,1)S(1)}, bf16[256,128]{1,0:T(8,128)(2,1)S(1)}, u32[]{:S(2)}, u32[]{:S(2)}) %collective-permute-start.4) | collective-permute-done | bytes 65568 | tf_op jit(solution)/shard_map/ppermute | solution.py:454
  27.0 0.5 spectral.1.own_ref
  27.5 0.1 collective-permute-start.5
  27.6 1.2 %collective-permute-done.5.other_ref = bf16[256,128]{1,0:T(8,128)(2,1)S(1)} collective-permute-done((bf16[256,128]{1,0:T(8,128)(2,1)S(1)}, bf16[256,128]{1,0:T(8,128)(2,1)S(1)}, u32[]{:S(2)}, u32[]{:S(2)}) %collective-permute-start.5) | collective-permute-done | bytes 65568 | tf_op jit(solution)/shard_map/ppermute | solution.py:461
  28.8 2.8 %potentials.1 = bf16[8,64,256]{2,1,0:T(8,128)(2,1)} custom-call(s32[2]{0:T(128)S(1)} %pad_add_fusion.place_ref, bf16[256,128]{1,0:T(8,128)(2,1)S(1)} %spectral.1.own_ref, bf16[256,128]{1,0:T(8,128)(2,1)S(1)} %collective-permute-done.5.other_ref, bf16[384,4096]{1,0:T(8,128)(2,1)S(1)} %get-tuple-element.21.low_ref, bf16[128,4096]{1,0:T(8,128)(2,1)} %get-tuple-element.22.high_in), custom_call_target="tpu_custom_call" | custom-call | tf_op jit(solution)/shard_map/potentials/pallas_call | solution.py:238
  31.6 10.2 %all-to-all-start = ((bf16[8,64,256]{2,1,0:T(8,128)(2,1)}), bf16[8,64,256]{2,1,0:T(8,128)(2,1)S(1)}, u32[]{:S(2)}, u32[]{:S(2)}) async-start(bf16[8,64,256]{2,1,0:T(8,128)(2,1)} %potentials.1), calls=%async_computation | async-start | bytes 524288 | tf_op jit(solution)/shard_map/all_to_all | solution.py:425
  41.8 0.0 copy-done.2
  41.8 4.6 %collective-permute-start.7 = (bf16[88,2048]{1,0:T(8,128)(2,1)S(1)}, bf16[88,2048]{1,0:T(8,128)(2,1)S(1)}, u32[]{:S(2)}, u32[]{:S(2)}) collective-permute-start(bf16[88,2048]{1,0:T(8,128)(2,1)S(1)} %copy-done.2), channel_id=1, source_target_pairs={{0,252},{1,253},{2,254},{3,255},{4,248},{5,249},{6,250},{7,251},{8... | collective-permute-start | bytes 1081352 | tf_op jit(solution)/shard_map/ppermute | solution.py:421
  46.4 0.0 collective-permute-start.6
  46.4 5.4 %collective-permute-done.7.next_in = bf16[88,2048]{1,0:T(8,128)(2,1)S(1)} collective-permute-done((bf16[88,2048]{1,0:T(8,128)(2,1)S(1)}, bf16[88,2048]{1,0:T(8,128)(2,1)S(1)}, u32[]{:S(2)}, u32[]{:S(2)}) %collective-permute-start.7) | collective-permute-done | bytes 360480 | tf_op jit(solution)/shard_map/ppermute | solution.py:421
  51.8 5.5 %collective-permute-done.6.prev_in = bf16[88,2048]{1,0:T(8,128)(2,1)S(1)} collective-permute-done((bf16[88,2048]{1,0:T(8,128)(2,1)S(1)}, bf16[88,2048]{1,0:T(8,128)(2,1)S(1)}, u32[]{:S(2)}, u32[]{:S(2)}) %collective-permute-start.6) | collective-permute-done | bytes 360480 | tf_op jit(solution)/shard_map/ppermute | solution.py:421
  57.3 0.0 copy-done
  57.3 0.0 copy-done.1
  57.3 6.1 %pairs.1 = (f32[128,256]{1,0:T(8,128)S(1)}, bf16[64,256]{1,0:T(8,128)(2,1)S(1)}, f32[8,256]{1,0:T(8,128)S(1)}, bf16[128,64]{1,0:T(8,128)(2,1)S(1)}, bf16[64,128]{1,0:T(8,128)(2,1)S(1)}) custom-call(s32[2]{0:T(128)S(1)} %pad_add_fusion.place_ref, s32[1]{0:T(128)S(6)} %copy.13.count_ref, s32[16,27]{1,0:T(8,128)S(1)} %bitcast.13, s32[16,27]{1,0:T(8,128)S(1)} %bitcast.14, ...), custom_call_target="tpu_custom_call" | custom-call | flops 130940928 | bytes 1081344 | tf_op jit(solution)/shard_map/pairs/pallas_call | solution.py:355
  63.4 0.0 all-to-all-done.arrived_ref
  63.5 0.3 update.1
  63.8 18.2 %all_to_all.10 = bf16[8,64,256]{2,1,0:T(8,128)(2,1)S(1)} all-to-all(bf16[8,64,256]{2,1,0:T(8,128)(2,1)S(1)} %update.1), channel_id=1, replica_groups=mesh['atoms'=32,'waves'=8] {'waves'}, dimensions={0} | all-to-all | bytes 524288 | tf_op jit(solution)/shard_map/all_to_all | solution.py:425
  82.0 0.7 copy.12
  (4 shorter events, 0.1 us)
Async XLA Ops:
  6.9 1.3 %collective-permute-start = (bf16[256,128]{1,0:T(8,128)(2,1)S(1)}, bf16[256,128]{1,0:T(8,128)(2,1)S(1)}, u32[]{:S(2)}, u32[]{:S(2)}) collective-permute-start(bf16[256,128]{1,0:T(8,128)(2,1)S(1)} %get-tuple-element.18), channel_id=1, source_target_pairs={{0,8},{8,0},{16,24},{24,16},{32,40},{40,32},{48,56},{56,48},{64,72... | collective-permute-start | bytes 196616 | tf_op jit(solution)/shard_map/ppermute | solution.py:454
  8.2 4.4 %collective-permute-start.1 = (bf16[256,128]{1,0:T(8,128)(2,1)S(1)}, bf16[256,128]{1,0:T(8,128)(2,1)S(1)}, u32[]{:S(2)}, u32[]{:S(2)}) collective-permute-start(bf16[256,128]{1,0:T(8,128)(2,1)S(1)} %fusion), channel_id=1, source_target_pairs={{0,16},{8,72},{16,0},{24,88},{32,48},{40,104},{48,32},{56,120},{64... | collective-permute-start | bytes 196616 | tf_op jit(solution)/shard_map/ppermute | solution.py:454
  12.6 5.6 %collective-permute-start.2 = (bf16[256,128]{1,0:T(8,128)(2,1)S(1)}, bf16[256,128]{1,0:T(8,128)(2,1)S(1)}, u32[]{:S(2)}, u32[]{:S(2)}) collective-permute-start(bf16[256,128]{1,0:T(8,128)(2,1)S(1)} %fusion.2), channel_id=1, source_target_pairs={{0,48},{8,200},{16,32},{24,216},{32,16},{40,232},{48,0},{56,248},{... | collective-permute-start | bytes 196616 | tf_op jit(solution)/shard_map/ppermute | solution.py:454
  18.2 23.6 %copy-start.2 = (bf16[88,2048]{1,0:T(8,128)(2,1)S(1)}, bf16[88,2048]{1,0:T(8,128)(2,1)}, u32[]{:S(2)}) copy-start(bf16[88,2048]{1,0:T(8,128)(2,1)} %get-tuple-element.23.own_in) | copy-start | bytes 1081348
  18.2 39.1 %copy-start = (s32[27,16]{0,1:T(8,128)S(1)}, s32[27,16]{0,1:T(8,128)}, u32[]{:S(2)}) copy-start(s32[27,16]{0,1:T(8,128)} %param.12) | copy-start | bytes 5188
  18.2 39.1 %copy-start.1 = (s32[27,16]{0,1:T(8,128)S(1)}, s32[27,16]{0,1:T(8,128)}, u32[]{:S(2)}) copy-start(s32[27,16]{0,1:T(8,128)} %param.13) | copy-start | bytes 5188
  18.2 4.4 %collective-permute-start.3 = (bf16[256,128]{1,0:T(8,128)(2,1)S(1)}, bf16[256,128]{1,0:T(8,128)(2,1)S(1)}, u32[]{:S(2)}, u32[]{:S(2)}) collective-permute-start(bf16[256,128]{1,0:T(8,128)(2,1)S(1)} %fusion.1), channel_id=1, source_target_pairs={{0,64},{8,24},{16,80},{24,8},{32,96},{40,56},{48,112},{56,40},{64,... | collective-permute-start | bytes 196616 | tf_op jit(solution)/shard_map/ppermute | solution.py:454
  22.7 4.4 %collective-permute-start.4 = (bf16[256,128]{1,0:T(8,128)(2,1)S(1)}, bf16[256,128]{1,0:T(8,128)(2,1)S(1)}, u32[]{:S(2)}, u32[]{:S(2)}) collective-permute-start(bf16[256,128]{1,0:T(8,128)(2,1)S(1)} %get-tuple-element.29), channel_id=1, source_target_pairs={{0,192},{8,56},{16,208},{24,40},{32,224},{40,24},{48,240},{56,8},{... | collective-permute-start | bytes 196616 | tf_op jit(solution)/shard_map/ppermute | solution.py:454
  27.5 1.3 %collective-permute-start.5 = (bf16[256,128]{1,0:T(8,128)(2,1)S(1)}, bf16[256,128]{1,0:T(8,128)(2,1)S(1)}, u32[]{:S(2)}, u32[]{:S(2)}) collective-permute-start(bf16[256,128]{1,0:T(8,128)(2,1)S(1)} %spectral.1.own_ref), channel_id=1, source_target_pairs={{0,8},{8,0},{16,24},{24,16},{32,40},{40,32},{48,56},{56,48},{64,72... | collective-permute-start | bytes 196616 | tf_op jit(solution)/shard_map/ppermute | solution.py:461
  31.6 31.8 %all-to-all-start = ((bf16[8,64,256]{2,1,0:T(8,128)(2,1)}), bf16[8,64,256]{2,1,0:T(8,128)(2,1)S(1)}, u32[]{:S(2)}, u32[]{:S(2)}) async-start(bf16[8,64,256]{2,1,0:T(8,128)(2,1)} %potentials.1), calls=%async_computation | async-start | bytes 524288 | tf_op jit(solution)/shard_map/all_to_all | solution.py:425
  41.8 10.0 %collective-permute-start.7 = (bf16[88,2048]{1,0:T(8,128)(2,1)S(1)}, bf16[88,2048]{1,0:T(8,128)(2,1)S(1)}, u32[]{:S(2)}, u32[]{:S(2)}) collective-permute-start(bf16[88,2048]{1,0:T(8,128)(2,1)S(1)} %copy-done.2), channel_id=1, source_target_pairs={{0,252},{1,253},{2,254},{3,255},{4,248},{5,249},{6,250},{7,251},{8... | collective-permute-start | bytes 1081352 | tf_op jit(solution)/shard_map/ppermute | solution.py:421
  46.4 10.9 %collective-permute-start.6 = (bf16[88,2048]{1,0:T(8,128)(2,1)S(1)}, bf16[88,2048]{1,0:T(8,128)(2,1)S(1)}, u32[]{:S(2)}, u32[]{:S(2)}) collective-permute-start(bf16[88,2048]{1,0:T(8,128)(2,1)S(1)} %copy-done.2), channel_id=1, source_target_pairs={{0,8},{1,9},{2,10},{3,11},{4,12},{5,13},{6,14},{7,15},{8,16},{9,17... | collective-permute-start | bytes 1081352 | tf_op jit(solution)/shard_map/ppermute | solution.py:421

commit v10 on v9

--- a/solution.py
+++ b/solution.py
@@ -52,15 +52,11 @@
 def structure_kernel(
     scale, regions, place_ref, count_ref, kvec_in, coords_in, h_in, weight_in, mixing_in,
     low_ref, high_out, kept_ref, sent_ref, carry_out, gain_ref, mixing_ref,
-    kvec_ref, coords_ref, h_ref, weight_ref, ka_ref, masked_ref, high_ref, carry_ref, whole_ref, gains_ref, in_sems, sems,
+    kvec_ref, coords_ref, h_ref, weight_ref, ka_ref, masked_ref, high_ref, carry_ref, in_sems, sems,
 ):
     waves = kvec_ref.shape[1]
     chans, atoms = h_ref.shape
     kept = low_ref.shape[0]
-    half = kept_ref.shape[0]
-    core = jnp.bitwise_and(place_ref[0], 1)
-    mine = pl.ds(pl.multiple_of(core * half, half), half)
-    theirs = pl.ds(pl.multiple_of((1 - core) * half, half), half)
     f32 = dict(preferred_element_type=jnp.float32)
     taken = [
         pltpu.make_async_copy(source, target, in_sems.at[at])
@@ -84,8 +80,7 @@
     kx = kf[0:1] / regions
     gain = GAIN_TOP / (4.0 + kx * kx + kf[1:2] * kf[1:2] + kf[2:3] * kf[2:3])
     columns = jnp.broadcast_to(gain * scale, (8, waves)).T
-    gains_ref[...] = jnp.broadcast_to(columns[:, 0:1], gains_ref.shape)
-    gain_ref[...] = gains_ref[mine, :]
+    gain_ref[...] = jnp.broadcast_to(columns[:, 0:1], gain_ref.shape)
     taken[1].wait()
     pieces = three_pieces(coords_ref[...])
     ones, gap = jnp.ones((3, atoms), jnp.float32), jnp.zeros((2, atoms), jnp.float32)
@@ -108,7 +103,9 @@
         term = term + lax.dot_general(sinv, jnp.concatenate([zero, ht], axis=0), NT, **f32)
         sums[row] = term if start == 0 else sums[row] + term
         if start + TILE == atoms:
-            whole_ref[row : row + ROWS, :] = sums.pop(row)
+            whole = sums.pop(row)
+            kept_ref[row : row + ROWS, :] = whole
+            sent_ref[row : row + ROWS, :] = whole.astype(jnp.bfloat16)
 
     pending = []
     copies = []
@@ -134,8 +131,6 @@
             if len(pending) > 1:
                 add_up(*pending.pop(0))
     add_up(*pending.pop(0))
-    kept_ref[...] = whole_ref[mine, :]
-    sent_ref[...] = whole_ref[theirs, :].astype(jnp.bfloat16)
     for copy in copies:
         copy.wait()
 
@@ -152,10 +147,10 @@
         out_shape=(
             jax.ShapeDtypeStruct((kept, 2 * atoms), jnp.bfloat16),
             pltpu.HBM((waves - kept, 2 * atoms), jnp.bfloat16),
-            jax.ShapeDtypeStruct((waves // 2, 2 * chans), jnp.float32),
-            jax.ShapeDtypeStruct((waves // 2, 2 * chans), jnp.bfloat16),
+            jax.ShapeDtypeStruct((waves, 2 * chans), jnp.float32),
+            jax.ShapeDtypeStruct((waves, 2 * chans), jnp.bfloat16),
             pltpu.HBM((chans + 24, atoms), jnp.bfloat16),
-            jax.ShapeDtypeStruct((waves // 2, 2 * chans), jnp.float32),
+            jax.ShapeDtypeStruct((waves, 2 * chans), jnp.float32),
             jax.ShapeDtypeStruct(mixing.shape, jnp.float32),
         ),
         in_specs=[SMEM_SPEC] * 2 + [HBM_SPEC] * 5,
@@ -169,8 +164,6 @@
             pltpu.VMEM(h.shape, jnp.bfloat16),
             pltpu.VMEM((waves - kept, 2 * atoms), jnp.bfloat16),
             pltpu.VMEM((chans + 24, atoms), jnp.bfloat16),
-            pltpu.VMEM((waves, 2 * chans), jnp.float32),
-            pltpu.VMEM((waves, 2 * chans), jnp.float32),
             pltpu.SemaphoreType.DMA((5,)),
             pltpu.SemaphoreType.DMA((2,)),
         ],
@@ -201,19 +194,18 @@
 
 
 def potentials_kernel(
-    place_ref, own_ref, other_ref, low_ref, high_in, out_ref, filtered_ref, high_ref, across_ref, sum_ref, sem,
+    place_ref, own_ref, other_ref, low_ref, high_in, out_ref, high_ref, across_ref, sum_ref, sem,
 ):
     chans = out_ref.shape[1]
     pieces, _, width = out_ref.shape
     atoms = pieces * width
-    kept, waves = low_ref.shape[0], filtered_ref.shape[0]
+    kept, waves = low_ref.shape[0], own_ref.shape[0]
     copy = pltpu.make_async_copy(high_in, high_ref, sem)
     copy.start()
-    half = own_ref.shape[0]
-    core = jnp.bitwise_and(place_ref[0], 1)
-    filtered_ref[pl.ds(pl.multiple_of(core * half, half), half), :] = own_ref[...]
-    filtered_ref[pl.ds(pl.multiple_of((1 - core) * half, half), half), :] = other_ref[...]
-    across_ref[...] = filtered_ref[...].astype(jnp.float32).T.astype(jnp.bfloat16)
+    filtered = jnp.where(
+        jnp.bitwise_and(place_ref[0], 1) == 1, own_ref[...].astype(jnp.float32), other_ref[...].astype(jnp.float32)
+    )
+    across_ref[...] = filtered.T.astype(jnp.bfloat16)
 
     def term(rows, table, piece):
         cos_span = slice(piece * width, (piece + 1) * width)
@@ -233,7 +225,7 @@
 
 def potentials(place, own, other, low, high, pieces):
     chans = own.shape[1] // 2
-    waves = 2 * own.shape[0]
+    waves = own.shape[0]
     atoms = low.shape[1] // 2
     return pl.pallas_call(
         potentials_kernel,
@@ -241,7 +233,6 @@
         in_specs=[SMEM_SPEC, VMEM_SPEC, VMEM_SPEC, VMEM_SPEC, HBM_SPEC],
         out_specs=VMEM_SPEC,
         scratch_shapes=[
-            pltpu.VMEM((waves, 2 * chans), jnp.bfloat16),
             pltpu.VMEM(high.shape, jnp.bfloat16),
             pltpu.VMEM((2 * chans, waves), jnp.bfloat16),
             pltpu.VMEM((pieces, chans, atoms // pieces), jnp.float32),
@@ -449,16 +440,18 @@
     low, high, factor, sent, carry, gain_rows, mixing = structure(
         place, block_count, kvec, coords, features, msg_weight[0], filter_weight[0], 1.0 / math.sqrt(total), regions
     )
-    exchanges = ((1, 1), (2, 8), (6, 24), (8, 2), (24, 6))
-    for step, flips in enumerate(exchanges):
-        arrived = lax.ppermute(sent, "atoms", [(i, i ^ flips[i % 2]) for i in range(regions)])
+    first_cores, second_cores = range(0, regions, 2), range(1, regions, 2)
+    exchanges = [[(i, i + 1) for i in first_cores]]
+    exchanges += [[(i, i ^ flip) for i in second_cores] for flip in (2, 6, 8, 24)]
+    for step, exchange in enumerate(exchanges):
+        arrived = lax.ppermute(sent, "atoms", exchange)
         if step + 1 < len(exchanges):
             factor = factor + arrived.astype(jnp.float32)
             sent = factor.astype(jnp.bfloat16)
     prev = shifted(carry, regions, groups_waves, 1)
     following = shifted(carry, regions, groups_waves, -1)
     filtered = spectral(factor, arrived, gain_rows, mixing)
-    other = lax.ppermute(filtered, "atoms", [(i, i ^ 1) for i in range(regions)])
+    other = lax.ppermute(filtered, "atoms", [(i, i - 1) for i in second_cores])
     partial_potential = potentials(place, filtered, other, low, high, groups_waves)
     potential = from_others(partial_potential, "waves")
     known = pairs(

time: 83 us -> 91.6 us (1.10)
  waiting for transfers between devices: 23.7 us -> 34.7 us
  starting transfers between devices: 23.3 us -> 20.3 us
    ppermute x6, waiting for transfers between devices: 12.8 us -> 23.8 us  [the longest x1 22.9 us: local(): other = lax.ppermute(filtered, 'atoms', [(i, i - 1) for i in second_cores])]
    ppermute x6, starting transfers between devices: 8.5 us -> 5.84 us  [the longest x5 4.55 us: local(): arrived = lax.ppermute(sent, 'atoms', exchange)]
  transfers between devices with their start and end apart: 9 -> 9, of which waited for: 8 -> 4; matrix products, arithmetic and copies ran while one was open for 0% -> 0% of each run, Pallas kernels for 7% -> 7%
where the time goes in v10:
time: 91.6 us; the launch traced here: 91.1 us
  waiting for transfers between devices  34.7 us (38%)
  starting transfers between devices  20.3 us (22%)
  blocking collectives  18.2 us (20%)
  Pallas kernels  16 us (17%)
    ppermute x1, waiting for transfers between devices, local(): other = lax.ppermute(filtered, 'atoms', [(i, i - 1) for i in second_cores])  22.9 us
    all_to_all x1, blocking collectives, from_others(): return lax.all_to_all(pieces, axis, 0, 0, tiled=True)  18.2 us
    ppermute x2, waiting for transfers between devices, shifted(): return lax.ppermute(cells, ('atoms', 'waves'), pairs_of)  10.9 us
    all_to_all x1, starting transfers between devices, from_others(): return lax.all_to_all(pieces, axis, 0, 0, tiled=True)  9.85 us
    pallas_call x1, Pallas kernels, pairs(): pl.pallas_call(functools.partial(pairs_kernel, float(regions), regions, u...  6.12 us
    pallas_call x1, Pallas kernels, structure(): pl.pallas_call(functools.partial(structure_kernel, scale, float(regions))...  6.08 us
    ppermute x2, starting transfers between devices, shifted(): return lax.ppermute(cells, ('atoms', 'waves'), pairs_of)  4.6 us
    ppermute x5, starting transfers between devices, local(): arrived = lax.ppermute(sent, 'atoms', exchange)  4.55 us
  transfers between devices with their start and end apart: 9, of which 4 were waited for; matrix products, arithmetic and copies ran while one was open for 0% of the time, Pallas kernels for 7%

profile of v10, /device:TPU:32, one launch (start us, length us, event | category | flops | bytes accessed | tf_op | source)
XLA Modules:
  0.0 91.1 jit_solution(8140124237006079100)
XLA Ops:
  0.7 0.1 pad_add_fusion.place_ref
  0.7 6.1 %structure.1 = (bf16[384,4096]{1,0:T(8,128)(2,1)S(1)}, bf16[128,4096]{1,0:T(8,128)(2,1)}, f32[512,128]{1,0:T(8,128)S(1)}, bf16[512,128]{1,0:T(8,128)(2,1)S(1)}, ...) custom-call(s32[2]{0:T(128)S(1)} %pad_add_fusion.place_ref, s32[1]{0:T(128)S(6)} %copy.13.count_ref, ...), custom_call_target="tpu_custom_call" | custom-call | tf_op jit(solution)/shard_map/structure/pallas_call | solution.py:145
  6.8 1.7 %collective-permute-start = (bf16[512,128]{1,0:T(8,128)(2,1)S(1)}, bf16[512,128]{1,0:T(8,128)(2,1)S(1)}, u32[]{:S(2)}, u32[]{:S(2)}) collective-permute-start(bf16[512,128]{1,0:T(8,128)(2,1)S(1)} %get-tuple-element.18), channel_id=1, source_target_pairs={{0,8},{16,24},{32,40},{48,56},{64,72},{80,88},{96,104},{112,120},{... | collective-permute-start | bytes 393224 | tf_op jit(solution)/shard_map/ppermute | solution.py:447
  8.6 1.0 %collective-permute-done = bf16[512,128]{1,0:T(8,128)(2,1)S(1)} collective-permute-done((bf16[512,128]{1,0:T(8,128)(2,1)S(1)}, bf16[512,128]{1,0:T(8,128)(2,1)S(1)}, u32[]{:S(2)}, u32[]{:S(2)}) %collective-permute-start) | collective-permute-done | bytes 131104 | tf_op jit(solution)/shard_map/ppermute | solution.py:447
  9.6 0.7 collective-permute-start.1
  10.2 0.0 collective-permute-done.1
  10.3 0.1 fusion.2
  10.3 0.7 collective-permute-start.2
  11.0 0.0 collective-permute-done.2
  11.0 0.1 fusion.1
  11.1 0.7 collective-permute-start.3
  11.7 0.0 collective-permute-done.3
  11.8 0.1 fusion.3
  11.9 0.0 copy-start.2
  11.9 0.0 copy-start
  11.9 0.0 copy-start.1
  11.9 0.8 collective-permute-start.4
  12.7 0.0 collective-permute-done.4.arrived_ref
  12.7 0.7 spectral.1.own_ref
  13.4 1.3 %collective-permute-start.5 = (bf16[512,128]{1,0:T(8,128)(2,1)S(1)}, bf16[512,128]{1,0:T(8,128)(2,1)S(1)}, u32[]{:S(2)}, u32[]{:S(2)}) collective-permute-start(bf16[512,128]{1,0:T(8,128)(2,1)S(1)} %spectral.1.own_ref), channel_id=1, source_target_pairs={{8,0},{24,16},{40,32},{56,48},{72,64},{88,80},{104,96},{120,112},{... | collective-permute-start | bytes 393224 | tf_op jit(solution)/shard_map/ppermute | solution.py:454
  14.7 22.9 %collective-permute-done.5.other_ref = bf16[512,128]{1,0:T(8,128)(2,1)S(1)} collective-permute-done((bf16[512,128]{1,0:T(8,128)(2,1)S(1)}, bf16[512,128]{1,0:T(8,128)(2,1)S(1)}, u32[]{:S(2)}, u32[]{:S(2)}) %collective-permute-start.5) | collective-permute-done | bytes 131104 | tf_op jit(solution)/shard_map/ppermute | solution.py:454
  37.6 2.8 %potentials.1 = bf16[8,64,256]{2,1,0:T(8,128)(2,1)} custom-call(s32[2]{0:T(128)S(1)} %pad_add_fusion.place_ref, bf16[512,128]{1,0:T(8,128)(2,1)S(1)} %spectral.1.own_ref, bf16[512,128]{1,0:T(8,128)(2,1)S(1)} %collective-permute-done.5.other_ref, bf16[384,4096]{1,0:T(8,128)(2,1)S(1)} %get-tuple-element.21.low_ref, bf16[128,4096]{1,0:T(8,128)(2,1)} %get-tuple-element.22.high_in), custom_call_target="tpu_custom_call" | custom-call | tf_op jit(solution)/shard_map/potentials/pallas_call | solution.py:230
  40.3 9.8 %all-to-all-start = ((bf16[8,64,256]{2,1,0:T(8,128)(2,1)}), bf16[8,64,256]{2,1,0:T(8,128)(2,1)S(1)}, u32[]{:S(2)}, u32[]{:S(2)}) async-start(bf16[8,64,256]{2,1,0:T(8,128)(2,1)} %potentials.1), calls=%async_computation | async-start | bytes 524288 | tf_op jit(solution)/shard_map/all_to_all | solution.py:416
  50.2 0.0 copy-done.2
  50.2 4.6 %collective-permute-start.7 = (bf16[88,2048]{1,0:T(8,128)(2,1)S(1)}, bf16[88,2048]{1,0:T(8,128)(2,1)S(1)}, u32[]{:S(2)}, u32[]{:S(2)}) collective-permute-start(bf16[88,2048]{1,0:T(8,128)(2,1)S(1)} %copy-done.2), channel_id=1, source_target_pairs={{0,252},{1,253},{2,254},{3,255},{4,248},{5,249},{6,250},{7,251},{8... | collective-permute-start | bytes 1081352 | tf_op jit(solution)/shard_map/ppermute | solution.py:412
  54.8 0.0 collective-permute-start.6
  54.8 5.4 %collective-permute-done.7.next_in = bf16[88,2048]{1,0:T(8,128)(2,1)S(1)} collective-permute-done((bf16[88,2048]{1,0:T(8,128)(2,1)S(1)}, bf16[88,2048]{1,0:T(8,128)(2,1)S(1)}, u32[]{:S(2)}, u32[]{:S(2)}) %collective-permute-start.7) | collective-permute-done | bytes 360480 | tf_op jit(solution)/shard_map/ppermute | solution.py:412
  60.2 5.5 %collective-permute-done.6.prev_in = bf16[88,2048]{1,0:T(8,128)(2,1)S(1)} collective-permute-done((bf16[88,2048]{1,0:T(8,128)(2,1)S(1)}, bf16[88,2048]{1,0:T(8,128)(2,1)S(1)}, u32[]{:S(2)}, u32[]{:S(2)}) %collective-permute-start.6) | collective-permute-done | bytes 360480 | tf_op jit(solution)/shard_map/ppermute | solution.py:412
  65.7 0.0 copy-done
  65.7 0.0 copy-done.1
  65.7 6.1 %pairs.1 = (f32[128,256]{1,0:T(8,128)S(1)}, bf16[64,256]{1,0:T(8,128)(2,1)S(1)}, f32[8,256]{1,0:T(8,128)S(1)}, bf16[128,64]{1,0:T(8,128)(2,1)S(1)}, bf16[64,128]{1,0:T(8,128)(2,1)S(1)}) custom-call(s32[2]{0:T(128)S(1)} %pad_add_fusion.place_ref, s32[1]{0:T(128)S(6)} %copy.13.count_ref, s32[16,27]{1,0:T(8,128)S(1)} %bitcast.13, s32[16,27]{1,0:T(8,128)S(1)} %bitcast.14, ...), custom_call_target="tpu_custom_call" | custom-call | flops 130940928 | bytes 1081344 | tf_op jit(solution)/shard_map/pairs/pallas_call | solution.py:346
  71.8 0.0 all-to-all-done.arrived_ref
  71.8 0.3 update.1
  72.2 18.2 %all_to_all.10 = bf16[8,64,256]{2,1,0:T(8,128)(2,1)S(1)} all-to-all(bf16[8,64,256]{2,1,0:T(8,128)(2,1)S(1)} %update.1), channel_id=1, replica_groups=mesh['atoms'=32,'waves'=8] {'waves'}, dimensions={0} | all-to-all | bytes 524288 | tf_op jit(solution)/shard_map/all_to_all | solution.py:416
  90.4 0.7 copy.12
  (1 shorter events, 0.0 us)
Async XLA Ops:
  6.8 2.7 %collective-permute-start = (bf16[512,128]{1,0:T(8,128)(2,1)S(1)}, bf16[512,128]{1,0:T(8,128)(2,1)S(1)}, u32[]{:S(2)}, u32[]{:S(2)}) collective-permute-start(bf16[512,128]{1,0:T(8,128)(2,1)S(1)} %get-tuple-element.18), channel_id=1, source_target_pairs={{0,8},{16,24},{32,40},{48,56},{64,72},{80,88},{96,104},{112,120},{... | collective-permute-start | bytes 393224 | tf_op jit(solution)/shard_map/ppermute | solution.py:447
  9.6 0.7 collective-permute-start.1
  10.3 0.7 collective-permute-start.2
  11.1 0.7 collective-permute-start.3
  11.9 38.3 %copy-start.2 = (bf16[88,2048]{1,0:T(8,128)(2,1)S(1)}, bf16[88,2048]{1,0:T(8,128)(2,1)}, u32[]{:S(2)}) copy-start(bf16[88,2048]{1,0:T(8,128)(2,1)} %get-tuple-element.23.own_in) | copy-start | bytes 1081348
  11.9 53.8 %copy-start = (s32[27,16]{0,1:T(8,128)S(1)}, s32[27,16]{0,1:T(8,128)}, u32[]{:S(2)}) copy-start(s32[27,16]{0,1:T(8,128)} %param.12) | copy-start | bytes 5188
  11.9 53.8 %copy-start.1 = (s32[27,16]{0,1:T(8,128)S(1)}, s32[27,16]{0,1:T(8,128)}, u32[]{:S(2)}) copy-start(s32[27,16]{0,1:T(8,128)} %param.13) | copy-start | bytes 5188
  11.9 0.8 collective-permute-start.4
  13.4 24.2 %collective-permute-start.5 = (bf16[512,128]{1,0:T(8,128)(2,1)S(1)}, bf16[512,128]{1,0:T(8,128)(2,1)S(1)}, u32[]{:S(2)}, u32[]{:S(2)}) collective-permute-start(bf16[512,128]{1,0:T(8,128)(2,1)S(1)} %spectral.1.own_ref), channel_id=1, source_target_pairs={{8,0},{24,16},{40,32},{56,48},{72,64},{88,80},{104,96},{120,112},{... | collective-permute-start | bytes 393224 | tf_op jit(solution)/shard_map/ppermute | solution.py:454
  40.3 31.5 %all-to-all-start = ((bf16[8,64,256]{2,1,0:T(8,128)(2,1)}), bf16[8,64,256]{2,1,0:T(8,128)(2,1)S(1)}, u32[]{:S(2)}, u32[]{:S(2)}) async-start(bf16[8,64,256]{2,1,0:T(8,128)(2,1)} %potentials.1), calls=%async_computation | async-start | bytes 524288 | tf_op jit(solution)/shard_map/all_to_all | solution.py:416
  50.2 10.0 %collective-permute-start.7 = (bf16[88,2048]{1,0:T(8,128)(2,1)S(1)}, bf16[88,2048]{1,0:T(8,128)(2,1)S(1)}, u32[]{:S(2)}, u32[]{:S(2)}) collective-permute-start(bf16[88,2048]{1,0:T(8,128)(2,1)S(1)} %copy-done.2), channel_id=1, source_target_pairs={{0,252},{1,253},{2,254},{3,255},{4,248},{5,249},{6,250},{7,251},{8... | collective-permute-start | bytes 1081352 | tf_op jit(solution)/shard_map/ppermute | solution.py:412
  54.8 10.9 %collective-permute-start.6 = (bf16[88,2048]{1,0:T(8,128)(2,1)S(1)}, bf16[88,2048]{1,0:T(8,128)(2,1)S(1)}, u32[]{:S(2)}, u32[]{:S(2)}) collective-permute-start(bf16[88,2048]{1,0:T(8,128)(2,1)S(1)} %copy-done.2), channel_id=1, source_target_pairs={{0,8},{1,9},{2,10},{3,11},{4,12},{5,13},{6,14},{7,15},{8,16},{9,17... | collective-permute-start | bytes 1081352 | tf_op jit(solution)/shard_map/ppermute | solution.py:412

commit v11 on v8

--- a/solution.py
+++ b/solution.py
@@ -50,7 +50,7 @@
 
 
 def structure_kernel(
-    scale, regions, place_ref, count_ref, kvec_in, coords_in, h_in, weight_in, mixing_in,
+    scale, regions, count_ref, kvec_in, coords_in, h_in, weight_in, mixing_in,
     low_ref, high_out, kept_ref, sent_ref, carry_out, gain_ref, mixing_ref,
     kvec_ref, coords_ref, h_ref, weight_ref, ka_ref, masked_ref, high_ref, carry_ref, whole_ref, gains_ref, in_sems, sems,
 ):
@@ -58,7 +58,7 @@
     chans, atoms = h_ref.shape
     kept = low_ref.shape[0]
     half = kept_ref.shape[0]
-    core = jnp.bitwise_and(place_ref[0], 1)
+    core = jnp.bitwise_and(lax.axis_index("atoms"), 1)
     mine = pl.ds(pl.multiple_of(core * half, half), half)
     theirs = pl.ds(pl.multiple_of((1 - core) * half, half), half)
     f32 = dict(preferred_element_type=jnp.float32)
@@ -144,7 +144,7 @@
     return tuple(pltpu.with_memory_space_constraint(array, pltpu.HBM) for array in arrays)
 
 
-def structure(place, count, kvec, coords, h, weight, mixing, scale, regions):
+def structure(count, kvec, coords, h, weight, mixing, scale, regions):
     waves, atoms, chans = kvec.shape[1], coords.shape[1], h.shape[0]
     kept = kept_rows(waves)
     return pl.pallas_call(
@@ -158,7 +158,7 @@
             jax.ShapeDtypeStruct((waves // 2, 2 * chans), jnp.float32),
             jax.ShapeDtypeStruct(mixing.shape, jnp.float32),
         ),
-        in_specs=[SMEM_SPEC] * 2 + [HBM_SPEC] * 5,
+        in_specs=[SMEM_SPEC] + [HBM_SPEC] * 5,
         out_specs=(VMEM_SPEC, HBM_SPEC, VMEM_SPEC, VMEM_SPEC, HBM_SPEC, VMEM_SPEC, VMEM_SPEC),
         scratch_shapes=[
             pltpu.VMEM(kvec.shape, jnp.int32),
@@ -176,7 +176,7 @@
         ],
         compiler_params=PARAMS,
         name="structure",
-    )(place, count, *in_hbm(kvec, coords, h, weight, mixing))
+    )(count, *in_hbm(kvec, coords, h, weight, mixing))
 
 
 def spectral_kernel(kept_ref, arrived_ref, gain_ref, mixing_ref, out_ref):
@@ -201,7 +201,7 @@
 
 
 def potentials_kernel(
-    place_ref, own_ref, other_ref, low_ref, high_in, out_ref, filtered_ref, high_ref, across_ref, sum_ref, sem,
+    own_ref, other_ref, low_ref, high_in, out_ref, filtered_ref, high_ref, across_ref, sum_ref, sem,
 ):
     chans = out_ref.shape[1]
     pieces, _, width = out_ref.shape
@@ -210,7 +210,7 @@
     copy = pltpu.make_async_copy(high_in, high_ref, sem)
     copy.start()
     half = own_ref.shape[0]
-    core = jnp.bitwise_and(place_ref[0], 1)
+    core = jnp.bitwise_and(lax.axis_index("atoms"), 1)
     filtered_ref[pl.ds(pl.multiple_of(core * half, half), half), :] = own_ref[...]
     filtered_ref[pl.ds(pl.multiple_of((1 - core) * half, half), half), :] = other_ref[...]
     across_ref[...] = filtered_ref[...].astype(jnp.float32).T.astype(jnp.bfloat16)
@@ -231,14 +231,14 @@
         out_ref[piece] = (whole * (1.0 / math.sqrt(K))).astype(jnp.bfloat16)
 
 
-def potentials(place, own, other, low, high, pieces):
+def potentials(own, other, low, high, pieces):
     chans = own.shape[1] // 2
     waves = 2 * own.shape[0]
     atoms = low.shape[1] // 2
     return pl.pallas_call(
         potentials_kernel,
         out_shape=jax.ShapeDtypeStruct((pieces, chans, atoms // pieces), jnp.bfloat16),
-        in_specs=[SMEM_SPEC, VMEM_SPEC, VMEM_SPEC, VMEM_SPEC, HBM_SPEC],
+        in_specs=[VMEM_SPEC, VMEM_SPEC, VMEM_SPEC, HBM_SPEC],
         out_specs=VMEM_SPEC,
         scratch_shapes=[
             pltpu.VMEM((waves, 2 * chans), jnp.bfloat16),
@@ -249,11 +249,11 @@
         ],
         compiler_params=PARAMS,
         name="potentials",
-    )(place, own, other, low, *in_hbm(high))
+    )(own, other, low, *in_hbm(high))
 
 
 def pairs_kernel(
-    scale_x, regions, unroll, place_ref, count_ref, idx_ref, live_ref, prev_in, next_in, own_in, h_in, first_in, second_in,
+    scale_x, regions, unroll, count_ref, idx_ref, live_ref, prev_in, next_in, own_in, h_in, first_in, second_in,
     inner_ref, share_ref, alive_ref, third_ref, second_ref,
     ext_ref, first_ref, own_ref, pos_ref, weights_ref, near_ref, sum_ref, sems,
 ):
@@ -262,8 +262,8 @@
     nblocks = width // BLOCK
     slots = idx_ref.shape[1]
     count = share_ref.shape[1] // BLOCK
-    here = place_ref[0]
-    first = place_ref[1]
+    here = lax.axis_index("atoms")
+    first = lax.axis_index("waves") * count
     share = pl.ds(pl.multiple_of(first * BLOCK, BLOCK), count * BLOCK)
     moves = []
     for rows in (pl.ds(chans, ext_ref.shape[0] - chans), pl.ds(0, chans)):
@@ -344,7 +344,7 @@
         inner_ref[:, span] = lax.dot_general(outer, known, TN, **f32)
 
 
-def pairs(place, live_blocks, neighbours, live_slots, prev, own, following, h, first, second, count, regions):
+def pairs(live_blocks, neighbours, live_slots, prev, own, following, h, first, second, count, regions):
     rows, width = own.shape
     chans = h.shape[0]
     hidden = first.shape[1]
@@ -361,7 +361,7 @@
             jax.ShapeDtypeStruct((hidden, chans), jnp.bfloat16),
             jax.ShapeDtypeStruct(second.shape, jnp.bfloat16),
         ),
-        in_specs=[SMEM_SPEC] * 4 + [ANY_SPEC] * 2 + [HBM_SPEC] * 4,
+        in_specs=[SMEM_SPEC] * 3 + [ANY_SPEC] * 2 + [HBM_SPEC] * 4,
         out_specs=(VMEM_SPEC,) * 5,
         scratch_shapes=[
             pltpu.VMEM((rows, 3 * width), jnp.bfloat16),
@@ -378,7 +378,7 @@
             flops=work * (2 * chans + 20), bytes_accessed=6 * rows * width, transcendentals=work
         ),
         name="pairs",
-    )(place, live_blocks, neighbours, live_slots, prev, following, *in_hbm(own, h, first, second))
+    )(live_blocks, neighbours, live_slots, prev, following, *in_hbm(own, h, first, second))
 
 
 def update_kernel(arrived_ref, inner_ref, share_ref, alive_ref, third_ref, second_ref, out_ref):
@@ -441,15 +441,12 @@
     nblocks = width // BLOCK
     regions = lax.axis_size("atoms")
     groups_waves = lax.axis_size("waves")
-    here = lax.axis_index("atoms")
     per_group = nblocks // groups_waves
-    first = lax.axis_index("waves") * per_group
-    place = jnp.stack([here, first]).astype(jnp.int32)
     total = regions * width
     low, high, factor, sent, carry, gain_rows, mixing = structure(
-        place, block_count, kvec, coords, features, msg_weight[0], filter_weight[0], 1.0 / math.sqrt(total), regions
+        block_count, kvec, coords, features, msg_weight[0], filter_weight[0], 1.0 / math.sqrt(total), regions
     )
-    exchanges = (1, 2, 6, 8, 24)
+    exchanges = (1, 2, 6, 8, 16)
     for step, flip in enumerate(exchanges):
         arrived = lax.ppermute(sent, "atoms", [(i, i ^ flip) for i in range(regions)])
         if step + 1 < len(exchanges):
@@ -459,10 +456,10 @@
     following = shifted(carry, regions, groups_waves, -1)
     filtered = spectral(factor, arrived, gain_rows, mixing)
     other = lax.ppermute(filtered, "atoms", [(i, i ^ 1) for i in range(regions)])
-    partial_potential = potentials(place, filtered, other, low, high, groups_waves)
+    partial_potential = potentials(filtered, other, low, high, groups_waves)
     potential = from_others(partial_potential, "waves")
     known = pairs(
-        place, block_count, neighbours.T, live_slots.T, prev, carry, following,
+        block_count, neighbours.T, live_slots.T, prev, carry, following,
         features, mlp_in[0].T, mlp_out[0], per_group, regions,
     )
     new = update(potential, known)

time: 83 us -> 83.2 us (level)
  Pallas kernels: 15.8 us -> 14.7 us
  waiting for transfers between devices: 23.7 us -> 24.6 us
    ppermute x5, starting transfers between devices: 8.41 us -> 9.76 us  [local(): lax.ppermute(sent, 'atoms', [(i, i ^ flip) for i in range(regions)])]
    ppermute x2, starting transfers between devices: 4.56 us -> 3.27 us  [shifted(): return lax.ppermute(cells, ('atoms', 'waves'), pairs_of)]
where the time goes in v11:
time: 83.2 us; the launch traced here: 82.2 us
  waiting for transfers between devices  24.6 us (30%)
  starting transfers between devices  23 us (28%)
  blocking collectives  18.3 us (22%)
  Pallas kernels  14.7 us (18%)
    all_to_all x1, blocking collectives, from_others(): return lax.all_to_all(pieces, axis, 0, 0, tiled=True)  18.3 us
    ppermute x2, waiting for transfers between devices, shifted(): return lax.ppermute(cells, ('atoms', 'waves'), pairs_of)  11.7 us
    ppermute x5, waiting for transfers between devices, local(): lax.ppermute(sent, 'atoms', [(i, i ^ flip) for i in range(regions)])  11.6 us
    all_to_all x1, starting transfers between devices, from_others(): return lax.all_to_all(pieces, axis, 0, 0, tiled=True)  9.89 us
    ppermute x5, starting transfers between devices, local(): lax.ppermute(sent, 'atoms', [(i, i ^ flip) for i in range(regions)])  9.76 us
    pallas_call x1, Pallas kernels, pairs(): pl.pallas_call(functools.partial(pairs_kernel, float(regions), regions, u...  6.11 us
    pallas_call x1, Pallas kernels, structure(): pl.pallas_call(functools.partial(structure_kernel, scale, float(regions))...  5.56 us
    ppermute x2, starting transfers between devices, shifted(): return lax.ppermute(cells, ('atoms', 'waves'), pairs_of)  3.27 us
  transfers between devices with their start and end apart: 9, of which 8 were waited for; matrix products, arithmetic and copies ran while one was open for 0% of the time, Pallas kernels for 7%

profile of v11, /device:TPU:32, one launch (start us, length us, event | category | flops | bytes accessed | tf_op | source)
XLA Modules:
  0.0 82.2 jit_solution(5021612593402263758)
XLA Ops:
  0.7 5.6 %structure.1 = (bf16[384,4096]{1,0:T(8,128)(2,1)S(1)}, bf16[128,4096]{1,0:T(8,128)(2,1)}, f32[256,128]{1,0:T(8,128)S(1)}, bf16[256,128]{1,0:T(8,128)(2,1)S(1)}, ...) custom-call(s32[1]{0:T(128)S(6)} %copy.13.count_ref, s32[3,512]{1,0:T(4,128)} %kvec_in.1, ...), custom_call_target="tpu_custom_call" | custom-call | tf_op jit(solution)/shard_map/structure/pallas_call | solution.py:150
  6.2 0.1 collective-permute-start
  6.3 1.2 %collective-permute-done = bf16[256,128]{1,0:T(8,128)(2,1)S(1)} collective-permute-done((bf16[256,128]{1,0:T(8,128)(2,1)S(1)}, bf16[256,128]{1,0:T(8,128)(2,1)S(1)}, u32[]{:S(2)}, u32[]{:S(2)}) %collective-permute-start) | collective-permute-done | bytes 65568 | tf_op jit(solution)/shard_map/ppermute | solution.py:451
  7.6 1.6 %collective-permute-start.1 = (bf16[256,128]{1,0:T(8,128)(2,1)S(1)}, bf16[256,128]{1,0:T(8,128)(2,1)S(1)}, u32[]{:S(2)}, u32[]{:S(2)}) collective-permute-start(bf16[256,128]{1,0:T(8,128)(2,1)S(1)} %fusion), channel_id=1, source_target_pairs={{0,16},{8,24},{16,0},{24,8},{32,48},{40,56},{48,32},{56,40},{64,80... | collective-permute-start | bytes 196616 | tf_op jit(solution)/shard_map/ppermute | solution.py:451
  9.2 2.8 %collective-permute-done.1 = bf16[256,128]{1,0:T(8,128)(2,1)S(1)} collective-permute-done((bf16[256,128]{1,0:T(8,128)(2,1)S(1)}, bf16[256,128]{1,0:T(8,128)(2,1)S(1)}, u32[]{:S(2)}, u32[]{:S(2)}) %collective-permute-start.1) | collective-permute-done | bytes 65568 | tf_op jit(solution)/shard_map/ppermute | solution.py:451
  12.0 2.8 %collective-permute-start.2 = (bf16[256,128]{1,0:T(8,128)(2,1)S(1)}, bf16[256,128]{1,0:T(8,128)(2,1)S(1)}, u32[]{:S(2)}, u32[]{:S(2)}) collective-permute-start(bf16[256,128]{1,0:T(8,128)(2,1)S(1)} %fusion.2), channel_id=1, source_target_pairs={{0,48},{8,56},{16,32},{24,40},{32,16},{40,24},{48,0},{56,8},{64,11... | collective-permute-start | bytes 196616 | tf_op jit(solution)/shard_map/ppermute | solution.py:451
  14.8 2.7 %collective-permute-done.2 = bf16[256,128]{1,0:T(8,128)(2,1)S(1)} collective-permute-done((bf16[256,128]{1,0:T(8,128)(2,1)S(1)}, bf16[256,128]{1,0:T(8,128)(2,1)S(1)}, u32[]{:S(2)}, u32[]{:S(2)}) %collective-permute-start.2) | collective-permute-done | bytes 65568 | tf_op jit(solution)/shard_map/ppermute | solution.py:451
  17.6 0.0 copy-start.2
  17.6 0.0 copy-start
  17.6 0.0 copy-start.1
  17.6 1.9 %collective-permute-start.3 = (bf16[256,128]{1,0:T(8,128)(2,1)S(1)}, bf16[256,128]{1,0:T(8,128)(2,1)S(1)}, u32[]{:S(2)}, u32[]{:S(2)}) collective-permute-start(bf16[256,128]{1,0:T(8,128)(2,1)S(1)} %fusion.1), channel_id=1, source_target_pairs={{0,64},{8,72},{16,80},{24,88},{32,96},{40,104},{48,112},{56,120},{... | collective-permute-start | bytes 196616 | tf_op jit(solution)/shard_map/ppermute | solution.py:451
  19.5 2.5 %collective-permute-done.3 = bf16[256,128]{1,0:T(8,128)(2,1)S(1)} collective-permute-done((bf16[256,128]{1,0:T(8,128)(2,1)S(1)}, bf16[256,128]{1,0:T(8,128)(2,1)S(1)}, u32[]{:S(2)}, u32[]{:S(2)}) %collective-permute-start.3) | collective-permute-done | bytes 65568 | tf_op jit(solution)/shard_map/ppermute | solution.py:451
  22.0 3.3 %collective-permute-start.4 = (bf16[256,128]{1,0:T(8,128)(2,1)S(1)}, bf16[256,128]{1,0:T(8,128)(2,1)S(1)}, u32[]{:S(2)}, u32[]{:S(2)}) collective-permute-start(bf16[256,128]{1,0:T(8,128)(2,1)S(1)} %get-tuple-element.29), channel_id=1, source_target_pairs={{0,128},{8,136},{16,144},{24,152},{32,160},{40,168},{48,176},{56,1... | collective-permute-start | bytes 196616 | tf_op jit(solution)/shard_map/ppermute | solution.py:451
  25.4 2.4 %collective-permute-done.4.arrived_ref = bf16[256,128]{1,0:T(8,128)(2,1)S(1)} collective-permute-done((bf16[256,128]{1,0:T(8,128)(2,1)S(1)}, bf16[256,128]{1,0:T(8,128)(2,1)S(1)}, u32[]{:S(2)}, u32[]{:S(2)}) %collective-permute-start.4) | collective-permute-done | bytes 65568 | tf_op jit(solution)/shard_map/ppermute | solution.py:451
  27.8 0.5 spectral.1.own_ref
  28.2 0.1 collective-permute-start.5
  28.3 1.2 %collective-permute-done.5.other_ref = bf16[256,128]{1,0:T(8,128)(2,1)S(1)} collective-permute-done((bf16[256,128]{1,0:T(8,128)(2,1)S(1)}, bf16[256,128]{1,0:T(8,128)(2,1)S(1)}, u32[]{:S(2)}, u32[]{:S(2)}) %collective-permute-start.5) | collective-permute-done | bytes 65568 | tf_op jit(solution)/shard_map/ppermute | solution.py:458
  29.6 2.2 %potentials.1 = bf16[8,64,256]{2,1,0:T(8,128)(2,1)} custom-call(bf16[256,128]{1,0:T(8,128)(2,1)S(1)} %spectral.1.own_ref, bf16[256,128]{1,0:T(8,128)(2,1)S(1)} %collective-permute-done.5.other_ref, bf16[384,4096]{1,0:T(8,128)(2,1)S(1)} %get-tuple-element.21.low_ref, bf16[128,4096]{1,0:T(8,128)(2,1)} %get-tuple-element.22.high_in), custom_call_target="tpu_custom_call" | custom-call | tf_op jit(solution)/shard_map/potentials/pallas_call | solution.py:238
  31.8 9.9 %all-to-all-start = ((bf16[8,64,256]{2,1,0:T(8,128)(2,1)}), bf16[8,64,256]{2,1,0:T(8,128)(2,1)S(1)}, u32[]{:S(2)}, u32[]{:S(2)}) async-start(bf16[8,64,256]{2,1,0:T(8,128)(2,1)} %potentials.1), calls=%async_computation | async-start | bytes 524288 | tf_op jit(solution)/shard_map/all_to_all | solution.py:425
  41.7 0.0 copy-done.2
  41.7 3.3 %collective-permute-start.7 = (bf16[88,2048]{1,0:T(8,128)(2,1)S(1)}, bf16[88,2048]{1,0:T(8,128)(2,1)S(1)}, u32[]{:S(2)}, u32[]{:S(2)}) collective-permute-start(bf16[88,2048]{1,0:T(8,128)(2,1)S(1)} %copy-done.2), channel_id=1, source_target_pairs={{0,252},{1,253},{2,254},{3,255},{4,248},{5,249},{6,250},{7,251},{8... | collective-permute-start | bytes 1081352 | tf_op jit(solution)/shard_map/ppermute | solution.py:421
  45.0 0.0 collective-permute-start.6
  45.0 6.7 %collective-permute-done.7.next_in = bf16[88,2048]{1,0:T(8,128)(2,1)S(1)} collective-permute-done((bf16[88,2048]{1,0:T(8,128)(2,1)S(1)}, bf16[88,2048]{1,0:T(8,128)(2,1)S(1)}, u32[]{:S(2)}, u32[]{:S(2)}) %collective-permute-start.7) | collective-permute-done | bytes 360480 | tf_op jit(solution)/shard_map/ppermute | solution.py:421
  51.7 5.0 %collective-permute-done.6.prev_in = bf16[88,2048]{1,0:T(8,128)(2,1)S(1)} collective-permute-done((bf16[88,2048]{1,0:T(8,128)(2,1)S(1)}, bf16[88,2048]{1,0:T(8,128)(2,1)S(1)}, u32[]{:S(2)}, u32[]{:S(2)}) %collective-permute-start.6) | collective-permute-done | bytes 360480 | tf_op jit(solution)/shard_map/ppermute | solution.py:421
  56.7 0.0 copy-done
  56.7 0.0 copy-done.1
  56.7 6.1 %pairs.1 = (f32[128,256]{1,0:T(8,128)S(1)}, bf16[64,256]{1,0:T(8,128)(2,1)S(1)}, f32[8,256]{1,0:T(8,128)S(1)}, bf16[128,64]{1,0:T(8,128)(2,1)S(1)}, bf16[64,128]{1,0:T(8,128)(2,1)S(1)}) custom-call(s32[1]{0:T(128)S(6)} %copy.13.count_ref, s32[16,27]{1,0:T(8,128)S(1)} %bitcast.11, s32[16,27]{1,0:T(8,128)S(1)} %bitcast.12, ...), custom_call_target="tpu_custom_call" | custom-call | flops 130940928 | bytes 1081344 | tf_op jit(solution)/shard_map/pairs/pallas_call | solution.py:355
  62.8 0.0 all-to-all-done.arrived_ref
  62.8 0.3 update.1
  63.2 18.3 %all_to_all.10 = bf16[8,64,256]{2,1,0:T(8,128)(2,1)S(1)} all-to-all(bf16[8,64,256]{2,1,0:T(8,128)(2,1)S(1)} %update.1), channel_id=1, replica_groups=mesh['atoms'=32,'waves'=8] {'waves'}, dimensions={0} | all-to-all | bytes 524288 | tf_op jit(solution)/shard_map/all_to_all | solution.py:425
  81.5 0.7 copy.12
  (4 shorter events, 0.1 us)
Async XLA Ops:
  6.2 1.3 %collective-permute-start = (bf16[256,128]{1,0:T(8,128)(2,1)S(1)}, bf16[256,128]{1,0:T(8,128)(2,1)S(1)}, u32[]{:S(2)}, u32[]{:S(2)}) collective-permute-start(bf16[256,128]{1,0:T(8,128)(2,1)S(1)} %get-tuple-element.18), channel_id=1, source_target_pairs={{0,8},{8,0},{16,24},{24,16},{32,40},{40,32},{48,56},{56,48},{64,72... | collective-permute-start | bytes 196616 | tf_op jit(solution)/shard_map/ppermute | solution.py:451
  7.6 4.4 %collective-permute-start.1 = (bf16[256,128]{1,0:T(8,128)(2,1)S(1)}, bf16[256,128]{1,0:T(8,128)(2,1)S(1)}, u32[]{:S(2)}, u32[]{:S(2)}) collective-permute-start(bf16[256,128]{1,0:T(8,128)(2,1)S(1)} %fusion), channel_id=1, source_target_pairs={{0,16},{8,24},{16,0},{24,8},{32,48},{40,56},{48,32},{56,40},{64,80... | collective-permute-start | bytes 196616 | tf_op jit(solution)/shard_map/ppermute | solution.py:451
  12.0 5.6 %collective-permute-start.2 = (bf16[256,128]{1,0:T(8,128)(2,1)S(1)}, bf16[256,128]{1,0:T(8,128)(2,1)S(1)}, u32[]{:S(2)}, u32[]{:S(2)}) collective-permute-start(bf16[256,128]{1,0:T(8,128)(2,1)S(1)} %fusion.2), channel_id=1, source_target_pairs={{0,48},{8,56},{16,32},{24,40},{32,16},{40,24},{48,0},{56,8},{64,11... | collective-permute-start | bytes 196616 | tf_op jit(solution)/shard_map/ppermute | solution.py:451
  17.6 24.2 %copy-start.2 = (bf16[88,2048]{1,0:T(8,128)(2,1)S(1)}, bf16[88,2048]{1,0:T(8,128)(2,1)}, u32[]{:S(2)}) copy-start(bf16[88,2048]{1,0:T(8,128)(2,1)} %get-tuple-element.23.own_in) | copy-start | bytes 1081348
  17.6 39.1 %copy-start = (s32[27,16]{0,1:T(8,128)S(1)}, s32[27,16]{0,1:T(8,128)}, u32[]{:S(2)}) copy-start(s32[27,16]{0,1:T(8,128)} %param.12) | copy-start | bytes 5188
  17.6 39.1 %copy-start.1 = (s32[27,16]{0,1:T(8,128)S(1)}, s32[27,16]{0,1:T(8,128)}, u32[]{:S(2)}) copy-start(s32[27,16]{0,1:T(8,128)} %param.13) | copy-start | bytes 5188
  17.6 4.4 %collective-permute-start.3 = (bf16[256,128]{1,0:T(8,128)(2,1)S(1)}, bf16[256,128]{1,0:T(8,128)(2,1)S(1)}, u32[]{:S(2)}, u32[]{:S(2)}) collective-permute-start(bf16[256,128]{1,0:T(8,128)(2,1)S(1)} %fusion.1), channel_id=1, source_target_pairs={{0,64},{8,72},{16,80},{24,88},{32,96},{40,104},{48,112},{56,120},{... | collective-permute-start | bytes 196616 | tf_op jit(solution)/shard_map/ppermute | solution.py:451
  22.0 5.8 %collective-permute-start.4 = (bf16[256,128]{1,0:T(8,128)(2,1)S(1)}, bf16[256,128]{1,0:T(8,128)(2,1)S(1)}, u32[]{:S(2)}, u32[]{:S(2)}) collective-permute-start(bf16[256,128]{1,0:T(8,128)(2,1)S(1)} %get-tuple-element.29), channel_id=1, source_target_pairs={{0,128},{8,136},{16,144},{24,152},{32,160},{40,168},{48,176},{56,1... | collective-permute-start | bytes 196616 | tf_op jit(solution)/shard_map/ppermute | solution.py:451
  28.2 1.3 %collective-permute-start.5 = (bf16[256,128]{1,0:T(8,128)(2,1)S(1)}, bf16[256,128]{1,0:T(8,128)(2,1)S(1)}, u32[]{:S(2)}, u32[]{:S(2)}) collective-permute-start(bf16[256,128]{1,0:T(8,128)(2,1)S(1)} %spectral.1.own_ref), channel_id=1, source_target_pairs={{0,8},{8,0},{16,24},{24,16},{32,40},{40,32},{48,56},{56,48},{64,72... | collective-permute-start | bytes 196616 | tf_op jit(solution)/shard_map/ppermute | solution.py:458
  31.8 31.0 %all-to-all-start = ((bf16[8,64,256]{2,1,0:T(8,128)(2,1)}), bf16[8,64,256]{2,1,0:T(8,128)(2,1)S(1)}, u32[]{:S(2)}, u32[]{:S(2)}) async-start(bf16[8,64,256]{2,1,0:T(8,128)(2,1)} %potentials.1), calls=%async_computation | async-start | bytes 524288 | tf_op jit(solution)/shard_map/all_to_all | solution.py:425
  41.7 10.0 %collective-permute-start.7 = (bf16[88,2048]{1,0:T(8,128)(2,1)S(1)}, bf16[88,2048]{1,0:T(8,128)(2,1)S(1)}, u32[]{:S(2)}, u32[]{:S(2)}) collective-permute-start(bf16[88,2048]{1,0:T(8,128)(2,1)S(1)} %copy-done.2), channel_id=1, source_target_pairs={{0,252},{1,253},{2,254},{3,255},{4,248},{5,249},{6,250},{7,251},{8... | collective-permute-start | bytes 1081352 | tf_op jit(solution)/shard_map/ppermute | solution.py:421
  45.0 11.7 %collective-permute-start.6 = (bf16[88,2048]{1,0:T(8,128)(2,1)S(1)}, bf16[88,2048]{1,0:T(8,128)(2,1)S(1)}, u32[]{:S(2)}, u32[]{:S(2)}) collective-permute-start(bf16[88,2048]{1,0:T(8,128)(2,1)S(1)} %copy-done.2), channel_id=1, source_target_pairs={{0,8},{1,9},{2,10},{3,11},{4,12},{5,13},{6,14},{7,15},{8,16},{9,17... | collective-permute-start | bytes 1081352 | tf_op jit(solution)/shard_map/ppermute | solution.py:421

commit v12 on v11

--- a/solution.py
+++ b/solution.py
@@ -38,7 +38,7 @@
     s = r * ((SIN_COEFS[2] * u + SIN_COEFS[1]) * u + SIN_COEFS[0])
     q = s * s
     w = math.sqrt(8.0) - q
-    return 1.0 - q * w, (s * (w * lax.rsqrt(w))) * (math.sqrt(2.0) - q)
+    return 1.0 - q * w, ((s * w) * (math.sqrt(2.0) - q)) * lax.rsqrt(w)
 
 
 def three_pieces(values):
@@ -131,9 +131,10 @@
             if row == kept:
                 carry_ref[:chans, cos_span] = jnp.dot(weight_ref[...], h_ref[:, cos_span], **f32).astype(jnp.bfloat16)
             pending.append((place, at, row, start))
-            if len(pending) > 1:
+            if len(pending) > 2:
                 add_up(*pending.pop(0))
-    add_up(*pending.pop(0))
+    for last in pending:
+        add_up(*last)
     kept_ref[...] = whole_ref[mine, :]
     sent_ref[...] = whole_ref[theirs, :].astype(jnp.bfloat16)
     for copy in copies:
@@ -446,7 +447,7 @@
     low, high, factor, sent, carry, gain_rows, mixing = structure(
         block_count, kvec, coords, features, msg_weight[0], filter_weight[0], 1.0 / math.sqrt(total), regions
     )
-    exchanges = (1, 2, 6, 8, 16)
+    exchanges = (1, 2, 6, 8, 24)
     for step, flip in enumerate(exchanges):
         arrived = lax.ppermute(sent, "atoms", [(i, i ^ flip) for i in range(regions)])
         if step + 1 < len(exchanges):

time: 83.2 us -> 81.7 us (0.982)
  waiting for transfers between devices: 24.6 us -> 23.7 us
    ppermute x5, starting transfers between devices: 9.76 us -> 8.44 us  [local(): lax.ppermute(sent, 'atoms', [(i, i ^ flip) for i in range(regions)])]
    ppermute x2, starting transfers between devices: 3.27 us -> 4.56 us  [shifted(): return lax.ppermute(cells, ('atoms', 'waves'), pairs_of)]
  transfers between devices with their start and end apart: 9 -> 9, of which waited for: 8 -> 8; matrix products, arithmetic and copies ran while one was open for 0% -> 0% of each run, Pallas kernels for 7% -> 8%
where the time goes in v12:
time: 81.7 us; the launch traced here: 81.4 us
  waiting for transfers between devices  23.7 us (29%)
  starting transfers between devices  23.3 us (29%)
  blocking collectives  18.2 us (22%)
  Pallas kernels  14.6 us (18%)
    all_to_all x1, blocking collectives, from_others(): return lax.all_to_all(pieces, axis, 0, 0, tiled=True)  18.2 us
    ppermute x5, waiting for transfers between devices, local(): lax.ppermute(sent, 'atoms', [(i, i ^ flip) for i in range(regions)])  11.5 us
    ppermute x2, waiting for transfers between devices, shifted(): return lax.ppermute(cells, ('atoms', 'waves'), pairs_of)  10.9 us
    all_to_all x1, starting transfers between devices, from_others(): return lax.all_to_all(pieces, axis, 0, 0, tiled=True)  10.2 us
    ppermute x5, starting transfers between devices, local(): lax.ppermute(sent, 'atoms', [(i, i ^ flip) for i in range(regions)])  8.44 us
    pallas_call x1, Pallas kernels, pairs(): pl.pallas_call(functools.partial(pairs_kernel, float(regions), regions, u...  6.11 us
    pallas_call x1, Pallas kernels, structure(): pl.pallas_call(functools.partial(structure_kernel, scale, float(regions))...  5.45 us
    ppermute x2, starting transfers between devices, shifted(): return lax.ppermute(cells, ('atoms', 'waves'), pairs_of)  4.56 us
  transfers between devices with their start and end apart: 9, of which 8 were waited for; matrix products, arithmetic and copies ran while one was open for 0% of the time, Pallas kernels for 8%

profile of v12, /device:TPU:32, one launch (start us, length us, event | category | flops | bytes accessed | tf_op | source)
XLA Modules:
  0.0 81.4 jit_solution(4374260436365183781)
XLA Ops:
  0.7 5.5 %structure.1 = (bf16[384,4096]{1,0:T(8,128)(2,1)S(1)}, bf16[128,4096]{1,0:T(8,128)(2,1)}, f32[256,128]{1,0:T(8,128)S(1)}, bf16[256,128]{1,0:T(8,128)(2,1)S(1)}, ...) custom-call(s32[1]{0:T(128)S(6)} %copy.13.count_ref, s32[3,512]{1,0:T(4,128)} %kvec_in.1, ...), custom_call_target="tpu_custom_call" | custom-call | tf_op jit(solution)/shard_map/structure/pallas_call | solution.py:151
  6.1 0.1 collective-permute-start
  6.2 1.2 %collective-permute-done = bf16[256,128]{1,0:T(8,128)(2,1)S(1)} collective-permute-done((bf16[256,128]{1,0:T(8,128)(2,1)S(1)}, bf16[256,128]{1,0:T(8,128)(2,1)S(1)}, u32[]{:S(2)}, u32[]{:S(2)}) %collective-permute-start) | collective-permute-done | bytes 65568 | tf_op jit(solution)/shard_map/ppermute | solution.py:452
  7.5 1.6 %collective-permute-start.1 = (bf16[256,128]{1,0:T(8,128)(2,1)S(1)}, bf16[256,128]{1,0:T(8,128)(2,1)S(1)}, u32[]{:S(2)}, u32[]{:S(2)}) collective-permute-start(bf16[256,128]{1,0:T(8,128)(2,1)S(1)} %fusion), channel_id=1, source_target_pairs={{0,16},{8,24},{16,0},{24,8},{32,48},{40,56},{48,32},{56,40},{64,80... | collective-permute-start | bytes 196616 | tf_op jit(solution)/shard_map/ppermute | solution.py:452
  9.1 2.8 %collective-permute-done.1 = bf16[256,128]{1,0:T(8,128)(2,1)S(1)} collective-permute-done((bf16[256,128]{1,0:T(8,128)(2,1)S(1)}, bf16[256,128]{1,0:T(8,128)(2,1)S(1)}, u32[]{:S(2)}, u32[]{:S(2)}) %collective-permute-start.1) | collective-permute-done | bytes 65568 | tf_op jit(solution)/shard_map/ppermute | solution.py:452
  11.9 2.8 %collective-permute-start.2 = (bf16[256,128]{1,0:T(8,128)(2,1)S(1)}, bf16[256,128]{1,0:T(8,128)(2,1)S(1)}, u32[]{:S(2)}, u32[]{:S(2)}) collective-permute-start(bf16[256,128]{1,0:T(8,128)(2,1)S(1)} %fusion.2), channel_id=1, source_target_pairs={{0,48},{8,56},{16,32},{24,40},{32,16},{40,24},{48,0},{56,8},{64,11... | collective-permute-start | bytes 196616 | tf_op jit(solution)/shard_map/ppermute | solution.py:452
  14.7 2.7 %collective-permute-done.2 = bf16[256,128]{1,0:T(8,128)(2,1)S(1)} collective-permute-done((bf16[256,128]{1,0:T(8,128)(2,1)S(1)}, bf16[256,128]{1,0:T(8,128)(2,1)S(1)}, u32[]{:S(2)}, u32[]{:S(2)}) %collective-permute-start.2) | collective-permute-done | bytes 65568 | tf_op jit(solution)/shard_map/ppermute | solution.py:452
  17.5 0.0 copy-start.2
  17.5 0.0 copy-start
  17.5 0.0 copy-start.1
  17.5 1.9 %collective-permute-start.3 = (bf16[256,128]{1,0:T(8,128)(2,1)S(1)}, bf16[256,128]{1,0:T(8,128)(2,1)S(1)}, u32[]{:S(2)}, u32[]{:S(2)}) collective-permute-start(bf16[256,128]{1,0:T(8,128)(2,1)S(1)} %fusion.1), channel_id=1, source_target_pairs={{0,64},{8,72},{16,80},{24,88},{32,96},{40,104},{48,112},{56,120},{... | collective-permute-start | bytes 196616 | tf_op jit(solution)/shard_map/ppermute | solution.py:452
  19.4 2.4 %collective-permute-done.3 = bf16[256,128]{1,0:T(8,128)(2,1)S(1)} collective-permute-done((bf16[256,128]{1,0:T(8,128)(2,1)S(1)}, bf16[256,128]{1,0:T(8,128)(2,1)S(1)}, u32[]{:S(2)}, u32[]{:S(2)}) %collective-permute-start.3) | collective-permute-done | bytes 65568 | tf_op jit(solution)/shard_map/ppermute | solution.py:452
  21.9 2.0 %collective-permute-start.4 = (bf16[256,128]{1,0:T(8,128)(2,1)S(1)}, bf16[256,128]{1,0:T(8,128)(2,1)S(1)}, u32[]{:S(2)}, u32[]{:S(2)}) collective-permute-start(bf16[256,128]{1,0:T(8,128)(2,1)S(1)} %get-tuple-element.29), channel_id=1, source_target_pairs={{0,192},{8,200},{16,208},{24,216},{32,224},{40,232},{48,240},{56,2... | collective-permute-start | bytes 196616 | tf_op jit(solution)/shard_map/ppermute | solution.py:452
  23.9 2.3 %collective-permute-done.4.arrived_ref = bf16[256,128]{1,0:T(8,128)(2,1)S(1)} collective-permute-done((bf16[256,128]{1,0:T(8,128)(2,1)S(1)}, bf16[256,128]{1,0:T(8,128)(2,1)S(1)}, u32[]{:S(2)}, u32[]{:S(2)}) %collective-permute-start.4) | collective-permute-done | bytes 65568 | tf_op jit(solution)/shard_map/ppermute | solution.py:452
  26.2 0.5 spectral.1.own_ref
  26.7 0.1 collective-permute-start.5
  26.8 1.2 %collective-permute-done.5.other_ref = bf16[256,128]{1,0:T(8,128)(2,1)S(1)} collective-permute-done((bf16[256,128]{1,0:T(8,128)(2,1)S(1)}, bf16[256,128]{1,0:T(8,128)(2,1)S(1)}, u32[]{:S(2)}, u32[]{:S(2)}) %collective-permute-start.5) | collective-permute-done | bytes 65568 | tf_op jit(solution)/shard_map/ppermute | solution.py:459
  28.1 2.2 %potentials.1 = bf16[8,64,256]{2,1,0:T(8,128)(2,1)} custom-call(bf16[256,128]{1,0:T(8,128)(2,1)S(1)} %spectral.1.own_ref, bf16[256,128]{1,0:T(8,128)(2,1)S(1)} %collective-permute-done.5.other_ref, bf16[384,4096]{1,0:T(8,128)(2,1)S(1)} %get-tuple-element.21.low_ref, bf16[128,4096]{1,0:T(8,128)(2,1)} %get-tuple-element.22.high_in), custom_call_target="tpu_custom_call" | custom-call | tf_op jit(solution)/shard_map/potentials/pallas_call | solution.py:239
  30.3 10.2 %all-to-all-start = ((bf16[8,64,256]{2,1,0:T(8,128)(2,1)}), bf16[8,64,256]{2,1,0:T(8,128)(2,1)S(1)}, u32[]{:S(2)}, u32[]{:S(2)}) async-start(bf16[8,64,256]{2,1,0:T(8,128)(2,1)} %potentials.1), calls=%async_computation | async-start | bytes 524288 | tf_op jit(solution)/shard_map/all_to_all | solution.py:426
  40.5 0.0 copy-done.2
  40.5 4.6 %collective-permute-start.7 = (bf16[88,2048]{1,0:T(8,128)(2,1)S(1)}, bf16[88,2048]{1,0:T(8,128)(2,1)S(1)}, u32[]{:S(2)}, u32[]{:S(2)}) collective-permute-start(bf16[88,2048]{1,0:T(8,128)(2,1)S(1)} %copy-done.2), channel_id=1, source_target_pairs={{0,252},{1,253},{2,254},{3,255},{4,248},{5,249},{6,250},{7,251},{8... | collective-permute-start | bytes 1081352 | tf_op jit(solution)/shard_map/ppermute | solution.py:422
  45.1 0.0 collective-permute-start.6
  45.1 5.4 %collective-permute-done.7.next_in = bf16[88,2048]{1,0:T(8,128)(2,1)S(1)} collective-permute-done((bf16[88,2048]{1,0:T(8,128)(2,1)S(1)}, bf16[88,2048]{1,0:T(8,128)(2,1)S(1)}, u32[]{:S(2)}, u32[]{:S(2)}) %collective-permute-start.7) | collective-permute-done | bytes 360480 | tf_op jit(solution)/shard_map/ppermute | solution.py:422
  50.5 5.5 %collective-permute-done.6.prev_in = bf16[88,2048]{1,0:T(8,128)(2,1)S(1)} collective-permute-done((bf16[88,2048]{1,0:T(8,128)(2,1)S(1)}, bf16[88,2048]{1,0:T(8,128)(2,1)S(1)}, u32[]{:S(2)}, u32[]{:S(2)}) %collective-permute-start.6) | collective-permute-done | bytes 360480 | tf_op jit(solution)/shard_map/ppermute | solution.py:422
  56.0 0.0 copy-done
  56.0 0.0 copy-done.1
  56.0 6.1 %pairs.1 = (f32[128,256]{1,0:T(8,128)S(1)}, bf16[64,256]{1,0:T(8,128)(2,1)S(1)}, f32[8,256]{1,0:T(8,128)S(1)}, bf16[128,64]{1,0:T(8,128)(2,1)S(1)}, bf16[64,128]{1,0:T(8,128)(2,1)S(1)}) custom-call(s32[1]{0:T(128)S(6)} %copy.13.count_ref, s32[16,27]{1,0:T(8,128)S(1)} %bitcast.11, s32[16,27]{1,0:T(8,128)S(1)} %bitcast.12, ...), custom_call_target="tpu_custom_call" | custom-call | flops 130940928 | bytes 1081344 | tf_op jit(solution)/shard_map/pairs/pallas_call | solution.py:356
  62.2 0.0 all-to-all-done.arrived_ref
  62.2 0.3 update.1
  62.5 18.2 %all_to_all.10 = bf16[8,64,256]{2,1,0:T(8,128)(2,1)S(1)} all-to-all(bf16[8,64,256]{2,1,0:T(8,128)(2,1)S(1)} %update.1), channel_id=1, replica_groups=mesh['atoms'=32,'waves'=8] {'waves'}, dimensions={0} | all-to-all | bytes 524288 | tf_op jit(solution)/shard_map/all_to_all | solution.py:426
  80.7 0.7 copy.12
  (4 shorter events, 0.1 us)
Async XLA Ops:
  6.1 1.3 %collective-permute-start = (bf16[256,128]{1,0:T(8,128)(2,1)S(1)}, bf16[256,128]{1,0:T(8,128)(2,1)S(1)}, u32[]{:S(2)}, u32[]{:S(2)}) collective-permute-start(bf16[256,128]{1,0:T(8,128)(2,1)S(1)} %get-tuple-element.18), channel_id=1, source_target_pairs={{0,8},{8,0},{16,24},{24,16},{32,40},{40,32},{48,56},{56,48},{64,72... | collective-permute-start | bytes 196616 | tf_op jit(solution)/shard_map/ppermute | solution.py:452
  7.5 4.4 %collective-permute-start.1 = (bf16[256,128]{1,0:T(8,128)(2,1)S(1)}, bf16[256,128]{1,0:T(8,128)(2,1)S(1)}, u32[]{:S(2)}, u32[]{:S(2)}) collective-permute-start(bf16[256,128]{1,0:T(8,128)(2,1)S(1)} %fusion), channel_id=1, source_target_pairs={{0,16},{8,24},{16,0},{24,8},{32,48},{40,56},{48,32},{56,40},{64,80... | collective-permute-start | bytes 196616 | tf_op jit(solution)/shard_map/ppermute | solution.py:452
  11.9 5.6 %collective-permute-start.2 = (bf16[256,128]{1,0:T(8,128)(2,1)S(1)}, bf16[256,128]{1,0:T(8,128)(2,1)S(1)}, u32[]{:S(2)}, u32[]{:S(2)}) collective-permute-start(bf16[256,128]{1,0:T(8,128)(2,1)S(1)} %fusion.2), channel_id=1, source_target_pairs={{0,48},{8,56},{16,32},{24,40},{32,16},{40,24},{48,0},{56,8},{64,11... | collective-permute-start | bytes 196616 | tf_op jit(solution)/shard_map/ppermute | solution.py:452
  17.5 23.1 %copy-start.2 = (bf16[88,2048]{1,0:T(8,128)(2,1)S(1)}, bf16[88,2048]{1,0:T(8,128)(2,1)}, u32[]{:S(2)}) copy-start(bf16[88,2048]{1,0:T(8,128)(2,1)} %get-tuple-element.23.own_in) | copy-start | bytes 1081348
  17.5 38.6 %copy-start = (s32[27,16]{0,1:T(8,128)S(1)}, s32[27,16]{0,1:T(8,128)}, u32[]{:S(2)}) copy-start(s32[27,16]{0,1:T(8,128)} %param.12) | copy-start | bytes 5188
  17.5 38.5 %copy-start.1 = (s32[27,16]{0,1:T(8,128)S(1)}, s32[27,16]{0,1:T(8,128)}, u32[]{:S(2)}) copy-start(s32[27,16]{0,1:T(8,128)} %param.13) | copy-start | bytes 5188
  17.5 4.4 %collective-permute-start.3 = (bf16[256,128]{1,0:T(8,128)(2,1)S(1)}, bf16[256,128]{1,0:T(8,128)(2,1)S(1)}, u32[]{:S(2)}, u32[]{:S(2)}) collective-permute-start(bf16[256,128]{1,0:T(8,128)(2,1)S(1)} %fusion.1), channel_id=1, source_target_pairs={{0,64},{8,72},{16,80},{24,88},{32,96},{40,104},{48,112},{56,120},{... | collective-permute-start | bytes 196616 | tf_op jit(solution)/shard_map/ppermute | solution.py:452
  21.9 4.4 %collective-permute-start.4 = (bf16[256,128]{1,0:T(8,128)(2,1)S(1)}, bf16[256,128]{1,0:T(8,128)(2,1)S(1)}, u32[]{:S(2)}, u32[]{:S(2)}) collective-permute-start(bf16[256,128]{1,0:T(8,128)(2,1)S(1)} %get-tuple-element.29), channel_id=1, source_target_pairs={{0,192},{8,200},{16,208},{24,216},{32,224},{40,232},{48,240},{56,2... | collective-permute-start | bytes 196616 | tf_op jit(solution)/shard_map/ppermute | solution.py:452
  26.7 1.3 %collective-permute-start.5 = (bf16[256,128]{1,0:T(8,128)(2,1)S(1)}, bf16[256,128]{1,0:T(8,128)(2,1)S(1)}, u32[]{:S(2)}, u32[]{:S(2)}) collective-permute-start(bf16[256,128]{1,0:T(8,128)(2,1)S(1)} %spectral.1.own_ref), channel_id=1, source_target_pairs={{0,8},{8,0},{16,24},{24,16},{32,40},{40,32},{48,56},{56,48},{64,72... | collective-permute-start | bytes 196616 | tf_op jit(solution)/shard_map/ppermute | solution.py:459
  30.3 31.8 %all-to-all-start = ((bf16[8,64,256]{2,1,0:T(8,128)(2,1)}), bf16[8,64,256]{2,1,0:T(8,128)(2,1)S(1)}, u32[]{:S(2)}, u32[]{:S(2)}) async-start(bf16[8,64,256]{2,1,0:T(8,128)(2,1)} %potentials.1), calls=%async_computation | async-start | bytes 524288 | tf_op jit(solution)/shard_map/all_to_all | solution.py:426
  40.5 10.0 %collective-permute-start.7 = (bf16[88,2048]{1,0:T(8,128)(2,1)S(1)}, bf16[88,2048]{1,0:T(8,128)(2,1)S(1)}, u32[]{:S(2)}, u32[]{:S(2)}) collective-permute-start(bf16[88,2048]{1,0:T(8,128)(2,1)S(1)} %copy-done.2), channel_id=1, source_target_pairs={{0,252},{1,253},{2,254},{3,255},{4,248},{5,249},{6,250},{7,251},{8... | collective-permute-start | bytes 1081352 | tf_op jit(solution)/shard_map/ppermute | solution.py:422
  45.1 10.9 %collective-permute-start.6 = (bf16[88,2048]{1,0:T(8,128)(2,1)S(1)}, bf16[88,2048]{1,0:T(8,128)(2,1)S(1)}, u32[]{:S(2)}, u32[]{:S(2)}) collective-permute-start(bf16[88,2048]{1,0:T(8,128)(2,1)S(1)} %copy-done.2), channel_id=1, source_target_pairs={{0,8},{1,9},{2,10},{3,11},{4,12},{5,13},{6,14},{7,15},{8,16},{9,17... | collective-permute-start | bytes 1081352 | tf_op jit(solution)/shard_map/ppermute | solution.py:422
